TPU v7x, 512 devices: a whole 4x4x16 slice. The times are simulated.
512 devices in a mesh: dp: 32 (over x_hi, z), tm: 16 (over y, x_lo, core).
Axes of the slice: x: 4 (x_hi: 2, x_lo: 2; x = x_hi * 2 + x_lo), y: 4, z: 16, core: 2. Of those that a mesh axis runs over, the one named last changes fastest.
Arguments:
- clip_input: bfloat16 [32, 32, 256, 384], P('dp', 'tm'), may hold values from -32 to 32
- norm_gain: float32 [384], replicated, may hold values from 0.1 to 1.9
- qkv_weight: bfloat16 [384, 1152], replicated, may hold values from -2 to 2
- out_weight: bfloat16 [384, 384], replicated, may hold values from -0.3125 to 0.3125
- time_weight: bfloat16 [3, 384, 768], P(None, 'dp'), may hold values from -0.1875 to 0.1875
- upsample_cotangent: bfloat16 [32, 32, 256, 768], P('dp', 'tm'), may hold values from -6 to 6
Outputs:
- input_grad: bfloat16 [32, 32, 256, 384], P('dp', 'tm')
- qkv_grad: float32 [384, 1152], P('dp', 'tm')
All inputs are finite; a program needn't handle non-finite values.
Results may differ from a plain program's by a relative error of at most 0.024.
Values may be sent and summed in bfloat16 or wider, within the bound.
No kernel may reach another device: no remote copies, remote signals or barrier semaphores. Data moves between devices by JAX's collectives and lax.ppermute only.
A program may use at most 64 MiB of HBM per device.

v0:
```python
import math

import jax
import jax.numpy as jnp
from jax import lax
from jax.sharding import PartitionSpec as P


def passed_along(block, axis, distance):
    devices = range(lax.axis_size(axis))
    route = [(i - distance, i) for i in devices if i - distance in devices]
    return lax.ppermute(block, axis, route)


def rms_scaled(features, norm_gain):
    squares = jnp.mean(features * features, axis=-1, keepdims=True)
    return features * lax.rsqrt(squares + 1e-06) * norm_gain


def block_tail(qkv_rows, features, out_weight):
    width = features.shape[-1]
    queries = qkv_rows[..., :width]
    keys = qkv_rows[..., width : 2 * width]
    values = qkv_rows[..., 2 * width :]
    scores = jnp.einsum(
        "fqc,fkc->fqk", queries, keys, preferred_element_type=jnp.float32
    ) / math.sqrt(width)
    weights = jax.nn.softmax(scores, axis=-1).astype(jnp.bfloat16)
    mixed = jnp.einsum("fqk,fkc->fqc", weights, values, preferred_element_type=jnp.float32).astype(
        jnp.bfloat16
    )
    branch = jnp.einsum("fqc,cd->fqd", mixed, out_weight, preferred_element_type=jnp.float32)
    return (features + branch).astype(jnp.bfloat16)


def attention_grads(clip_rows, norm_gain, qkv_weight, out_weight, upstream):
    features = clip_rows.astype(jnp.float32)
    normed, pre_back = jax.vjp(lambda value: rms_scaled(value, norm_gain), features)
    normed_bf = normed.astype(jnp.bfloat16)
    qkv_rows = jnp.einsum(
        "fhc,cd->fhd", normed_bf, qkv_weight, preferred_element_type=jnp.float32
    ).astype(jnp.bfloat16)
    block_out, tail_back = jax.vjp(
        lambda first, second: block_tail(first, second, out_weight), qkv_rows, features
    )
    qkv_cot, feature_cot = tail_back(upstream)
    normed_cot = jnp.einsum("fhd,cd->fhc", qkv_cot, qkv_weight, preferred_element_type=jnp.float32)
    direct = pre_back(normed_cot)[0]
    input_grad = (feature_cot + direct).astype(jnp.bfloat16)
    return (input_grad, normed_bf, qkv_cot)


def on_device(clip_input, norm_gain, qkv_weight, out_weight, time_weight, upsample_cotangent):
    rows = clip_input[0]
    cotangent = upsample_cotangent[0]
    frames = cotangent.shape[0]
    width = rows.shape[-1]
    incoming = passed_along(cotangent, "tm", -1)
    padded = jnp.concatenate([cotangent, incoming], 0)
    piece = lax.all_gather(time_weight, "dp", axis=1, tiled=True)
    result = jnp.einsum(
        "fhd,cd->fhc", padded[2 : 2 + frames], piece[0], preferred_element_type=jnp.float32
    )
    result = result + jnp.einsum(
        "fhd,cd->fhc", padded[1 : 1 + frames], piece[1], preferred_element_type=jnp.float32
    )
    upstream = (
        result
        + jnp.einsum("fhd,cd->fhc", padded[0:frames], piece[2], preferred_element_type=jnp.float32)
    ).astype(jnp.bfloat16)
    input_grad, normed_bf, qkv_cot = attention_grads(
        rows, norm_gain, qkv_weight, out_weight, upstream
    )
    flat_normed = normed_bf.reshape(-1, width)
    flat_cot = qkv_cot.reshape(-1, 3 * width)
    shares = lax.psum_scatter(
        jnp.einsum("rc,rd->cd", flat_normed, flat_cot, preferred_element_type=jnp.float32).astype(
            jnp.bfloat16
        ),
        "dp",
        scatter_dimension=0,
        tiled=True,
    )
    qkv_grad = lax.psum_scatter(shares, "tm", scatter_dimension=1, tiled=True).astype(jnp.float32)
    return (input_grad[None], qkv_grad)


def solution(mesh):
    in_specs = (
        P("dp", "tm", None, None),
        P(),
        P(),
        P(),
        P(None, "dp", None),
        P("dp", "tm", None, None),
    )
    out_specs = (P("dp", "tm", None, None), P("dp", "tm"))
    return jax.shard_map(
        on_device, mesh=mesh, in_specs=in_specs, out_specs=out_specs, check_vma=False
    )
```

profile of v0, /device:TPU:4, one launch (start us, length us, event | category | flops | bytes accessed | tf_op | source)
XLA Modules:
  0.0 387.8 jit_solution(9534692791571639131)
XLA Ops:
  7.2 0.0 copy-start
  7.2 0.0 all-gather.2.cloned.1.call-start
  7.2 1.6 copy.10
  8.8 0.0 all-gather.2.cloned.1.call-update
  8.9 1.3 collective-permute-start
  10.2 1.3 dynamic-slice.6
  12.1 1.3 dynamic-slice.2
  14.0 1.1 fusion.16
  15.2 0.0 copy-done
  15.2 1.9 convolution_convert_fusion
  17.1 0.0 copy-start.2
  17.1 0.3 convolution_multiply_fusion.1
  17.4 0.4 fusion.38
  17.8 0.3 copy-done.2
  18.1 0.0 copy-start.3
  18.1 147.2 %all-gather.2.cloned.1.call-done = bf16[3,384,768]{2,0,1:T(4,128)(2,1)} async-done(((bf16[3,12,768]{2,0,1:T(4,128)(2,1)}), bf16[3,384,768]{2,0,1:T(4,128)(2,1)}) %all-gather.2.cloned.1.call-update) | async-done | bytes 1769488 | tf_op jit(solution)/shard_map/all_gather | solution.py:60
  165.3 6.4 %fusion.37 = (bf16[1,384,768]{2,0,1:T(2,128)(2,1)S(1)}, bf16[1,384,768]{2,0,1:T(2,128)(2,1)S(1)}, bf16[1,384,768]{2,0,1:T(2,128)(2,1)S(1)}) fusion(bf16[3,384,768]{2,0,1:T(4,128)(2,1)} %all-gather.2.cloned.1.call-done), kind=kLoop, calls=%fused_computation.61 | loop fusion | bytes 3538944 | tf_op jit(solution)/shard_map/slice | solution.py:62
  171.7 0.0 copy-done.3
  171.8 0.6 fusion.20
  172.4 0.0 collective-permute-done
  172.4 1.6 fusion.3
  174.0 0.0 copy-start.4
  174.0 1.8 fusion.9
  175.8 0.0 copy-done.4
  175.8 0.4 convolution_convert_fusion.4
  176.2 1.3 multiply_reduce_fusion
  177.5 2.1 convolution_convert_fusion.2
  179.7 2.2 convolution_convert_fusion.1
  181.8 0.0 copy-start.1
  181.8 0.0 copy-start.5
  181.8 0.0 copy-start.6
  181.9 1.1 convolution_convert_fusion.3
  182.9 0.0 copy-done.1
  183.0 0.0 copy-done.5
  183.0 0.0 copy-done.6
  183.0 1.9 fusion.2
  184.9 84.6 %fusion = bf16[16,1152]{1,0:T(8,128)(2,1)S(1)} fusion(bf16[384,1152]{1,0:T(8,128)(2,1)S(1)} %fusion.2), kind=kCustom, calls=%all-reduce-scatter | all-reduce-scatter fusion | flops 589825 | bytes 923648
  269.5 1.9 collective-permute-start.1
  271.4 1.9 collective-permute-start.2
  273.3 1.9 collective-permute-start.3
  275.3 1.9 collective-permute-start.4
  277.2 2.0 fusion.19
  279.2 8.9 %collective-permute-start.8 = (bf16[12,1152]{1,0:T(8,128)(2,1)S(1)}, bf16[12,1152]{1,0:T(8,128)(2,1)S(1)}, u32[]{:S(2)}, u32[]{:S(2)}) collective-permute-start(bf16[12,1152]{1,0:T(8,128)(2,1)S(1)} %slice.34), channel_id=1, source_target_pairs={{0,128},{16,144},{32,160},{48,176},{64,192},{80,208},{96,224},{112... | collective-permute-start | bytes 82952
  288.2 9.5 %collective-permute-done.8 = bf16[12,1152]{1,0:T(8,128)(2,1)S(1)} collective-permute-done((bf16[12,1152]{1,0:T(8,128)(2,1)S(1)}, bf16[12,1152]{1,0:T(8,128)(2,1)S(1)}, u32[]{:S(2)}, u32[]{:S(2)}) %collective-permute-start.8) | collective-permute-done | bytes 27680
  297.7 8.0 %collective-permute-start.5 = (bf16[16,1152]{1,0:T(8,128)(2,1)S(1)}, bf16[16,1152]{1,0:T(8,128)(2,1)S(1)}, u32[]{:S(2)}, u32[]{:S(2)}) collective-permute-start(bf16[16,1152]{1,0:T(8,128)(2,1)S(1)} %fusion), channel_id=1, source_target_pairs={{0,80},{16,96},{32,112},{48,128},{64,144},{80,160},{96,176},{112,1... | collective-permute-start | bytes 110600
  305.7 0.0 collective-permute-done.1
  305.7 3.3 collective-permute-start.6
  309.0 0.0 collective-permute-done.2
  309.0 1.9 collective-permute-start.7
  310.9 1.0 fusion.21
  311.9 0.0 collective-permute-done.3
  311.9 0.0 collective-permute-done.4
  312.0 0.0 collective-permute-done.5
  312.0 9.4 %collective-permute-done.6 = bf16[16,1152]{1,0:T(8,128)(2,1)S(1)} collective-permute-done((bf16[16,1152]{1,0:T(8,128)(2,1)S(1)}, bf16[16,1152]{1,0:T(8,128)(2,1)S(1)}, u32[]{:S(2)}, u32[]{:S(2)}) %collective-permute-start.6) | collective-permute-done | bytes 36896
  321.4 4.5 %collective-permute-done.7 = bf16[16,1152]{1,0:T(8,128)(2,1)S(1)} collective-permute-done((bf16[16,1152]{1,0:T(8,128)(2,1)S(1)}, bf16[16,1152]{1,0:T(8,128)(2,1)S(1)}, u32[]{:S(2)}, u32[]{:S(2)}) %collective-permute-start.7) | collective-permute-done | bytes 36896
  325.9 1.5 concatenate.4
  327.4 53.0 %all-reduce.4 = bf16[12,1152]{1,0:T(8,128)(2,1)S(1)} all-reduce(bf16[12,1152]{1,0:T(8,128)(2,1)S(1)} %constant_dynamic-slice_fusion), channel_id=3, replica_groups=mesh['dp'=32,'tm'=16] {'tm'}, use_global_device_ids=true, to_apply=%region_6.0.clone | all-reduce | flops 13824 | bytes 55296
  380.3 0.7 dynamic-slice_convert_fusion
  (6 shorter events, 0.1 us)
Async XLA Ops:
  7.2 8.0 %copy-start = (bf16[384,1152]{1,0:T(8,128)(2,1)S(1)}, bf16[384,1152]{1,0:T(8,128)(2,1)}, u32[]{:S(2)}) copy-start(bf16[384,1152]{1,0:T(8,128)(2,1)} %param.8) | copy-start | bytes 2654212
  7.2 158.1 %all-gather.2.cloned.1.call-start = ((), (), s32[]{:S(2)}) async-start(), calls=%async_computation | async-start | bytes 2433024 | tf_op jit(solution)/shard_map/all_gather | solution.py:60
  8.9 163.5 %collective-permute-start = (bf16[2,256,768]{2,1,0:T(8,128)(2,1)}, bf16[2,256,768]{2,1,0:T(8,128)(2,1)}, u32[]{:S(2)}, u32[]{:S(2)}) collective-permute-start(bf16[2,256,768]{2,1,0:T(8,128)(2,1)} %bitcast.53), channel_id=1, source_target_pairs={{1,0},{2,1},{3,2},{4,3},{5,4},{6,5},{7,6},{8,7},{9,8},{10,9},{11,1... | collective-permute-start | bytes 2359304 | tf_op jit(solution)/shard_map/ppermute | solution.py:12
  17.1 1.0 copy-start.2
  18.1 153.6 %copy-start.3 = (bf16[1,2,256,768]{3,2,1,0:T(8,128)(2,1)S(1)}, bf16[1,2,256,768]{3,2,1,0:T(8,128)(2,1)}, u32[]{:S(2)}) copy-start(bf16[1,2,256,768]{3,2,1,0:T(8,128)(2,1)} %param.11) | copy-start | bytes 2359300
  174.0 1.8 copy-start.4
  181.8 1.1 copy-start.1
  181.8 1.1 copy-start.5
  181.8 1.1 copy-start.6
  269.5 36.2 %collective-permute-start.1 = (bf16[16,1152]{1,0:T(8,128)(2,1)S(1)}, bf16[16,1152]{1,0:T(8,128)(2,1)S(1)}, u32[]{:S(2)}, u32[]{:S(2)}) collective-permute-start(bf16[16,1152]{1,0:T(8,128)(2,1)S(1)} %fusion), channel_id=1, source_target_pairs={{0,16},{16,32},{32,48},{48,64},{64,80},{80,96},{96,112},{112,128},... | collective-permute-start | bytes 110600
  271.4 37.6 %collective-permute-start.2 = (bf16[16,1152]{1,0:T(8,128)(2,1)S(1)}, bf16[16,1152]{1,0:T(8,128)(2,1)S(1)}, u32[]{:S(2)}, u32[]{:S(2)}) collective-permute-start(bf16[16,1152]{1,0:T(8,128)(2,1)S(1)} %fusion), channel_id=1, source_target_pairs={{0,32},{16,48},{32,64},{48,80},{64,96},{80,112},{96,128},{112,144}... | collective-permute-start | bytes 110600
  273.3 38.6 %collective-permute-start.3 = (bf16[16,1152]{1,0:T(8,128)(2,1)S(1)}, bf16[16,1152]{1,0:T(8,128)(2,1)S(1)}, u32[]{:S(2)}, u32[]{:S(2)}) collective-permute-start(bf16[16,1152]{1,0:T(8,128)(2,1)S(1)} %fusion), channel_id=1, source_target_pairs={{0,48},{16,64},{32,80},{48,96},{64,112},{80,128},{96,144},{112,160... | collective-permute-start | bytes 110600
  275.3 36.7 %collective-permute-start.4 = (bf16[16,1152]{1,0:T(8,128)(2,1)S(1)}, bf16[16,1152]{1,0:T(8,128)(2,1)S(1)}, u32[]{:S(2)}, u32[]{:S(2)}) collective-permute-start(bf16[16,1152]{1,0:T(8,128)(2,1)S(1)} %fusion), channel_id=1, source_target_pairs={{0,64},{16,80},{32,96},{48,112},{64,128},{80,144},{96,160},{112,17... | collective-permute-start | bytes 110600
  279.2 18.5 %collective-permute-start.8 = (bf16[12,1152]{1,0:T(8,128)(2,1)S(1)}, bf16[12,1152]{1,0:T(8,128)(2,1)S(1)}, u32[]{:S(2)}, u32[]{:S(2)}) collective-permute-start(bf16[12,1152]{1,0:T(8,128)(2,1)S(1)} %slice.34), channel_id=1, source_target_pairs={{0,128},{16,144},{32,160},{48,176},{64,192},{80,208},{96,224},{112... | collective-permute-start | bytes 82952
  297.7 14.3 %collective-permute-start.5 = (bf16[16,1152]{1,0:T(8,128)(2,1)S(1)}, bf16[16,1152]{1,0:T(8,128)(2,1)S(1)}, u32[]{:S(2)}, u32[]{:S(2)}) collective-permute-start(bf16[16,1152]{1,0:T(8,128)(2,1)S(1)} %fusion), channel_id=1, source_target_pairs={{0,80},{16,96},{32,112},{48,128},{64,144},{80,160},{96,176},{112,1... | collective-permute-start | bytes 110600
  305.7 15.7 %collective-permute-start.6 = (bf16[16,1152]{1,0:T(8,128)(2,1)S(1)}, bf16[16,1152]{1,0:T(8,128)(2,1)S(1)}, u32[]{:S(2)}, u32[]{:S(2)}) collective-permute-start(bf16[16,1152]{1,0:T(8,128)(2,1)S(1)} %fusion), channel_id=1, source_target_pairs={{0,96},{16,112},{32,128},{48,144},{64,160},{80,176},{96,192},{112,... | collective-permute-start | bytes 110600
  309.0 16.9 %collective-permute-start.7 = (bf16[16,1152]{1,0:T(8,128)(2,1)S(1)}, bf16[16,1152]{1,0:T(8,128)(2,1)S(1)}, u32[]{:S(2)}, u32[]{:S(2)}) collective-permute-start(bf16[16,1152]{1,0:T(8,128)(2,1)S(1)} %fusion), channel_id=1, source_target_pairs={{0,112},{16,128},{32,144},{48,160},{64,176},{80,192},{96,208},{112... | collective-permute-start | bytes 110600
Sparse Core Ops, SparseCore 0:
  11.7 153.5 all-gather.1
where the time goes:
time: 389 us; the launch traced here: 388 us
  waiting for transfers between devices  171 us (44%)
  blocking collectives  138 us (35%)
  starting transfers between devices  31.1 us (8%)
  matrix products  17.3 us (4%)
  between operations  15.6 us (4%)
  local copies, waits for them, and re-layouts  12.4 us (3%)
    all_gather x1, waiting for transfers between devices, on_device(): piece = lax.all_gather(time_weight, 'dp', axis=1, tiled=True)  147 us
    unnamed x2, blocking collectives  138 us
    unnamed x8, starting transfers between devices  29.8 us
    unnamed x9, waiting for transfers between devices  23.5 us
  transfers between devices with their start and end apart: 10, of which 4 were waited for; matrix products, arithmetic and copies ran while one was open for 4% of the time, Pallas kernels for 0%

commit v1 on v0

--- a/solution.py
+++ b/solution.py
@@ -3,13 +3,16 @@
 import jax
 import jax.numpy as jnp
 from jax import lax
+from jax.sharding import Mesh
 from jax.sharding import PartitionSpec as P
 
-
-def passed_along(block, axis, distance):
-    devices = range(lax.axis_size(axis))
-    route = [(i - distance, i) for i in devices if i - distance in devices]
-    return lax.ppermute(block, axis, route)
+AXES = ("xh", "z", "y", "xl", "co")
+SIZES = (2, 16, 4, 2, 2)
+DP = ("xh", "z")
+TM = ("y", "xl", "co")
+PLANE = ("xh", "y", "xl")
+PIECES = 8
+TILES = 7
 
 
 def rms_scaled(features, norm_gain):
@@ -50,14 +53,47 @@
     return (input_grad, normed_bf, qkv_cot)
 
 
+def spread(block, axes):
+    count = math.prod(lax.axis_size(a) for a in axes)
+    return lax.all_to_all(
+        jnp.broadcast_to(block[None], (count,) + block.shape), axes, 0, 0, tiled=True
+    )
+
+
+def gathered_taps(shard):
+    taps, held, wide = shard.shape
+    rows, lanes = held // 4, wide // 128
+    tiles = shard.reshape(taps, rows, 4, lanes, 128).transpose(0, 3, 1, 2, 4)
+    count = taps * lanes * rows
+    tiles = tiles.reshape(count, 4, 128)
+    tiles = jnp.concatenate([tiles, jnp.zeros((PIECES * TILES - count, 4, 128), tiles.dtype)], 0)
+    tiles = tiles.reshape(PIECES, TILES, 4, 128)
+    place = lax.axis_index("y") * lax.axis_size("xl") + lax.axis_index("xl")
+    mine = lax.dynamic_index_in_dim(tiles, place, 0, keepdims=False)
+    column = spread(mine, ("z",))
+    half = lax.axis_size("z") // 2
+    core = lax.axis_index("co")
+    part = lax.dynamic_slice_in_dim(column, core * half, half, 0)
+    own = spread(part, PLANE)
+    other = lax.ppermute(own, "co", [(0, 1), (1, 0)])
+    low = jnp.where(core == 0, own, other)
+    high = jnp.where(core == 0, other, own)
+    both = jnp.stack([low, high]).reshape(2, lax.axis_size("xh"), PIECES, half, TILES, 4, 128)
+    both = both.transpose(1, 0, 3, 2, 4, 5, 6).reshape(-1, PIECES * TILES, 4, 128)[:, :count]
+    both = both.reshape(-1, taps, lanes, rows, 4, 128).transpose(1, 0, 3, 4, 2, 5)
+    return both.reshape(taps, -1, wide)
+
+
 def on_device(clip_input, norm_gain, qkv_weight, out_weight, time_weight, upsample_cotangent):
     rows = clip_input[0]
     cotangent = upsample_cotangent[0]
     frames = cotangent.shape[0]
     width = rows.shape[-1]
-    incoming = passed_along(cotangent, "tm", -1)
+    slabs = math.prod(lax.axis_size(a) for a in TM)
+    clips = math.prod(lax.axis_size(a) for a in DP)
+    incoming = lax.ppermute(cotangent, TM, [(i + 1, i) for i in range(slabs - 1)])
     padded = jnp.concatenate([cotangent, incoming], 0)
-    piece = lax.all_gather(time_weight, "dp", axis=1, tiled=True)
+    piece = gathered_taps(time_weight)
     result = jnp.einsum(
         "fhd,cd->fhc", padded[2 : 2 + frames], piece[0], preferred_element_type=jnp.float32
     )
@@ -73,28 +109,27 @@
     )
     flat_normed = normed_bf.reshape(-1, width)
     flat_cot = qkv_cot.reshape(-1, 3 * width)
-    shares = lax.psum_scatter(
-        jnp.einsum("rc,rd->cd", flat_normed, flat_cot, preferred_element_type=jnp.float32).astype(
-            jnp.bfloat16
-        ),
-        "dp",
-        scatter_dimension=0,
-        tiled=True,
-    )
-    qkv_grad = lax.psum_scatter(shares, "tm", scatter_dimension=1, tiled=True).astype(jnp.float32)
+    share = jnp.einsum("rd,rc->dc", flat_cot, flat_normed, preferred_element_type=jnp.float32)
+    share = share.astype(jnp.bfloat16).reshape(slabs, -1, width)
+    share = lax.all_to_all(share, TM, 0, 0, tiled=True)
+    share = jnp.sum(share.astype(jnp.float32), axis=0).astype(jnp.bfloat16)
+    share = share.T.reshape(clips, width // clips, -1)
+    share = lax.all_to_all(share, DP, 0, 0, tiled=True)
+    qkv_grad = jnp.sum(share.astype(jnp.float32), axis=0)
     return (input_grad[None], qkv_grad)
 
 
 def solution(mesh):
+    split = Mesh(mesh.devices.reshape(SIZES), AXES)
     in_specs = (
-        P("dp", "tm", None, None),
+        P(DP, TM, None, None),
         P(),
         P(),
         P(),
-        P(None, "dp", None),
-        P("dp", "tm", None, None),
+        P(None, DP, None),
+        P(DP, TM, None, None),
     )
-    out_specs = (P("dp", "tm", None, None), P("dp", "tm"))
+    out_specs = (P(DP, TM, None, None), P(DP, TM))
     return jax.shard_map(
-        on_device, mesh=mesh, in_specs=in_specs, out_specs=out_specs, check_vma=False
+        on_device, mesh=split, in_specs=in_specs, out_specs=out_specs, check_vma=False
     )

time: 389 us -> 127 us (0.33)
  the two profiles are of different devices: /device:TPU:4 before, /device:TPU:2 now
where the time goes in v1:
time: 127 us
  waiting for transfers between devices  50.9 us (40%)
  starting transfers between devices  43.6 us (34%)
  matrix products  17.4 us (14%)
  local copies, waits for them, and re-layouts  11.5 us (9%)
  other arithmetic  2.39 us (2%)
    all_to_all x2, waiting for transfers between devices, spread(): lax.all_to_all(jnp.broadcast_to(block[None], (count,) + block.shape), axe...  24.2 us
    all_to_all x2, starting transfers between devices, spread(): lax.all_to_all(jnp.broadcast_to(block[None], (count,) + block.shape), axe...  22.8 us
    all_to_all x1, waiting for transfers between devices, on_device(): share = lax.all_to_all(share, DP, 0, 0, tiled=True)  15 us
    all_to_all x1, waiting for transfers between devices, on_device(): share = lax.all_to_all(share, TM, 0, 0, tiled=True)  11.6 us
    all_to_all x1, starting transfers between devices, on_device(): share = lax.all_to_all(share, TM, 0, 0, tiled=True)  11.2 us
    all_to_all x1, starting transfers between devices, on_device(): share = lax.all_to_all(share, DP, 0, 0, tiled=True)  5.82 us
    dot_general x3, matrix products, block_tail(): jnp.einsum('fqc,fkc->fqk', queries, keys, preferred_element_type=jnp.floa...  3.94 us
    dot_general x2, matrix products, block_tail(): jnp.einsum('fqk,fkc->fqc', weights, values, preferred_element_type=jnp.fl...  3.11 us
  transfers between devices with their start and end apart: 6, of which 5 were waited for; matrix products, arithmetic and copies ran while one was open for 11% of the time, Pallas kernels for 0%

profile of v1, /device:TPU:2, one launch (start us, length us, event | category | flops | bytes accessed | tf_op | source)
XLA Modules:
  0.0 126.8 jit_solution(10763761022778695510)
XLA Ops:
  0.6 0.0 copy-start
  0.7 1.0 reshape.71
  1.8 0.7 broadcast_in_dim.15
  2.5 15.2 %all-to-all-start = ((bf16[16,7,4,128]{3,2,1,0:T(4,128)(2,1)}), bf16[16,7,4,128]{3,2,1,0:T(4,128)(2,1)S(1)}, u32[]{:S(2)}, u32[]{:S(2)}) async-start(bf16[16,7,4,128]{3,2,1,0:T(4,128)(2,1)} %broadcast_in_dim.15), calls=%async_computation | async-start | bytes 229376 | tf_op jit(solution)/shard_map/all_to_all | solution.py:58
  17.7 0.0 copy-start.5
  17.7 14.1 %all-to-all-done = bf16[16,7,4,128]{3,2,1,0:T(4,128)(2,1)S(1)} async-done(((bf16[16,7,4,128]{3,2,1,0:T(4,128)(2,1)}), bf16[16,7,4,128]{3,2,1,0:T(4,128)(2,1)S(1)}, u32[]{:S(2)}, u32[]{:S(2)}) %all-to-all-start) | async-done | bytes 114720 | tf_op jit(solution)/shard_map/all_to_all | solution.py:58
  31.8 1.0 broadcast_in_dim.16
  32.9 7.6 %all-to-all-start.1 = ((bf16[16,8,7,4,128]{4,1,3,2,0:T(8,128)(2,1)}), bf16[16,8,7,4,128]{4,1,3,2,0:T(8,128)(2,1)S(1)}, u32[]{:S(2)}, u32[]{:S(2)}) async-start(bf16[16,8,7,4,128]{4,1,3,2,0:T(8,128)(2,1)} %broadcast_in_dim.16), calls=%async_computation.1 | async-start | bytes 1835008 | tf_op jit(solution)/shard_map/all_to_all | solution.py:58
  40.5 1.9 %collective-permute-start.1 = (bf16[2,256,768]{2,1,0:T(8,128)(2,1)}, bf16[2,256,768]{2,1,0:T(8,128)(2,1)}, u32[]{:S(2)}, u32[]{:S(2)}) collective-permute-start(bf16[2,256,768]{2,1,0:T(8,128)(2,1)} %bitcast.10), channel_id=1, source_target_pairs={{1,0},{2,1},{3,2},{4,3},{5,4},{6,5},{7,6},{8,7},{9,8},{10,9},{11,1... | collective-permute-start | bytes 2359304 | tf_op jit(solution)/shard_map/ppermute | solution.py:94
  42.4 0.0 copy-done.5
  42.4 0.2 copy.51
  42.6 0.1 fusion.16
  42.7 10.1 %all-to-all-done.1 = bf16[16,8,7,4,128]{4,1,3,2,0:T(8,128)(2,1)S(1)} async-done(((bf16[16,8,7,4,128]{4,1,3,2,0:T(8,128)(2,1)}), bf16[16,8,7,4,128]{4,1,3,2,0:T(8,128)(2,1)S(1)}, u32[]{:S(2)}, u32[]{:S(2)}) %all-to-all-start.1) | async-done | bytes 917536 | tf_op jit(solution)/shard_map/all_to_all | solution.py:58
  52.8 1.9 %collective-permute-start = (bf16[16,8,7,4,128]{4,1,3,2,0:T(8,128)(2,1)S(1)}, bf16[16,8,7,4,128]{4,1,3,2,0:T(8,128)(2,1)S(1)}, u32[]{:S(2)}, u32[]{:S(2)}) collective-permute-start(bf16[16,8,7,4,128]{4,1,3,2,0:T(8,128)(2,1)S(1)} %all-to-all-done.1), channel_id=1, source_target_pairs={{0,1},{1,0},{2,3},{3,2},{4,5},{5,4},{6,7},{7,6},{8,9},{9,8},{10,11... | collective-permute-start | bytes 2752520 | tf_op jit(solution)/shard_map/ppermute | solution.py:78
  54.7 0.0 copy-done
  54.8 0.0 copy-done.7
  54.8 0.9 convolution_convert_fusion
  55.7 0.0 copy-start.3
  55.7 0.3 convolution_multiply_fusion.1
  56.1 0.0 copy-start.2
  56.1 1.0 fusion.37
  57.1 0.0 copy-done.3
  57.1 0.0 copy-done.2
  57.1 0.1 collective-permute-done
  57.2 0.1 broadcast_select_fusion.1
  57.3 0.2 maximum_bitcast_fusion
  57.5 0.5 copy.46
  58.0 0.5 slice.35
  58.6 0.3 fusion.36
  58.9 0.4 copy.48
  59.3 1.5 %reshape.80 = bf16[384,768,1]{1,0,2:T(8,128)(2,1)} reshape(bf16[1,32,3,4,6,128]{5,4,3,2,1,0:T(8,128)(2,1)S(1)} %copy.48) | data formatting | bytes 1179648 | tf_op jit(solution)/shard_map/squeeze | solution.py:101
  60.8 0.4 copy.50
  61.2 1.5 %reshape.81 = bf16[384,768,1]{1,0,2:T(8,128)(2,1)} reshape(bf16[1,32,3,4,6,128]{5,4,3,2,1,0:T(8,128)(2,1)S(1)} %copy.50) | data formatting | bytes 1179648 | tf_op jit(solution)/shard_map/squeeze | solution.py:105
  62.7 0.4 copy.47
  63.2 0.7 reshape.79
  63.8 0.0 copy-start.4
  63.9 1.9 %convolution_bitcast_fusion.1 = f32[2,256,384]{1,2,0:T(8,128)S(1)} fusion(bf16[384,768,1]{1,0,2:T(8,128)(2,1)} %reshape.81, bf16[1,2,256,768]{3,2,1,0:T(8,128)(2,1)} %param.11), kind=kOutput, calls=%fused_computation.13 | convolution fusion | flops 301989888 | bytes 2162688 | tf_op jit(solution)/shard_map/fhd,cd->fhc/dot_general | solution.py:105
  65.7 0.0 collective-permute-done.1
  65.7 0.0 copy-done.4
  65.8 1.6 %fusion.2 = f32[2,256,384]{1,2,0:T(8,128)S(1)} fusion(bf16[384,768,1]{1,0,2:T(8,128)(2,1)S(1)} %copy-done.4, bf16[2,256,768]{2,1,0:T(8,128)(2,1)} %collective-permute-done.1, bf16[2,256,768]{2,1,0:T(8,128)(2,1)} %bitcast.10), kind=kOutput, calls=%fused_computation.5 | convolution fusion | flops 305135616 | bytes 2949120 | tf_op jit(solution)/shard_map/fhd,cd->fhc/dot_general | solution.py:100
  67.4 0.0 copy-start.6
  67.4 1.7 %fusion.9 = bf16[2,256,384]{1,2,0:T(8,128)(2,1)S(1)} fusion(f32[2,256,384]{1,2,0:T(8,128)S(1)} %convolution_bitcast_fusion.1, f32[2,256,384]{1,2,0:T(8,128)S(1)} %fusion.2, bf16[384,768,1]{1,0,2:T(8,128)(2,1)S(1)} %reshape.79, bf16[2,256,768]{2,1,0:T(8,128)(2,1)} %collective-permute-done.1), kind=kOutput, calls=%fused_computation.19 | convolution fusion | flops 302579712 | bytes 3342336 | tf_op jit(solution)/shard_map/fhd,cd->fhc/dot_general | solution.py:97
  69.1 0.0 copy-done.6
  69.1 0.5 convolution_convert_fusion.4
  69.5 0.0 copy-start.1
  69.6 1.6 %convolution_convert_fusion.3 = bf16[2,256,384]{2,1,0:T(8,128)(2,1)S(1)} fusion(bf16[2,256,384]{2,1,0:T(8,128)(2,1)S(1)} %convolution_convert_fusion.4, f32[2,256]{1,0:T(2,128)S(1)} %get-tuple-element.15, f32[2,256,256]{1,2,0:T(8,128)} %copy-done.2), kind=kOutput, calls=%fused_computation.22 | convolution fusion | flops 101253888 | bytes 1312768 | tf_op jit(solution)/shard_map/transpose(jvp(fqk,fkc->fqc))/dot_general | solution.py:32
  71.2 1.5 %multiply_reduce_fusion = (f32[2,256]{1,0:T(2,128)S(1)}, f32[2,256,256]{1,2,0:T(8,128)S(1)}) fusion(f32[2,256,256]{1,2,0:T(8,128)S(1)} %copy-done.1, f32[2,256]{1,0:T(2,128)S(1)} %multiply_divide_fusion, bf16[2,256,384]{2,1,0:T(8,128)(2,1)S(1)} %convolution_convert_fusion.4, bf16[2,256,1152]{2,1,0:T(8,128)(2,1)} %copy-done.3), kind=kOutput, calls=%fused_computation.41 | convolution fusion | flops 101318144 | bytes 1839104 | tf_op jit(solution)/shard_map/transpose(jvp(fqk,fkc->fqc))/dot_general | solution.py:32
  72.7 1.7 %convolution_convert_fusion.2 = bf16[2,256,384]{2,1,0:T(8,128)(2,1)S(1)} fusion(bf16[2,256,1152]{2,1,0:T(8,128)(2,1)} %copy-done.3, f32[2,256,256]{1,2,0:T(8,128)S(1)} %get-tuple-element.18, f32[2,256]{1,0:T(2,128)S(1)} %neg.6, f32[2,256]{1,0:T(2,128)S(1)} %get-tuple-element.15, f32[2,256,256]{1,2,0:T(8,128)} %copy-done.2), kind=kOutput, calls=%fused_computation.21 | convolution fusion | flops 101516032 | bytes 2363392 | tf_op jit(solution)/shard_map/transpose(jvp(fqc,fkc->fqk))/dot_general | solution.py:28
  74.4 1.9 %convolution_convert_fusion.1 = bf16[2,256,384]{2,1,0:T(8,128)(2,1)S(1)} fusion(bf16[2,256,1152]{2,1,0:T(8,128)(2,1)} %copy-done.3, f32[2,256,256]{1,2,0:T(8,128)S(1)} %get-tuple-element.18, f32[2,256]{1,0:T(2,128)S(1)} %neg.6, f32[2,256]{1,0:T(2,128)S(1)} %get-tuple-element.15, f32[2,256,256]{1,2,0:T(8,128)} %copy-done.2), kind=kOutput, calls=%fused_computation.20 | convolution fusion | flops 101516032 | bytes 2363392 | tf_op jit(solution)/shard_map/transpose(jvp(fqc,fkc->fqk))/dot_general | solution.py:28
  76.4 0.0 copy-start.8
  76.4 1.8 %fusion.1 = bf16[1152,384]{1,0:T(8,128)(2,1)} fusion(bf16[2,256,384]{2,1,0:T(8,128)(2,1)S(1)} %convolution_convert_fusion.1, bf16[2,256,384]{2,1,0:T(8,128)(2,1)S(1)} %convolution_convert_fusion.2, bf16[2,256,384]{2,1,0:T(8,128)(2,1)S(1)} %convolution_convert_fusion.3, bf16[1,2,256,384]{2,3,1,0:T(8,128)(2,1)S(1)} %copy.51, f32[384]{0:T(512)S(1)} %copy-done.7, ...), kind=kOutput, calls=%fused_computation.3 | convolution fusion | flops 457752576 | bytes 2461184 | tf_op jit(solution)/shard_map/rd,rc->dc/dot_general | solution.py:112
  78.2 0.0 copy-done.8
  78.2 11.2 %all-to-all-start.2 = ((bf16[16,72,384]{2,1,0:T(8,128)(2,1)}), bf16[16,72,384]{2,1,0:T(8,128)(2,1)S(1)}, u32[]{:S(2)}, u32[]{:S(2)}) async-start(bf16[16,72,384]{2,1,0:T(8,128)(2,1)} %bitcast.20), calls=%async_computation.2 | async-start | bytes 1769472 | tf_op jit(solution)/shard_map/all_to_all | solution.py:114
  89.4 1.9 %fusion.19 = (f32[2,256]{1,0:T(2,128)S(1)}, f32[2,256,384]{1,2,0:T(8,128)S(1)}) fusion(bf16[1,2,256,384]{2,3,1,0:T(8,128)(2,1)S(1)} %copy.51, f32[384]{0:T(512)S(1)} %copy-done.7, bf16[384,1152]{1,0:T(8,128)(2,1)S(1)} %copy-done, bf16[2,256,384]{2,1,0:T(8,128)(2,1)} %copy-done.8, bf16[2,256,384]{2,1,0:T(8,128)(2,1)} %copy-done.10, ...), kind=kOutput, calls=%fused_computation.39 | convolution fusion | flops 457309696 | bytes 3247616 | tf_op jit(solution)/shard_map/fhd,cd->fhc/dot_general | solution.py:50
  91.4 11.6 %all-to-all-done.2 = bf16[16,72,384]{2,1,0:T(8,128)(2,1)S(1)} async-done(((bf16[16,72,384]{2,1,0:T(8,128)(2,1)}), bf16[16,72,384]{2,1,0:T(8,128)(2,1)S(1)}, u32[]{:S(2)}, u32[]{:S(2)}) %all-to-all-start.2) | async-done | bytes 884768 | tf_op jit(solution)/shard_map/all_to_all | solution.py:114
  103.0 0.1 reduce_sum.69
  103.1 0.1 copy.58
  103.3 0.8 reshape.88
  104.0 5.8 %all-to-all-start.3 = ((bf16[32,2,432]{2,1,0:T(2,128)(2,1)}), bf16[32,2,432]{2,1,0:T(2,128)(2,1)S(1)}, u32[]{:S(2)}, u32[]{:S(2)}) async-start(bf16[32,2,432]{2,1,0:T(2,128)(2,1)} %reshape.88), calls=%async_computation.3 | async-start | bytes 131072 | tf_op jit(solution)/shard_map/all_to_all | solution.py:117
  109.9 0.2 fusion.20
  110.1 0.9 copy.59
  111.0 15.0 %all-to-all-done.3 = bf16[32,2,432]{2,1,0:T(2,128)(2,1)S(1)} async-done(((bf16[32,2,432]{2,1,0:T(2,128)(2,1)}), bf16[32,2,432]{2,1,0:T(2,128)(2,1)S(1)}, u32[]{:S(2)}, u32[]{:S(2)}) %all-to-all-start.3) | async-done | bytes 55328 | tf_op jit(solution)/shard_map/all_to_all | solution.py:117
  126.0 0.2 reshape.89
  126.1 0.6 convert_reduce_fusion
  (16 shorter events, 0.2 us)
Async XLA Ops:
  0.6 54.1 %copy-start = (bf16[384,1152]{1,0:T(8,128)(2,1)S(1)}, bf16[384,1152]{1,0:T(8,128)(2,1)}, u32[]{:S(2)}) copy-start(bf16[384,1152]{1,0:T(8,128)(2,1)} %param.8) | copy-start | bytes 2654212
  2.5 29.3 %all-to-all-start = ((bf16[16,7,4,128]{3,2,1,0:T(4,128)(2,1)}), bf16[16,7,4,128]{3,2,1,0:T(4,128)(2,1)S(1)}, u32[]{:S(2)}, u32[]{:S(2)}) async-start(bf16[16,7,4,128]{3,2,1,0:T(4,128)(2,1)} %broadcast_in_dim.15), calls=%async_computation | async-start | bytes 229376 | tf_op jit(solution)/shard_map/all_to_all | solution.py:58
  17.7 24.7 %copy-start.5 = (bf16[1,2,256,384]{3,2,1,0:T(8,128)(2,1)S(1)}, bf16[1,2,256,384]{3,2,1,0:T(8,128)(2,1)}, u32[]{:S(2)}) copy-start(bf16[1,2,256,384]{3,2,1,0:T(8,128)(2,1)} %param.6) | copy-start | bytes 1179652
  32.9 21.9 %copy-start.7 = (f32[384]{0:T(512)S(1)}, f32[384]{0:T(512)}, u32[]{:S(2)}) copy-start(f32[384]{0:T(512)} %param.7) | copy-start | bytes 4612
  32.9 20.0 %all-to-all-start.1 = ((bf16[16,8,7,4,128]{4,1,3,2,0:T(8,128)(2,1)}), bf16[16,8,7,4,128]{4,1,3,2,0:T(8,128)(2,1)S(1)}, u32[]{:S(2)}, u32[]{:S(2)}) async-start(bf16[16,8,7,4,128]{4,1,3,2,0:T(8,128)(2,1)} %broadcast_in_dim.16), calls=%async_computation.1 | async-start | bytes 1835008 | tf_op jit(solution)/shard_map/all_to_all | solution.py:58
  40.5 25.3 %collective-permute-start.1 = (bf16[2,256,768]{2,1,0:T(8,128)(2,1)}, bf16[2,256,768]{2,1,0:T(8,128)(2,1)}, u32[]{:S(2)}, u32[]{:S(2)}) collective-permute-start(bf16[2,256,768]{2,1,0:T(8,128)(2,1)} %bitcast.10), channel_id=1, source_target_pairs={{1,0},{2,1},{3,2},{4,3},{5,4},{6,5},{7,6},{8,7},{9,8},{10,9},{11,1... | collective-permute-start | bytes 2359304 | tf_op jit(solution)/shard_map/ppermute | solution.py:94
  52.8 4.4 %collective-permute-start = (bf16[16,8,7,4,128]{4,1,3,2,0:T(8,128)(2,1)S(1)}, bf16[16,8,7,4,128]{4,1,3,2,0:T(8,128)(2,1)S(1)}, u32[]{:S(2)}, u32[]{:S(2)}) collective-permute-start(bf16[16,8,7,4,128]{4,1,3,2,0:T(8,128)(2,1)S(1)} %all-to-all-done.1), channel_id=1, source_target_pairs={{0,1},{1,0},{2,3},{3,2},{4,5},{5,4},{6,7},{7,6},{8,9},{9,8},{10,11... | collective-permute-start | bytes 2752520 | tf_op jit(solution)/shard_map/ppermute | solution.py:78
  55.7 1.3 %copy-start.3 = (bf16[2,256,1152]{2,1,0:T(8,128)(2,1)}, bf16[2,256,1152]{2,1,0:T(8,128)(2,1)S(1)}, u32[]{:S(2)}) copy-start(bf16[2,256,1152]{2,1,0:T(8,128)(2,1)S(1)} %convolution_convert_fusion) | copy-start | bytes 3538948
  56.1 1.0 copy-start.2
  63.8 1.9 %copy-start.4 = (bf16[384,768,1]{1,0,2:T(8,128)(2,1)S(1)}, bf16[384,768,1]{1,0,2:T(8,128)(2,1)}, u32[]{:S(2)}) copy-start(bf16[384,768,1]{1,0,2:T(8,128)(2,1)} %reshape.80) | copy-start | bytes 1769476
  67.4 1.7 %copy-start.6 = (bf16[384,384]{1,0:T(8,128)(2,1)S(1)}, bf16[384,384]{1,0:T(8,128)(2,1)}, u32[]{:S(2)}) copy-start(bf16[384,384]{1,0:T(8,128)(2,1)} %param.9) | copy-start | bytes 884740
  69.5 1.7 %copy-start.1 = (f32[2,256,256]{1,2,0:T(8,128)S(1)}, f32[2,256,256]{1,2,0:T(8,128)}, u32[]{:S(2)}) copy-start(f32[2,256,256]{1,2,0:T(8,128)} %get-tuple-element.16) | copy-start | bytes 1572868
  71.2 5.2 %copy-start.9 = (bf16[2,256,384]{2,1,0:T(8,128)(2,1)}, bf16[2,256,384]{2,1,0:T(8,128)(2,1)S(1)}, u32[]{:S(2)}) copy-start(bf16[2,256,384]{2,1,0:T(8,128)(2,1)S(1)} %convolution_convert_fusion.3) | copy-start | bytes 1179652
  74.4 1.9 %copy-start.10 = (bf16[2,256,384]{2,1,0:T(8,128)(2,1)}, bf16[2,256,384]{2,1,0:T(8,128)(2,1)S(1)}, u32[]{:S(2)}) copy-start(bf16[2,256,384]{2,1,0:T(8,128)(2,1)S(1)} %convolution_convert_fusion.2) | copy-start | bytes 1179652
  76.4 1.8 %copy-start.8 = (bf16[2,256,384]{2,1,0:T(8,128)(2,1)}, bf16[2,256,384]{2,1,0:T(8,128)(2,1)S(1)}, u32[]{:S(2)}) copy-start(bf16[2,256,384]{2,1,0:T(8,128)(2,1)S(1)} %convolution_convert_fusion.1) | copy-start | bytes 1179652
  78.2 24.8 %all-to-all-start.2 = ((bf16[16,72,384]{2,1,0:T(8,128)(2,1)}), bf16[16,72,384]{2,1,0:T(8,128)(2,1)S(1)}, u32[]{:S(2)}, u32[]{:S(2)}) async-start(bf16[16,72,384]{2,1,0:T(8,128)(2,1)} %bitcast.20), calls=%async_computation.2 | async-start | bytes 1769472 | tf_op jit(solution)/shard_map/all_to_all | solution.py:114
  104.0 21.9 %all-to-all-start.3 = ((bf16[32,2,432]{2,1,0:T(2,128)(2,1)}), bf16[32,2,432]{2,1,0:T(2,128)(2,1)S(1)}, u32[]{:S(2)}, u32[]{:S(2)}) async-start(bf16[32,2,432]{2,1,0:T(2,128)(2,1)} %reshape.88), calls=%async_computation.3 | async-start | bytes 131072 | tf_op jit(solution)/shard_map/all_to_all | solution.py:117

commit v2 on v1

v2 whole, which is shorter than its diff:
```python
import math

import jax
import jax.numpy as jnp
from jax import lax
from jax.experimental import pallas as pl
from jax.experimental.pallas import tpu as pltpu
from jax.sharding import Mesh
from jax.sharding import PartitionSpec as P

AXES = ("xh", "z", "y", "xl", "co")
SIZES = (2, 16, 4, 2, 2)
DP = ("xh", "z")
TM = ("y", "xl", "co")
PLANE = ("xh", "y", "xl")
PIECES = 8
TILES = 7
LANES = 128
bf16, f32 = jnp.bfloat16, jnp.float32


def dot(a, b, contract):
    return lax.dot_general(a, b, (contract, ((), ())), preferred_element_type=f32)


NN, NT, TN = ((1,), (0,)), ((1,), (1,)), ((0,), (0,))


def forward_kernel(clip_ref, gain_ref, weight_ref, normed_ref, qkv_ref, prob_ref):
    frames, positions, width = clip_ref.shape
    for f in range(frames):
        features = clip_ref[f].astype(f32)
        squares = jnp.mean(features * features, axis=-1, keepdims=True)
        normed = (features * lax.rsqrt(squares + 1e-06) * gain_ref[...]).astype(bf16)
        normed_ref[f] = normed
        qkv = dot(normed, weight_ref[...], NN).astype(bf16)
        qkv_ref[f] = qkv
        scores = dot(qkv[:, :width], qkv[:, width : 2 * width], NT) / math.sqrt(width)
        raised = jnp.exp(scores - jnp.max(scores, axis=-1, keepdims=True))
        prob_ref[f] = raised / jnp.sum(raised, axis=-1, keepdims=True)


def backward_kernel(
    cot_ref, next_ref, own_ref, other_ref, order_ref, out_weight_ref, qkv_ref, prob_ref,
    normed_ref, upstream_ref, qkv_cot_ref, grad_ref, taps_ref,
):
    frames, positions, width = upstream_ref.shape
    rows = frames * positions
    wide = cot_ref.shape[-1]
    taps = taps_ref.shape[0]
    block = own_ref.shape[2]
    groups = own_ref.shape[0] // PIECES
    lanes = wide // LANES
    parts = width // (2 * groups * block)
    for half, source in enumerate((own_ref, other_ref)):
        for group in range(groups):
            for tile in range(taps * lanes * parts):
                tap, rest = divmod(tile, lanes * parts)
                lane, part = divmod(rest, parts)
                start = ((half * groups + group) * parts + part) * block
                taps_ref[tap, start : start + block, lane * LANES : (lane + 1) * LANES] = source[
                    group * PIECES + tile // TILES, tile % TILES
                ]
    middle = jnp.concatenate([cot_ref[1], next_ref[0]], axis=0)
    total = dot(cot_ref[...].reshape(rows, wide), taps_ref[2], NT)
    total = total + dot(middle, taps_ref[1], NT)
    total = total + dot(next_ref[...].reshape(rows, wide), taps_ref[0], NT)
    upstream = dot(total.astype(bf16), order_ref[...], NN).astype(bf16)
    upstream_ref[...] = upstream.reshape(upstream_ref.shape)
    mixed_cot = dot(upstream, out_weight_ref[...], NT).astype(bf16)
    for f in range(frames):
        cot = mixed_cot[f * positions : (f + 1) * positions]
        prob = prob_ref[f]
        queries = qkv_ref[f, :, :width]
        keys = qkv_ref[f, :, width : 2 * width]
        values = qkv_ref[f, :, 2 * width :]
        weights_cot = dot(cot, values, NT).astype(bf16).astype(f32)
        pull = jnp.sum(weights_cot * prob, axis=-1, keepdims=True)
        scores_cot = (prob * (weights_cot - pull) / math.sqrt(width)).astype(bf16)
        qkv_cot_ref[f, :, :width] = dot(scores_cot, keys, NN).astype(bf16)
        qkv_cot_ref[f, :, width : 2 * width] = dot(scores_cot, queries, TN).astype(bf16)
        qkv_cot_ref[f, :, 2 * width :] = dot(prob.astype(bf16), cot, TN).astype(bf16)
    grad_ref[...] = dot(
        qkv_cot_ref[...].reshape(rows, 3 * width), normed_ref[...].reshape(rows, width), TN
    ).astype(bf16)


def input_kernel(clip_ref, gain_ref, weight_ref, qkv_cot_ref, upstream_ref, out_ref):
    frames, positions, width = clip_ref.shape
    for f in range(frames):
        features = clip_ref[f].astype(f32)
        squares = jnp.mean(features * features, axis=-1, keepdims=True)
        scale = lax.rsqrt(squares + 1e-06)
        cot = dot(qkv_cot_ref[f], weight_ref[...], NT) * gain_ref[...]
        along = jnp.mean(features * cot, axis=-1, keepdims=True)
        direct = scale * cot - features * (scale * scale * scale * along)
        out_ref[f] = (upstream_ref[f].astype(f32) + direct).astype(bf16)


def whole(count):
    return [pl.BlockSpec(memory_space=pltpu.VMEM)] * count


def call(kernel, outs, args, flops, limit, scratch=()):
    moved = sum(a.size * a.dtype.itemsize for a in args)
    moved += sum(math.prod(s) * jnp.dtype(d).itemsize for s, d in outs)
    return pl.pallas_call(
        kernel,
        out_shape=tuple(jax.ShapeDtypeStruct(s, d) for s, d in outs),
        in_specs=whole(len(args)),
        out_specs=tuple(whole(len(outs))),
        scratch_shapes=list(scratch),
        cost_estimate=pl.CostEstimate(flops=flops, bytes_accessed=moved, transcendentals=0),
        compiler_params=pltpu.CompilerParams(vmem_limit_bytes=limit << 20),
    )(*args)


def spread(block, axes):
    count = math.prod(lax.axis_size(a) for a in axes)
    return lax.all_to_all(
        jnp.broadcast_to(block[None], (count,) + block.shape), axes, 0, 0, tiled=True
    )


def tap_column(shard):
    taps, held, wide = shard.shape
    rows, lanes = held // 4, wide // LANES
    tiles = shard.reshape(taps, rows, 4, lanes, LANES).transpose(0, 3, 1, 2, 4)
    count = taps * lanes * rows
    tiles = tiles.reshape(count, 4, LANES)
    tiles = jnp.concatenate([tiles, jnp.zeros((PIECES * TILES - count, 4, LANES), tiles.dtype)], 0)
    tiles = tiles.reshape(PIECES, TILES, 4, LANES)
    place = lax.axis_index("y") * lax.axis_size("xl") + lax.axis_index("xl")
    column = spread(lax.dynamic_index_in_dim(tiles, place, 0, keepdims=False), ("z",))
    half = lax.axis_size("z") // 2
    part = lax.dynamic_slice_in_dim(column, lax.axis_index("co") * half, half, 0)
    return part.transpose(1, 0, 2, 3).reshape(TILES, half * 4, LANES)


def channel_order(width):
    depth, groups = lax.axis_size("z"), lax.axis_size("xh")
    half = depth // 2
    held = width // (depth * groups)
    parts = held // 4
    place = jnp.arange(width)
    row, place = place % 4, place // 4
    level, place = place % half, place // half
    part, place = place % parts, place // parts
    group, side = place % groups, place // groups
    level = level + half * jnp.where(lax.axis_index("co") == 0, side, 1 - side)
    channel = held * (group * depth + level) + 4 * part + row
    return (channel[:, None] == jnp.arange(width)[None, :]).astype(bf16)


def on_device(clip_input, norm_gain, qkv_weight, out_weight, time_weight, upsample_cotangent):
    clip = clip_input[0]
    cotangent = upsample_cotangent[0]
    frames, positions, width = clip.shape
    wide = cotangent.shape[-1]
    rows = frames * positions
    slabs = math.prod(lax.axis_size(a) for a in TM)
    clips = math.prod(lax.axis_size(a) for a in DP)
    gain = norm_gain[None]

    incoming = lax.ppermute(cotangent, TM, [(i + 1, i) for i in range(slabs - 1)])
    column = tap_column(time_weight)
    normed, qkv, prob = call(
        forward_kernel,
        [((frames, positions, width), bf16), ((frames, positions, 3 * width), bf16),
         ((frames, positions, positions), f32)],
        [clip, gain, qkv_weight],
        2 * rows * width * (3 * width + positions),
        16,
    )
    order = channel_order(width)
    column, incoming, normed, qkv, prob, order = lax.optimization_barrier(
        (column, incoming, normed, qkv, prob, order)
    )
    own = spread(column, PLANE)
    other = lax.ppermute(own, "co", [(0, 1), (1, 0)])
    upstream, qkv_cot, grad = call(
        backward_kernel,
        [((frames, positions, width), bf16), ((frames, positions, 3 * width), bf16),
         ((3 * width, width), bf16)],
        [cotangent, incoming, own, other, order, out_weight, qkv, prob, normed],
        2 * rows * width * (3 * wide + 2 * width + 4 * positions + 3 * width),
        32,
        [pltpu.VMEM((3, width, wide), bf16)],
    )
    share = grad.reshape(slabs, -1, width)
    share = lax.all_to_all(share, TM, 0, 0, tiled=True)
    (input_grad,) = call(
        input_kernel,
        [((frames, positions, width), bf16)],
        [clip, gain, qkv_weight, qkv_cot, upstream],
        2 * rows * width * 3 * width,
        16,
    )
    share = jnp.sum(share.astype(f32), axis=0).astype(bf16)
    share = share.T.reshape(clips, width // clips, -1)
    share = lax.all_to_all(share, DP, 0, 0, tiled=True)
    qkv_grad = jnp.sum(share.astype(f32), axis=0)
    return (input_grad[None], qkv_grad)


def solution(mesh):
    split = Mesh(mesh.devices.reshape(SIZES), AXES)
    in_specs = (
        P(DP, TM, None, None),
        P(),
        P(),
        P(),
        P(None, DP, None),
        P(DP, TM, None, None),
    )
    out_specs = (P(DP, TM, None, None), P(DP, TM))
    return jax.shard_map(
        on_device, mesh=split, in_specs=in_specs, out_specs=out_specs, check_vma=False
    )
```

time: 127 us -> 108 us (0.85)
  blocking collectives: 0 us -> 38.5 us
  waiting for transfers between devices: 50.9 us -> 24.5 us
  starting transfers between devices: 43.6 us -> 25.3 us
  matrix products: 17.4 us -> 0 us
  Pallas kernels: 0 us -> 6.94 us
  local copies, waits for them, and re-layouts: 11.5 us -> 8.78 us
    all_to_all x0 -> x2, blocking collectives: none -> 38.5 us  [the longest x1 20.3 us: spread(): lax.all_to_all(jnp.broadcast_to(block[None], (count,) + block.shape), axe...]
    dot_general x12 -> x0, matrix products: 17.4 us -> none  [the longest x3 3.94 us: block_tail(): jnp.einsum('fqc,fkc->fqk', queries, keys, preferred_element_type=jnp.floa...]
    all_to_all x2 -> x1, waiting for transfers between devices: 24.2 us -> 7.79 us  [spread(): lax.all_to_all(jnp.broadcast_to(block[None], (count,) + block.shape), axe...]
    all_to_all x1 -> x0, waiting for transfers between devices: 11.6 us -> none  [on_device(): share = lax.all_to_all(share, TM, 0, 0, tiled=True)]
    all_to_all x1 -> x0, starting transfers between devices: 11.2 us -> none  [on_device(): share = lax.all_to_all(share, TM, 0, 0, tiled=True)]
    all_to_all x2 -> x1, starting transfers between devices: 22.8 us -> 15.2 us  [spread(): lax.all_to_all(jnp.broadcast_to(block[None], (count,) + block.shape), axe...]
    pallas_call x0 -> x3, Pallas kernels: none -> 6.94 us  [call(): pl.pallas_call(kernel, out_shape=tuple((jax.ShapeDtypeStruct(s, d) for s,...]
    unnamed x26, local copies, waits for them, and re-layouts: 2.12 us -> 6.06 us
  transfers between devices with their start and end apart: 6 -> 4, of which waited for: 5 -> 3; matrix products, arithmetic and copies ran while one was open for 11% -> 2% of each run, Pallas kernels for 0% -> 3%
where the time goes in v2:
time: 108 us; the launch traced here: 107 us
  blocking collectives  38.5 us (36%)
  starting transfers between devices  25.3 us (23%)
  waiting for transfers between devices  24.5 us (23%)
  local copies, waits for them, and re-layouts  8.78 us (8%)
  Pallas kernels  6.94 us (6%)
  other arithmetic  2.19 us (2%)
    all_to_all x1, blocking collectives, spread(): lax.all_to_all(jnp.broadcast_to(block[None], (count,) + block.shape), axe...  20.3 us
    all_to_all x1, blocking collectives, on_device(): share = lax.all_to_all(share, TM, 0, 0, tiled=True)  18.2 us
    all_to_all x1, starting transfers between devices, spread(): lax.all_to_all(jnp.broadcast_to(block[None], (count,) + block.shape), axe...  15.2 us
    all_to_all x1, waiting for transfers between devices, on_device(): share = lax.all_to_all(share, DP, 0, 0, tiled=True)  14.3 us
    all_to_all x1, waiting for transfers between devices, spread(): lax.all_to_all(jnp.broadcast_to(block[None], (count,) + block.shape), axe...  7.79 us
    pallas_call x3, Pallas kernels, call(): pl.pallas_call(kernel, out_shape=tuple((jax.ShapeDtypeStruct(s, d) for s,...  6.94 us
    all_to_all x1, starting transfers between devices, on_device(): share = lax.all_to_all(share, DP, 0, 0, tiled=True)  6.29 us
    unnamed x26, local copies, waits for them, and re-layouts  6.06 us
  transfers between devices with their start and end apart: 4, of which 3 were waited for; matrix products, arithmetic and copies ran while one was open for 2% of the time, Pallas kernels for 3%

profile of v2, /device:TPU:2, one launch (start us, length us, event | category | flops | bytes accessed | tf_op | source)
XLA Modules:
  0.0 107.1 jit_solution(13895236959608816777)
XLA Ops:
  0.6 1.9 %collective-permute-start = (bf16[2,256,768]{2,1,0:T(8,128)(2,1)}, bf16[2,256,768]{2,1,0:T(8,128)(2,1)S(1)}, u32[]{:S(2)}, u32[]{:S(2)}) collective-permute-start(bf16[2,256,768]{2,1,0:T(8,128)(2,1)} %bitcast.16), channel_id=1, source_target_pairs={{1,0},{2,1},{3,2},{4,3},{5,4},{6,5},{7,6},{8,7},{9,8},{10,9},{11,1... | collective-permute-start | bytes 2359304 | tf_op jit(solution)/shard_map/ppermute | solution.py:165
  2.6 1.0 reshape.117
  3.6 0.7 broadcast_in_dim.12
  4.3 15.2 %all-to-all-start = ((bf16[16,7,4,128]{3,2,1,0:T(4,128)(2,1)}), bf16[16,7,4,128]{3,2,1,0:T(4,128)(2,1)S(1)}, u32[]{:S(2)}, u32[]{:S(2)}) async-start(bf16[16,7,4,128]{3,2,1,0:T(4,128)(2,1)} %broadcast_in_dim.12), calls=%async_computation | async-start | bytes 229376 | tf_op jit(solution)/shard_map/all_to_all | solution.py:120
  19.5 0.7 broadcast_in_dim.10.gain_ref
  20.2 0.0 copy-start
  20.2 1.2 %copy-done = bf16[384,1152]{1,0:T(8,128)(2,1)S(1)} copy-done((bf16[384,1152]{1,0:T(8,128)(2,1)S(1)}, bf16[384,1152]{1,0:T(8,128)(2,1)}, u32[]{:S(2)}) %copy-start) | copy-done | bytes 884760
  21.4 0.0 copy-start.2
  21.4 1.0 copy-done.2
  22.4 1.4 %shard_map.77 = (bf16[2,256,384]{2,1,0:T(8,128)(2,1)S(1)}, bf16[2,256,1152]{2,1,0:T(8,128)(2,1)S(1)}, f32[2,256,256]{2,1,0:T(8,128)S(1)}) custom-call(bf16[2,256,384]{2,1,0:T(8,128)(2,1)S(1)} %bitcast.14, f32[1,384]{1,0:T(1,128)S(1)} %broadcast_in_dim.10.gain_ref, bf16[384,1152]{1,0:T(8,128)(2,1)S(1)} %copy-done), custom_call_target="tpu_custom_call" | custom-call | flops 553648128 | bytes 3376640 | tf_op jit(solution)/shard_map/pallas_call | solution.py:107
  23.8 0.0 copy-start.8
  23.8 1.0 copy-done.8
  24.8 0.0 copy-start.10
  24.8 0.7 copy-done.10
  25.6 0.1 fusion.order_ref
  25.7 7.8 %all-to-all-done = bf16[16,7,4,128]{3,2,1,0:T(4,128)(2,1)S(1)} async-done(((bf16[16,7,4,128]{3,2,1,0:T(4,128)(2,1)}), bf16[16,7,4,128]{3,2,1,0:T(4,128)(2,1)S(1)}, u32[]{:S(2)}, u32[]{:S(2)}) %all-to-all-start) | async-done | bytes 114720 | tf_op jit(solution)/shard_map/all_to_all | solution.py:120
  33.5 0.0 collective-permute-done.next_ref
  33.6 0.0 copy-start.5
  33.6 0.0 copy-start.4
  33.6 0.0 copy-start.7
  33.6 0.0 copy-start.9
  33.6 0.0 copy-start.11
  33.6 0.1 broadcast_in_dim.26
  33.7 20.3 %all_to_all.20.own_ref = bf16[16,7,32,128]{3,2,1,0:T(8,128)(2,1)S(1)} all-to-all(bf16[16,7,32,128]{3,2,1,0:T(8,128)(2,1)S(1)} %broadcast_in_dim.26), channel_id=1, replica_groups=mesh['xh'=2,'z'=16,'y'=4,'xl'=2,'co'=2] {'xh','y','xl'}, dimensions={0} | all-to-all | bytes 1835008 | tf_op jit(solution)/shard_map/all_to_all | solution.py:120
  54.0 0.0 copy-done.5
  54.1 1.9 %collective-permute-start.1 = (bf16[16,7,32,128]{3,2,1,0:T(8,128)(2,1)S(1)}, bf16[16,7,32,128]{3,2,1,0:T(8,128)(2,1)S(1)}, u32[]{:S(2)}, u32[]{:S(2)}) collective-permute-start(bf16[16,7,32,128]{3,2,1,0:T(8,128)(2,1)S(1)} %all_to_all.20.own_ref), channel_id=1, source_target_pairs={{0,1},{1,0},{2,3},{3,2},{4,5},{5,4},{6,7},{7,6},{8,9},{9,8},{10,11... | collective-permute-start | bytes 2752520 | tf_op jit(solution)/shard_map/ppermute | solution.py:180
  56.0 2.4 %collective-permute-done.1.other_ref = bf16[16,7,32,128]{3,2,1,0:T(8,128)(2,1)S(1)} collective-permute-done((bf16[16,7,32,128]{3,2,1,0:T(8,128)(2,1)S(1)}, bf16[16,7,32,128]{3,2,1,0:T(8,128)(2,1)S(1)}, u32[]{:S(2)}, u32[]{:S(2)}) %collective-permute-start.1) | collective-permute-done | bytes 917536 | tf_op jit(solution)/shard_map/ppermute | solution.py:180
  58.4 0.0 copy-done.4
  58.4 0.0 copy-done.7
  58.4 0.0 copy-done.9
  58.4 0.0 copy-done.11
  58.4 0.0 copy-start.6
  58.4 1.1 %copy-done.6 = bf16[2,256,768]{2,1,0:T(8,128)(2,1)S(1)} copy-done((bf16[2,256,768]{2,1,0:T(8,128)(2,1)S(1)}, bf16[2,256,768]{2,1,0:T(8,128)(2,1)}, u32[]{:S(2)}) %copy-start.6) | copy-done | bytes 786456
  59.6 3.8 %shard_map.78 = (bf16[2,256,384]{2,1,0:T(8,128)(2,1)S(1)}, bf16[2,256,1152]{2,1,0:T(8,128)(2,1)S(1)}, bf16[1152,384]{1,0:T(8,128)(2,1)S(1)}) custom-call(bf16[2,256,768]{2,1,0:T(8,128)(2,1)S(1)} %bitcast.17, bf16[2,256,768]{2,1,0:T(8,128)(2,1)S(1)} %copy-done.6, bf16[16,7,32,128]{3,2,1,0:T(8,128)(2,1)S(1)} %all_to_all.20.own_ref, ...), custom_call_target="tpu_custom_call" | custom-call | flops 2063597568 | bytes 8552448 | tf_op jit(solution)/shard_map/pallas_call | solution.py:107
  63.4 18.2 %all_to_all.21 = bf16[16,72,384]{2,1,0:T(8,128)(2,1)} all-to-all(bf16[16,72,384]{2,1,0:T(8,128)(2,1)S(1)} %bitcast.13), channel_id=1, replica_groups=mesh['xh'=2,'z'=16,'y'=4,'xl'=2,'co'=2] {'y','xl','co'}, dimensions={0} | all-to-all | bytes 1769472 | tf_op jit(solution)/shard_map/all_to_all | solution.py:191
  81.5 0.0 copy-start.1
  81.5 0.0 copy-start.3
  81.6 1.4 %reduce_sum.21 = bf16[72,384]{1,0:T(8,128)(2,1)S(1)} reduce(bf16[16,72,384]{2,1,0:T(8,128)(2,1)} %all_to_all.21, bf16[]{:T(256)} %constant.92.clone.1), dimensions={0}, to_apply=%region_0.1 | reduce | flops 414720 | bytes 940034 | tf_op jit(solution)/shard_map/reduce_sum | solution.py:199
  82.9 0.1 copy.13
  83.1 0.8 reshape.123
  83.9 6.3 %all-to-all-start.3 = ((bf16[32,2,432]{2,1,0:T(2,128)(2,1)}), bf16[32,2,432]{2,1,0:T(2,128)(2,1)S(1)}, u32[]{:S(2)}, u32[]{:S(2)}) async-start(bf16[32,2,432]{2,1,0:T(2,128)(2,1)} %reshape.123), calls=%async_computation.3 | async-start | bytes 131072 | tf_op jit(solution)/shard_map/all_to_all | solution.py:201
  90.2 0.0 copy-done.1
  90.2 0.0 copy-done.3
  90.2 1.8 %shard_map.79 = bf16[2,256,384]{2,1,0:T(8,128)(2,1)} custom-call(bf16[2,256,384]{2,1,0:T(8,128)(2,1)S(1)} %bitcast.15, f32[1,384]{1,0:T(1,128)S(1)} %broadcast_in_dim.10.gain_ref, bf16[384,1152]{1,0:T(8,128)(2,1)S(1)} %copy-done.1, bf16[2,256,1152]{2,1,0:T(8,128)(2,1)S(1)} %get-tuple-element.23.qkv_cot_ref, ...), custom_call_target="tpu_custom_call" | custom-call | flops 452984832 | bytes 3245568 | tf_op jit(solution)/shard_map/pallas_call | solution.py:107
  92.0 14.3 %all-to-all-done.3 = bf16[32,2,432]{2,1,0:T(2,128)(2,1)S(1)} async-done(((bf16[32,2,432]{2,1,0:T(2,128)(2,1)}), bf16[32,2,432]{2,1,0:T(2,128)(2,1)S(1)}, u32[]{:S(2)}, u32[]{:S(2)}) %all-to-all-start.3) | async-done | bytes 55328 | tf_op jit(solution)/shard_map/all_to_all | solution.py:201
  106.3 0.2 reshape.124
  106.5 0.6 convert_reduce_fusion
  (7 shorter events, 0.2 us)
Async XLA Ops:
  0.6 32.9 %collective-permute-start = (bf16[2,256,768]{2,1,0:T(8,128)(2,1)}, bf16[2,256,768]{2,1,0:T(8,128)(2,1)S(1)}, u32[]{:S(2)}, u32[]{:S(2)}) collective-permute-start(bf16[2,256,768]{2,1,0:T(8,128)(2,1)} %bitcast.16), channel_id=1, source_target_pairs={{1,0},{2,1},{3,2},{4,3},{5,4},{6,5},{7,6},{8,7},{9,8},{10,9},{11,1... | collective-permute-start | bytes 2359304 | tf_op jit(solution)/shard_map/ppermute | solution.py:165
  4.3 29.2 %all-to-all-start = ((bf16[16,7,4,128]{3,2,1,0:T(4,128)(2,1)}), bf16[16,7,4,128]{3,2,1,0:T(4,128)(2,1)S(1)}, u32[]{:S(2)}, u32[]{:S(2)}) async-start(bf16[16,7,4,128]{3,2,1,0:T(4,128)(2,1)} %broadcast_in_dim.12), calls=%async_computation | async-start | bytes 229376 | tf_op jit(solution)/shard_map/all_to_all | solution.py:120
  20.2 1.2 %copy-start = (bf16[384,1152]{1,0:T(8,128)(2,1)S(1)}, bf16[384,1152]{1,0:T(8,128)(2,1)}, u32[]{:S(2)}) copy-start(bf16[384,1152]{1,0:T(8,128)(2,1)} %weight_ref.3) | copy-start | bytes 2654212
  21.4 1.0 copy-start.2
  23.8 1.0 copy-start.8
  24.8 0.7 copy-start.10
  33.6 20.5 %copy-start.5 = (bf16[2,256,768]{2,1,0:T(8,128)(2,1)}, bf16[2,256,768]{2,1,0:T(8,128)(2,1)S(1)}, u32[]{:S(2)}) copy-start(bf16[2,256,768]{2,1,0:T(8,128)(2,1)S(1)} %collective-permute-done.next_ref) | copy-start | bytes 2359300
  33.6 24.8 %copy-start.4 = (bf16[1,2,256,768]{3,2,1,0:T(8,128)(2,1)S(1)}, bf16[1,2,256,768]{3,2,1,0:T(8,128)(2,1)}, u32[]{:S(2)}) copy-start(bf16[1,2,256,768]{3,2,1,0:T(8,128)(2,1)} %param.11) | copy-start | bytes 2359300
  33.6 24.8 %copy-start.7 = (bf16[384,384]{1,0:T(8,128)(2,1)S(1)}, bf16[384,384]{1,0:T(8,128)(2,1)}, u32[]{:S(2)}) copy-start(bf16[384,384]{1,0:T(8,128)(2,1)} %out_weight_ref.1) | copy-start | bytes 884740
  33.6 24.8 %copy-start.9 = (bf16[2,256,1152]{2,1,0:T(8,128)(2,1)S(1)}, bf16[2,256,1152]{2,1,0:T(8,128)(2,1)}, u32[]{:S(2)}) copy-start(bf16[2,256,1152]{2,1,0:T(8,128)(2,1)} %copy-done.8) | copy-start | bytes 3538948
  33.6 24.8 %copy-start.11 = (bf16[2,256,384]{2,1,0:T(8,128)(2,1)S(1)}, bf16[2,256,384]{2,1,0:T(8,128)(2,1)}, u32[]{:S(2)}) copy-start(bf16[2,256,384]{2,1,0:T(8,128)(2,1)} %copy-done.10) | copy-start | bytes 1179652
  54.1 4.4 %collective-permute-start.1 = (bf16[16,7,32,128]{3,2,1,0:T(8,128)(2,1)S(1)}, bf16[16,7,32,128]{3,2,1,0:T(8,128)(2,1)S(1)}, u32[]{:S(2)}, u32[]{:S(2)}) collective-permute-start(bf16[16,7,32,128]{3,2,1,0:T(8,128)(2,1)S(1)} %all_to_all.20.own_ref), channel_id=1, source_target_pairs={{0,1},{1,0},{2,3},{3,2},{4,5},{5,4},{6,7},{7,6},{8,9},{9,8},{10,11... | collective-permute-start | bytes 2752520 | tf_op jit(solution)/shard_map/ppermute | solution.py:180
  58.4 1.1 %copy-start.6 = (bf16[2,256,768]{2,1,0:T(8,128)(2,1)S(1)}, bf16[2,256,768]{2,1,0:T(8,128)(2,1)}, u32[]{:S(2)}) copy-start(bf16[2,256,768]{2,1,0:T(8,128)(2,1)} %copy-done.5) | copy-start | bytes 2359300
  81.5 8.7 %copy-start.1 = (bf16[384,1152]{1,0:T(8,128)(2,1)S(1)}, bf16[384,1152]{1,0:T(8,128)(2,1)}, u32[]{:S(2)}) copy-start(bf16[384,1152]{1,0:T(8,128)(2,1)} %weight_ref.3) | copy-start | bytes 2654212
  81.5 8.7 %copy-start.3 = (bf16[1,2,256,384]{3,2,1,0:T(8,128)(2,1)S(1)}, bf16[1,2,256,384]{3,2,1,0:T(8,128)(2,1)}, u32[]{:S(2)}) copy-start(bf16[1,2,256,384]{3,2,1,0:T(8,128)(2,1)} %param.6) | copy-start | bytes 1179652
  83.9 22.4 %all-to-all-start.3 = ((bf16[32,2,432]{2,1,0:T(2,128)(2,1)}), bf16[32,2,432]{2,1,0:T(2,128)(2,1)S(1)}, u32[]{:S(2)}, u32[]{:S(2)}) async-start(bf16[32,2,432]{2,1,0:T(2,128)(2,1)} %reshape.123), calls=%async_computation.3 | async-start | bytes 131072 | tf_op jit(solution)/shard_map/all_to_all | solution.py:201

commit v3 on v2

--- a/solution.py
+++ b/solution.py
@@ -41,8 +41,9 @@
 
 
 def backward_kernel(
-    cot_ref, next_ref, own_ref, other_ref, order_ref, out_weight_ref, qkv_ref, prob_ref,
-    normed_ref, upstream_ref, qkv_cot_ref, grad_ref, taps_ref,
+    core_ref, cot_any, next_any, own_ref, other_ref, order_ref, out_weight_ref, qkv_ref, prob_ref,
+    normed_ref, upstream_ref, qkv_cot_ref, keep_ref, send_ref, taps_ref, cot_ref, next_ref,
+    grad_ref, sems,
 ):
     frames, positions, width = upstream_ref.shape
     rows = frames * positions
@@ -52,6 +53,12 @@
     groups = own_ref.shape[0] // PIECES
     lanes = wide // LANES
     parts = width // (2 * groups * block)
+    copies = [
+        pltpu.make_async_copy(cot_any, cot_ref, sems.at[0]),
+        pltpu.make_async_copy(next_any, next_ref, sems.at[1]),
+    ]
+    for copy in copies:
+        copy.start()
     for half, source in enumerate((own_ref, other_ref)):
         for group in range(groups):
             for tile in range(taps * lanes * parts):
@@ -61,6 +68,8 @@
                 taps_ref[tap, start : start + block, lane * LANES : (lane + 1) * LANES] = source[
                     group * PIECES + tile // TILES, tile % TILES
                 ]
+    for copy in copies:
+        copy.wait()
     middle = jnp.concatenate([cot_ref[1], next_ref[0]], axis=0)
     total = dot(cot_ref[...].reshape(rows, wide), taps_ref[2], NT)
     total = total + dot(middle, taps_ref[1], NT)
@@ -82,7 +91,50 @@
         qkv_cot_ref[f, :, 2 * width :] = dot(prob.astype(bf16), cot, TN).astype(bf16)
     grad_ref[...] = dot(
         qkv_cot_ref[...].reshape(rows, 3 * width), normed_ref[...].reshape(rows, width), TN
-    ).astype(bf16)
+    )
+    columns = grad_ref.shape[0] // (2 * PIECES)
+    short = keep_ref.shape[1] - columns
+    left = lax.broadcasted_iota(jnp.int32, (short, LANES), 1) < LANES // 2
+    first = core_ref[0] == 0
+    for group in range(groups):
+        for chip in range(PIECES):
+            pair = []
+            for core in range(2):
+                top = (2 * chip + core) * columns
+                low = top + columns - short
+                upper = grad_ref[top : top + short, LANES : 2 * LANES]
+                lower = grad_ref[low : low + short, LANES : 2 * LANES]
+                if group == 0:
+                    lower = pltpu.roll(lower, LANES // 2, 1)
+                else:
+                    upper = pltpu.roll(upper, LANES // 2, 1)
+                side = 2 * group * LANES
+                pair.append(
+                    jnp.concatenate(
+                        [
+                            grad_ref[top : top + columns, side : side + LANES],
+                            jnp.where(left, upper, lower),
+                        ],
+                        axis=0,
+                    )
+                )
+            keep_ref[group * PIECES + chip] = jnp.where(first, pair[0], pair[1]).astype(bf16)
+            send_ref[group * PIECES + chip] = jnp.where(first, pair[1], pair[0]).astype(bf16)
+
+
+def turn_kernel(got_ref, turn_ref, out_ref):
+    columns, short = 72, got_ref.shape[1] - 72
+    total = got_ref[0].astype(f32)
+    for i in range(1, got_ref.shape[0]):
+        total = total + got_ref[i].astype(f32)
+    narrow = total[columns:]
+    other = pltpu.roll(narrow, LANES // 2, 1)
+    narrow = jnp.concatenate([narrow, other[2 * short - columns :]], axis=0)
+    turned = dot(turn_ref[0], total[:columns].astype(bf16), NT)
+    turned = turned + dot(turn_ref[1], narrow.astype(bf16), NT)
+    turned = turned.astype(bf16).reshape(out_ref.shape[0], 16, columns)
+    out_ref[...] = jnp.zeros_like(out_ref)
+    out_ref[:, :, :columns] = turned
 
 
 def input_kernel(clip_ref, gain_ref, weight_ref, qkv_cot_ref, upstream_ref, out_ref):
@@ -101,13 +153,13 @@
     return [pl.BlockSpec(memory_space=pltpu.VMEM)] * count
 
 
-def call(kernel, outs, args, flops, limit, scratch=()):
+def call(kernel, outs, args, flops, limit, scratch=(), specs=None):
     moved = sum(a.size * a.dtype.itemsize for a in args)
     moved += sum(math.prod(s) * jnp.dtype(d).itemsize for s, d in outs)
     return pl.pallas_call(
         kernel,
         out_shape=tuple(jax.ShapeDtypeStruct(s, d) for s, d in outs),
-        in_specs=whole(len(args)),
+        in_specs=specs or whole(len(args)),
         out_specs=tuple(whole(len(outs))),
         scratch_shapes=list(scratch),
         cost_estimate=pl.CostEstimate(flops=flops, bytes_accessed=moved, transcendentals=0),
@@ -124,32 +176,40 @@
 
 def tap_column(shard):
     taps, held, wide = shard.shape
-    rows, lanes = held // 4, wide // LANES
-    tiles = shard.reshape(taps, rows, 4, lanes, LANES).transpose(0, 3, 1, 2, 4)
-    count = taps * lanes * rows
-    tiles = tiles.reshape(count, 4, LANES)
-    tiles = jnp.concatenate([tiles, jnp.zeros((PIECES * TILES - count, 4, LANES), tiles.dtype)], 0)
-    tiles = tiles.reshape(PIECES, TILES, 4, LANES)
+    lanes, parts = wide // LANES, held // 4
+    tiles = shard.reshape(taps, 2, parts, 2, lanes, LANES).transpose(1, 0, 4, 2, 3, 5)
+    count = taps * lanes * parts
+    tiles = tiles.reshape(2, count, 2, LANES)
+    tiles = jnp.concatenate([tiles, jnp.zeros((2, PIECES * TILES - count, 2, LANES), bf16)], 1)
+    tiles = tiles.reshape(2 * PIECES, TILES, 2, LANES)
     place = lax.axis_index("y") * lax.axis_size("xl") + lax.axis_index("xl")
+    place = place + lax.axis_index("co") * PIECES
     column = spread(lax.dynamic_index_in_dim(tiles, place, 0, keepdims=False), ("z",))
-    half = lax.axis_size("z") // 2
-    part = lax.dynamic_slice_in_dim(column, lax.axis_index("co") * half, half, 0)
-    return part.transpose(1, 0, 2, 3).reshape(TILES, half * 4, LANES)
+    return column.transpose(1, 0, 2, 3).reshape(TILES, -1, LANES)
 
 
 def channel_order(width):
     depth, groups = lax.axis_size("z"), lax.axis_size("xh")
-    half = depth // 2
     held = width // (depth * groups)
     parts = held // 4
     place = jnp.arange(width)
-    row, place = place % 4, place // 4
-    level, place = place % half, place // half
+    row, place = place % 2, place // 2
+    level, place = place % depth, place // depth
     part, place = place % parts, place // parts
-    group, side = place % groups, place // groups
-    level = level + half * jnp.where(lax.axis_index("co") == 0, side, 1 - side)
-    channel = held * (group * depth + level) + 4 * part + row
+    group, half = place % groups, place // groups
+    side = jnp.where(lax.axis_index("co") == 0, half, 1 - half)
+    channel = held * (group * depth + level) + (held // 2) * side + 2 * part + row
     return (channel[:, None] == jnp.arange(width)[None, :]).astype(bf16)
+
+
+def turn_orders(held, depth):
+    group = lax.axis_index("xh")
+    row = jnp.arange(depth * 16)
+    channel = jnp.where(row % 16 < held, row // 16 * held + row % 16, -1)[:, None]
+    lane = jnp.arange(LANES)[None, :]
+    wide = channel == lane + 64 * group
+    narrow = (channel == lane + LANES * (1 - group)) & (lane < 64)
+    return jnp.stack([wide, narrow]).astype(bf16)
 
 
 def on_device(clip_input, norm_gain, qkv_weight, out_weight, time_weight, upsample_cotangent):
@@ -172,23 +232,33 @@
         2 * rows * width * (3 * width + positions),
         16,
     )
+    depth = lax.axis_size("z")
+    held = width // clips
     order = channel_order(width)
-    column, incoming, normed, qkv, prob, order = lax.optimization_barrier(
-        (column, incoming, normed, qkv, prob, order)
+    turn = turn_orders(held, depth)
+    core = lax.axis_index("co").reshape(1)
+    column, incoming, normed, qkv, prob, order, turn = lax.optimization_barrier(
+        (column, incoming, normed, qkv, prob, order, turn)
     )
     own = spread(column, PLANE)
-    other = lax.ppermute(own, "co", [(0, 1), (1, 0)])
-    upstream, qkv_cot, grad = call(
+    swap = [(0, 1), (1, 0)]
+    other = lax.ppermute(own, "co", swap)
+
+    chips = own.shape[0]
+    packed = ((chips, 112, LANES), bf16)
+    upstream, qkv_cot, keep, send = call(
         backward_kernel,
-        [((frames, positions, width), bf16), ((frames, positions, 3 * width), bf16),
-         ((3 * width, width), bf16)],
-        [cotangent, incoming, own, other, order, out_weight, qkv, prob, normed],
+        [((frames, positions, width), bf16), ((frames, positions, 3 * width), bf16), packed, packed],
+        [core, cotangent, incoming, own, other, order, out_weight, qkv, prob, normed],
         2 * rows * width * (3 * wide + 2 * width + 4 * positions + 3 * width),
         32,
-        [pltpu.VMEM((3, width, wide), bf16)],
-    )
-    share = grad.reshape(slabs, -1, width)
-    share = lax.all_to_all(share, TM, 0, 0, tiled=True)
+        [pltpu.VMEM((3, width, wide), bf16), pltpu.VMEM(cotangent.shape, bf16),
+         pltpu.VMEM(cotangent.shape, bf16), pltpu.VMEM((3 * width, width), f32),
+         pltpu.SemaphoreType.DMA((2,))],
+        [pl.BlockSpec(memory_space=pltpu.SMEM)] + [pl.BlockSpec(memory_space=pl.ANY)] * 2 + whole(7),
+    )
+    share = keep.astype(f32) + lax.ppermute(send, "co", swap).astype(f32)
+    share = lax.all_to_all(share.astype(bf16), PLANE, 0, 0, tiled=True)
     (input_grad,) = call(
         input_kernel,
         [((frames, positions, width), bf16)],
@@ -196,10 +266,15 @@
         2 * rows * width * 3 * width,
         16,
     )
-    share = jnp.sum(share.astype(f32), axis=0).astype(bf16)
-    share = share.T.reshape(clips, width // clips, -1)
-    share = lax.all_to_all(share, DP, 0, 0, tiled=True)
-    qkv_grad = jnp.sum(share.astype(f32), axis=0)
+    (share,) = call(
+        turn_kernel,
+        [((depth, 16, LANES), bf16)],
+        [share, turn],
+        2 * depth * 16 * 72 * 2 * LANES,
+        16,
+    )
+    share = lax.all_to_all(share, "z", 0, 0, tiled=True)
+    qkv_grad = jnp.sum(share[:, :held, : 3 * width // slabs].astype(f32), axis=0)
     return (input_grad[None], qkv_grad)
 
 

time: 108 us -> 106 us (0.981)
  starting transfers between devices: 25.3 us -> 32.1 us
  waiting for transfers between devices: 24.5 us -> 19.5 us
  local copies, waits for them, and re-layouts: 8.78 us -> 6.58 us
  blocking collectives: 38.5 us -> 37.3 us
  Pallas kernels: 6.94 us -> 8.06 us
  other arithmetic: 2.19 us -> 1.07 us
    all_to_all x1, starting transfers between devices: 6.29 us -> 11 us  [on_device(): share = lax.all_to_all(share, 'z', 0, 0, tiled=True)]
    all_to_all x1, blocking collectives: 18.2 us -> 14.2 us  [on_device(): share = lax.all_to_all(share.astype(bf16), PLANE, 0, 0, tiled=True)]
    all_to_all x1, waiting for transfers between devices: 7.79 us -> 4.36 us  [spread(): lax.all_to_all(jnp.broadcast_to(block[None], (count,) + block.shape), axe...]
    all_to_all x1, waiting for transfers between devices: 14.3 us -> 11 us  [on_device(): share = lax.all_to_all(share, 'z', 0, 0, tiled=True)]
    all_to_all x1, blocking collectives: 20.3 us -> 23.1 us  [spread(): lax.all_to_all(jnp.broadcast_to(block[None], (count,) + block.shape), axe...]
    unnamed x26 -> x20, local copies, waits for them, and re-layouts: 6.06 us -> 3.99 us
    ppermute x1 -> x2, starting transfers between devices: 1.91 us -> 3.95 us  [the longest x1 2.04 us: on_device(): share = keep.astype(f32) + lax.ppermute(send, 'co', swap).astype(f32)]
    ppermute x1 -> x2, waiting for transfers between devices: 2.44 us -> 4.1 us  [the longest x1 2.44 us: on_device(): other = lax.ppermute(own, 'co', swap)]
  transfers between devices with their start and end apart: 4 -> 5, of which waited for: 3 -> 4; matrix products, arithmetic and copies ran while one was open for 2% -> 1% of each run, Pallas kernels for 3% -> 3%
where the time goes in v3:
time: 106 us
  blocking collectives  37.3 us (35%)
  starting transfers between devices  32.1 us (30%)
  waiting for transfers between devices  19.5 us (18%)
  Pallas kernels  8.06 us (8%)
  local copies, waits for them, and re-layouts  6.58 us (6%)
  other arithmetic  1.07 us (1%)
    all_to_all x1, blocking collectives, spread(): lax.all_to_all(jnp.broadcast_to(block[None], (count,) + block.shape), axe...  23.1 us
    all_to_all x1, starting transfers between devices, spread(): lax.all_to_all(jnp.broadcast_to(block[None], (count,) + block.shape), axe...  15.2 us
    all_to_all x1, blocking collectives, on_device(): share = lax.all_to_all(share.astype(bf16), PLANE, 0, 0, tiled=True)  14.2 us
    all_to_all x1, waiting for transfers between devices, on_device(): share = lax.all_to_all(share, 'z', 0, 0, tiled=True)  11 us
    all_to_all x1, starting transfers between devices, on_device(): share = lax.all_to_all(share, 'z', 0, 0, tiled=True)  11 us
    pallas_call x4, Pallas kernels, call(): pl.pallas_call(kernel, out_shape=tuple((jax.ShapeDtypeStruct(s, d) for s,...  8.06 us
    all_to_all x1, waiting for transfers between devices, spread(): lax.all_to_all(jnp.broadcast_to(block[None], (count,) + block.shape), axe...  4.36 us
    unnamed x20, local copies, waits for them, and re-layouts  3.99 us
  transfers between devices with their start and end apart: 5, of which 4 were waited for; matrix products, arithmetic and copies ran while one was open for 1% of the time, Pallas kernels for 3%

profile of v3, /device:TPU:2, one launch (start us, length us, event | category | flops | bytes accessed | tf_op | source)
XLA Modules:
  0.0 105.5 jit_solution(16987222415302270679)
XLA Ops:
  0.6 1.0 reshape.264
  1.7 0.7 broadcast_in_dim.14
  2.4 15.2 %all-to-all-start = ((bf16[16,7,2,128]{3,2,1,0:T(2,128)(2,1)}), bf16[16,7,2,128]{3,2,1,0:T(2,128)(2,1)S(1)}, u32[]{:S(2)}, u32[]{:S(2)}) async-start(bf16[16,7,2,128]{3,2,1,0:T(2,128)(2,1)} %broadcast_in_dim.14), calls=%async_computation | async-start | bytes 114688 | tf_op jit(solution)/shard_map/all_to_all | solution.py:172
  17.6 1.9 %collective-permute-start = (bf16[2,256,768]{2,1,0:T(8,128)(2,1)}, bf16[2,256,768]{2,1,0:T(8,128)(2,1)S(1)}, u32[]{:S(2)}, u32[]{:S(2)}) collective-permute-start(bf16[2,256,768]{2,1,0:T(8,128)(2,1)} %bitcast.13), channel_id=1, source_target_pairs={{1,0},{2,1},{3,2},{4,3},{5,4},{6,5},{7,6},{8,7},{9,8},{10,9},{11,1... | collective-permute-start | bytes 2359304 | tf_op jit(solution)/shard_map/ppermute | solution.py:225
  19.6 0.7 broadcast_in_dim.12.gain_ref
  20.3 0.0 copy-start
  20.3 1.2 %copy-done = bf16[384,1152]{1,0:T(8,128)(2,1)S(1)} copy-done((bf16[384,1152]{1,0:T(8,128)(2,1)S(1)}, bf16[384,1152]{1,0:T(8,128)(2,1)}, u32[]{:S(2)}) %copy-start) | copy-done | bytes 884760
  21.4 0.0 copy-start.2
  21.4 1.0 copy-done.2
  22.4 1.4 %shard_map.77 = (bf16[2,256,384]{2,1,0:T(8,128)(2,1)S(1)}, bf16[2,256,1152]{2,1,0:T(8,128)(2,1)S(1)}, f32[2,256,256]{2,1,0:T(8,128)S(1)}) custom-call(bf16[2,256,384]{2,1,0:T(8,128)(2,1)S(1)} %bitcast.11, f32[1,384]{1,0:T(1,128)S(1)} %broadcast_in_dim.12.gain_ref, bf16[384,1152]{1,0:T(8,128)(2,1)S(1)} %copy-done), custom_call_target="tpu_custom_call" | custom-call | flops 553648128 | bytes 3376640 | tf_op jit(solution)/shard_map/pallas_call | solution.py:159
  23.8 0.0 copy-start.6
  23.8 1.0 copy-done.6
  24.9 0.0 copy-start.8
  24.9 0.7 copy-done.8
  25.7 0.1 broadcast_compare_fusion
  25.8 0.1 fusion.order_ref
  25.9 4.4 %all-to-all-done = bf16[16,7,2,128]{3,2,1,0:T(2,128)(2,1)S(1)} async-done(((bf16[16,7,2,128]{3,2,1,0:T(2,128)(2,1)}), bf16[16,7,2,128]{3,2,1,0:T(2,128)(2,1)S(1)}, u32[]{:S(2)}, u32[]{:S(2)}) %all-to-all-start) | async-done | bytes 57376 | tf_op jit(solution)/shard_map/all_to_all | solution.py:172
  30.3 0.0 collective-permute-done.next_any
  30.4 0.0 copy-start.4
  30.4 0.0 copy-start.5
  30.4 0.0 copy-start.7
  30.4 0.0 copy-start.9
  30.4 0.1 broadcast_in_dim.15
  30.5 23.1 %all_to_all.20.own_ref = bf16[16,7,32,128]{3,2,1,0:T(8,128)(2,1)S(1)} all-to-all(bf16[16,7,32,128]{3,2,1,0:T(8,128)(2,1)S(1)} %broadcast_in_dim.15), channel_id=1, replica_groups=mesh['xh'=2,'z'=16,'y'=4,'xl'=2,'co'=2] {'xh','y','xl'}, dimensions={0} | all-to-all | bytes 1835008 | tf_op jit(solution)/shard_map/all_to_all | solution.py:172
  53.6 1.9 %collective-permute-start.1 = (bf16[16,7,32,128]{3,2,1,0:T(8,128)(2,1)S(1)}, bf16[16,7,32,128]{3,2,1,0:T(8,128)(2,1)S(1)}, u32[]{:S(2)}, u32[]{:S(2)}) collective-permute-start(bf16[16,7,32,128]{3,2,1,0:T(8,128)(2,1)S(1)} %all_to_all.20.own_ref), channel_id=1, source_target_pairs={{0,1},{1,0},{2,3},{3,2},{4,5},{5,4},{6,7},{7,6},{8,9},{9,8},{10,11... | collective-permute-start | bytes 2752520 | tf_op jit(solution)/shard_map/ppermute | solution.py:245
  55.6 2.4 %collective-permute-done.1.other_ref = bf16[16,7,32,128]{3,2,1,0:T(8,128)(2,1)S(1)} collective-permute-done((bf16[16,7,32,128]{3,2,1,0:T(8,128)(2,1)S(1)}, bf16[16,7,32,128]{3,2,1,0:T(8,128)(2,1)S(1)}, u32[]{:S(2)}, u32[]{:S(2)}) %collective-permute-start.1) | collective-permute-done | bytes 917536 | tf_op jit(solution)/shard_map/ppermute | solution.py:245
  58.0 0.0 copy-done.4
  58.0 0.0 copy-done.5
  58.0 0.0 copy-done.7
  58.0 0.0 copy-done.9
  58.0 4.1 %shard_map.78 = (bf16[2,256,384]{2,1,0:T(8,128)(2,1)S(1)}, bf16[2,256,1152]{2,1,0:T(8,128)(2,1)S(1)}, bf16[16,112,128]{2,1,0:T(8,128)(2,1)S(1)}, bf16[16,112,128]{2,1,0:T(8,128)(2,1)S(1)}) custom-call(s32[1]{0:T(128)} %bitcast.1.core_ref, bf16[2,256,768]{2,1,0:T(8,128)(2,1)S(1)} %bitcast.14, bf16[2,256,768]{2,1,0:T(8,128)(2,1)S(1)} %collective-permute-done.next_any, ...), custom_call_target="tpu_custom_call" | custom-call | flops 2063597568 | bytes 8585220 | tf_op jit(solution)/shard_map/pallas_call | solution.py:159
  62.1 2.0 %collective-permute-start.2 = (bf16[16,112,128]{2,1,0:T(8,128)(2,1)S(1)}, bf16[16,112,128]{2,1,0:T(8,128)(2,1)S(1)}, u32[]{:S(2)}, u32[]{:S(2)}) collective-permute-start(bf16[16,112,128]{2,1,0:T(8,128)(2,1)S(1)} %get-tuple-element.28), channel_id=1, source_target_pairs={{0,1},{1,0},{2,3},{3,2},{4,5},{5,4},{6,7},{7,6},{8,9},{9,8},{10,11... | collective-permute-start | bytes 1376264 | tf_op jit(solution)/shard_map/ppermute | solution.py:260
  64.1 1.7 %collective-permute-done.2 = bf16[16,112,128]{2,1,0:T(8,128)(2,1)S(1)} collective-permute-done((bf16[16,112,128]{2,1,0:T(8,128)(2,1)S(1)}, bf16[16,112,128]{2,1,0:T(8,128)(2,1)S(1)}, u32[]{:S(2)}, u32[]{:S(2)}) %collective-permute-start.2) | collective-permute-done | bytes 458784 | tf_op jit(solution)/shard_map/ppermute | solution.py:260
  65.8 0.2 add_convert_fusion
  65.9 0.0 copy-start.1
  66.0 0.0 copy-start.3
  66.0 14.2 %all_to_all.21.got_ref = bf16[16,112,128]{2,1,0:T(8,128)(2,1)S(1)} all-to-all(bf16[16,112,128]{2,1,0:T(8,128)(2,1)S(1)} %add_convert_fusion), channel_id=1, replica_groups=mesh['xh'=2,'z'=16,'y'=4,'xl'=2,'co'=2] {'xh','y','xl'}, dimensions={0} | all-to-all | bytes 917504 | tf_op jit(solution)/shard_map/all_to_all | solution.py:261
  80.2 0.9 shard_map.80
  81.1 11.0 %all-to-all-start.3 = ((bf16[16,16,128]{2,1,0:T(8,128)(2,1)}), bf16[16,16,128]{2,1,0:T(8,128)(2,1)S(1)}, u32[]{:S(2)}, u32[]{:S(2)}) async-start(bf16[16,16,128]{2,1,0:T(8,128)(2,1)} %shard_map.80), calls=%async_computation.3 | async-start | bytes 131072 | tf_op jit(solution)/shard_map/all_to_all | solution.py:276
  92.1 0.0 copy-done.1
  92.1 0.0 copy-done.3
  92.1 1.7 %shard_map.79 = bf16[2,256,384]{2,1,0:T(8,128)(2,1)} custom-call(bf16[2,256,384]{2,1,0:T(8,128)(2,1)S(1)} %bitcast.12, f32[1,384]{1,0:T(1,128)S(1)} %broadcast_in_dim.12.gain_ref, bf16[384,1152]{1,0:T(8,128)(2,1)S(1)} %copy-done.1, bf16[2,256,1152]{2,1,0:T(8,128)(2,1)S(1)} %get-tuple-element.25.qkv_cot_ref, ...), custom_call_target="tpu_custom_call" | custom-call | flops 452984832 | bytes 3245568 | tf_op jit(solution)/shard_map/pallas_call | solution.py:159
  93.9 11.0 %all-to-all-done.3 = bf16[16,16,128]{2,1,0:T(8,128)(2,1)S(1)} async-done(((bf16[16,16,128]{2,1,0:T(8,128)(2,1)}), bf16[16,16,128]{2,1,0:T(8,128)(2,1)S(1)}, u32[]{:S(2)}, u32[]{:S(2)}) %all-to-all-start.3) | async-done | bytes 65568 | tf_op jit(solution)/shard_map/all_to_all | solution.py:276
  104.9 0.6 convert_reduce_fusion
  (9 shorter events, 0.2 us)
Async XLA Ops:
  2.4 27.9 %all-to-all-start = ((bf16[16,7,2,128]{3,2,1,0:T(2,128)(2,1)}), bf16[16,7,2,128]{3,2,1,0:T(2,128)(2,1)S(1)}, u32[]{:S(2)}, u32[]{:S(2)}) async-start(bf16[16,7,2,128]{3,2,1,0:T(2,128)(2,1)} %broadcast_in_dim.14), calls=%async_computation | async-start | bytes 114688 | tf_op jit(solution)/shard_map/all_to_all | solution.py:172
  17.6 12.7 %collective-permute-start = (bf16[2,256,768]{2,1,0:T(8,128)(2,1)}, bf16[2,256,768]{2,1,0:T(8,128)(2,1)S(1)}, u32[]{:S(2)}, u32[]{:S(2)}) collective-permute-start(bf16[2,256,768]{2,1,0:T(8,128)(2,1)} %bitcast.13), channel_id=1, source_target_pairs={{1,0},{2,1},{3,2},{4,3},{5,4},{6,5},{7,6},{8,7},{9,8},{10,9},{11,1... | collective-permute-start | bytes 2359304 | tf_op jit(solution)/shard_map/ppermute | solution.py:225
  20.3 1.2 %copy-start = (bf16[384,1152]{1,0:T(8,128)(2,1)S(1)}, bf16[384,1152]{1,0:T(8,128)(2,1)}, u32[]{:S(2)}) copy-start(bf16[384,1152]{1,0:T(8,128)(2,1)} %weight_ref.3) | copy-start | bytes 2654212
  21.4 1.0 copy-start.2
  23.8 1.1 %copy-start.6 = (bf16[2,256,1152]{2,1,0:T(8,128)(2,1)}, bf16[2,256,1152]{2,1,0:T(8,128)(2,1)S(1)}, u32[]{:S(2)}) copy-start(bf16[2,256,1152]{2,1,0:T(8,128)(2,1)S(1)} %get-tuple-element.22.qkv_ref) | copy-start | bytes 3538948
  24.9 0.7 copy-start.8
  30.4 27.6 %copy-start.4 = (bf16[1,2,256,768]{3,2,1,0:T(8,128)(2,1)S(1)}, bf16[1,2,256,768]{3,2,1,0:T(8,128)(2,1)}, u32[]{:S(2)}) copy-start(bf16[1,2,256,768]{3,2,1,0:T(8,128)(2,1)} %param.11) | copy-start | bytes 2359300
  30.4 27.6 %copy-start.5 = (bf16[384,384]{1,0:T(8,128)(2,1)S(1)}, bf16[384,384]{1,0:T(8,128)(2,1)}, u32[]{:S(2)}) copy-start(bf16[384,384]{1,0:T(8,128)(2,1)} %out_weight_ref.1) | copy-start | bytes 884740
  30.4 27.6 %copy-start.7 = (bf16[2,256,1152]{2,1,0:T(8,128)(2,1)S(1)}, bf16[2,256,1152]{2,1,0:T(8,128)(2,1)}, u32[]{:S(2)}) copy-start(bf16[2,256,1152]{2,1,0:T(8,128)(2,1)} %copy-done.6) | copy-start | bytes 3538948
  30.4 27.6 %copy-start.9 = (bf16[2,256,384]{2,1,0:T(8,128)(2,1)S(1)}, bf16[2,256,384]{2,1,0:T(8,128)(2,1)}, u32[]{:S(2)}) copy-start(bf16[2,256,384]{2,1,0:T(8,128)(2,1)} %copy-done.8) | copy-start | bytes 1179652
  53.6 4.4 %collective-permute-start.1 = (bf16[16,7,32,128]{3,2,1,0:T(8,128)(2,1)S(1)}, bf16[16,7,32,128]{3,2,1,0:T(8,128)(2,1)S(1)}, u32[]{:S(2)}, u32[]{:S(2)}) collective-permute-start(bf16[16,7,32,128]{3,2,1,0:T(8,128)(2,1)S(1)} %all_to_all.20.own_ref), channel_id=1, source_target_pairs={{0,1},{1,0},{2,3},{3,2},{4,5},{5,4},{6,7},{7,6},{8,9},{9,8},{10,11... | collective-permute-start | bytes 2752520 | tf_op jit(solution)/shard_map/ppermute | solution.py:245
  62.1 3.7 %collective-permute-start.2 = (bf16[16,112,128]{2,1,0:T(8,128)(2,1)S(1)}, bf16[16,112,128]{2,1,0:T(8,128)(2,1)S(1)}, u32[]{:S(2)}, u32[]{:S(2)}) collective-permute-start(bf16[16,112,128]{2,1,0:T(8,128)(2,1)S(1)} %get-tuple-element.28), channel_id=1, source_target_pairs={{0,1},{1,0},{2,3},{3,2},{4,5},{5,4},{6,7},{7,6},{8,9},{9,8},{10,11... | collective-permute-start | bytes 1376264 | tf_op jit(solution)/shard_map/ppermute | solution.py:260
  65.9 26.2 %copy-start.1 = (bf16[384,1152]{1,0:T(8,128)(2,1)S(1)}, bf16[384,1152]{1,0:T(8,128)(2,1)}, u32[]{:S(2)}) copy-start(bf16[384,1152]{1,0:T(8,128)(2,1)} %weight_ref.3) | copy-start | bytes 2654212
  66.0 26.2 %copy-start.3 = (bf16[1,2,256,384]{3,2,1,0:T(8,128)(2,1)S(1)}, bf16[1,2,256,384]{3,2,1,0:T(8,128)(2,1)}, u32[]{:S(2)}) copy-start(bf16[1,2,256,384]{3,2,1,0:T(8,128)(2,1)} %param.6) | copy-start | bytes 1179652
  81.1 23.8 %all-to-all-start.3 = ((bf16[16,16,128]{2,1,0:T(8,128)(2,1)}), bf16[16,16,128]{2,1,0:T(8,128)(2,1)S(1)}, u32[]{:S(2)}, u32[]{:S(2)}) async-start(bf16[16,16,128]{2,1,0:T(8,128)(2,1)} %shard_map.80), calls=%async_computation.3 | async-start | bytes 131072 | tf_op jit(solution)/shard_map/all_to_all | solution.py:276

commit v4 on v3

--- a/solution.py
+++ b/solution.py
@@ -27,7 +27,7 @@
 
 
 def forward_kernel(clip_ref, gain_ref, weight_ref, normed_ref, qkv_ref, prob_ref):
-    frames, positions, width = clip_ref.shape
+    frames, _, width = clip_ref.shape
     for f in range(frames):
         features = clip_ref[f].astype(f32)
         squares = jnp.mean(features * features, axis=-1, keepdims=True)
@@ -138,7 +138,7 @@
 
 
 def input_kernel(clip_ref, gain_ref, weight_ref, qkv_cot_ref, upstream_ref, out_ref):
-    frames, positions, width = clip_ref.shape
+    frames, _, _ = clip_ref.shape
     for f in range(frames):
         features = clip_ref[f].astype(f32)
         squares = jnp.mean(features * features, axis=-1, keepdims=True)
@@ -174,7 +174,7 @@
     )
 
 
-def tap_column(shard):
+def tap_column(shard, core, group):
     taps, held, wide = shard.shape
     lanes, parts = wide // LANES, held // 4
     tiles = shard.reshape(taps, 2, parts, 2, lanes, LANES).transpose(1, 0, 4, 2, 3, 5)
@@ -183,12 +183,14 @@
     tiles = jnp.concatenate([tiles, jnp.zeros((2, PIECES * TILES - count, 2, LANES), bf16)], 1)
     tiles = tiles.reshape(2 * PIECES, TILES, 2, LANES)
     place = lax.axis_index("y") * lax.axis_size("xl") + lax.axis_index("xl")
-    place = place + lax.axis_index("co") * PIECES
-    column = spread(lax.dynamic_index_in_dim(tiles, place, 0, keepdims=False), ("z",))
-    return column.transpose(1, 0, 2, 3).reshape(TILES, -1, LANES)
-
-
-def channel_order(width):
+    place = place + core * PIECES
+    piece = lax.dynamic_index_in_dim(tiles, place, 0, keepdims=False)
+    piece, core, group = lax.optimization_barrier((piece, core, group))
+    column = spread(piece, ("z",))
+    return column.transpose(1, 0, 2, 3).reshape(TILES, -1, LANES), core, group
+
+
+def channel_order(width, core):
     depth, groups = lax.axis_size("z"), lax.axis_size("xh")
     held = width // (depth * groups)
     parts = held // 4
@@ -197,13 +199,12 @@
     level, place = place % depth, place // depth
     part, place = place % parts, place // parts
     group, half = place % groups, place // groups
-    side = jnp.where(lax.axis_index("co") == 0, half, 1 - half)
+    side = jnp.where(core == 0, half, 1 - half)
     channel = held * (group * depth + level) + (held // 2) * side + 2 * part + row
     return (channel[:, None] == jnp.arange(width)[None, :]).astype(bf16)
 
 
-def turn_orders(held, depth):
-    group = lax.axis_index("xh")
+def turn_orders(held, depth, group):
     row = jnp.arange(depth * 16)
     channel = jnp.where(row % 16 < held, row // 16 * held + row % 16, -1)[:, None]
     lane = jnp.arange(LANES)[None, :]
@@ -222,8 +223,17 @@
     clips = math.prod(lax.axis_size(a) for a in DP)
     gain = norm_gain[None]
 
+    depth = lax.axis_size("z")
+    held = width // clips
+    swap = [(0, 1), (1, 0)]
     incoming = lax.ppermute(cotangent, TM, [(i + 1, i) for i in range(slabs - 1)])
-    column = tap_column(time_weight)
+    column, core, group = tap_column(
+        time_weight, lax.axis_index("co"), lax.axis_index("xh")
+    )
+    column, core, group = lax.optimization_barrier((column, core, group))
+    own = spread(column, PLANE)
+    own, clip, core, group = lax.optimization_barrier((own, clip, core, group))
+    other = lax.ppermute(own, "co", swap)
     normed, qkv, prob = call(
         forward_kernel,
         [((frames, positions, width), bf16), ((frames, positions, 3 * width), bf16),
@@ -232,17 +242,9 @@
         2 * rows * width * (3 * width + positions),
         16,
     )
-    depth = lax.axis_size("z")
-    held = width // clips
-    order = channel_order(width)
-    turn = turn_orders(held, depth)
-    core = lax.axis_index("co").reshape(1)
-    column, incoming, normed, qkv, prob, order, turn = lax.optimization_barrier(
-        (column, incoming, normed, qkv, prob, order, turn)
-    )
-    own = spread(column, PLANE)
-    swap = [(0, 1), (1, 0)]
-    other = lax.ppermute(own, "co", swap)
+    order = channel_order(width, core)
+    turn = turn_orders(held, depth, group)
+    core = core.reshape(1)
 
     chips = own.shape[0]
     packed = ((chips, 112, LANES), bf16)
@@ -257,8 +259,7 @@
          pltpu.SemaphoreType.DMA((2,))],
         [pl.BlockSpec(memory_space=pltpu.SMEM)] + [pl.BlockSpec(memory_space=pl.ANY)] * 2 + whole(7),
     )
-    share = keep.astype(f32) + lax.ppermute(send, "co", swap).astype(f32)
-    share = lax.all_to_all(share.astype(bf16), PLANE, 0, 0, tiled=True)
+    got = lax.ppermute(send, "co", swap)
     (input_grad,) = call(
         input_kernel,
         [((frames, positions, width), bf16)],
@@ -266,6 +267,9 @@
         2 * rows * width * 3 * width,
         16,
     )
+    got, input_grad, turn = lax.optimization_barrier((got, input_grad, turn))
+    share = (keep.astype(f32) + got.astype(f32)).astype(bf16)
+    share = lax.all_to_all(share, PLANE, 0, 0, tiled=True)
     (share,) = call(
         turn_kernel,
         [((depth, 16, LANES), bf16)],
@@ -289,6 +293,7 @@
         P(DP, TM, None, None),
     )
     out_specs = (P(DP, TM, None, None), P(DP, TM))
+
     return jax.shard_map(
         on_device, mesh=split, in_specs=in_specs, out_specs=out_specs, check_vma=False
     )

time: 106 us -> 107 us (level)
  blocking collectives: 37.3 us -> 77.3 us
  starting transfers between devices: 32.1 us -> 9.03 us
  waiting for transfers between devices: 19.5 us -> 8.17 us
  local copies, waits for them, and re-layouts: 6.58 us -> 1.3 us
    all_to_all x2 -> x0, starting transfers between devices: 26.2 us -> none  [the longest x1 15.2 us: spread(): lax.all_to_all(jnp.broadcast_to(block[None], (count,) + block.shape), axe...]
    all_to_all x1 -> x2, blocking collectives: 23.1 us -> 48.2 us  [spread(): lax.all_to_all(jnp.broadcast_to(block[None], (count,) + block.shape), axe...]
    all_to_all x2 -> x0, waiting for transfers between devices: 15.4 us -> none  [the longest x1 11 us: on_device(): share = lax.all_to_all(share, 'z', 0, 0, tiled=True)]
    all_to_all x1 -> x2, blocking collectives: 14.2 us -> 29 us  [the longest x1 15.6 us: on_device(): share = lax.all_to_all(share, 'z', 0, 0, tiled=True)]
    ppermute x1, waiting for transfers between devices: 0.01 us -> 8.16 us  [on_device(): lax.ppermute(cotangent, TM, [(i + 1, i) for i in range(slabs - 1)])]
    unnamed x20 -> x8, local copies, waits for them, and re-layouts: 3.99 us -> 0.03 us
    ppermute x1, waiting for transfers between devices: 2.44 us -> 0.01 us  [on_device(): other = lax.ppermute(own, 'co', swap)]
    ppermute x1, waiting for transfers between devices: 1.66 us -> 0.01 us  [on_device(): got = lax.ppermute(send, 'co', swap)]
  transfers between devices with their start and end apart: 5 -> 3, of which waited for: 4 -> 1; matrix products, arithmetic and copies ran while one was open for 1% -> 0% of each run, Pallas kernels for 3% -> 3%
where the time goes in v4:
time: 107 us; the launch traced here: 106 us
  blocking collectives  77.3 us (72%)
  starting transfers between devices  9.03 us (8%)
  Pallas kernels  8.41 us (8%)
  waiting for transfers between devices  8.17 us (8%)
  local copies, waits for them, and re-layouts  1.3 us (1%)
  other arithmetic  1.08 us (1%)
    all_to_all x2, blocking collectives, spread(): lax.all_to_all(jnp.broadcast_to(block[None], (count,) + block.shape), axe...  48.2 us
    all_to_all x1, blocking collectives, on_device(): share = lax.all_to_all(share, 'z', 0, 0, tiled=True)  15.6 us
    all_to_all x1, blocking collectives, on_device(): share = lax.all_to_all(share, PLANE, 0, 0, tiled=True)  13.5 us
    pallas_call x4, Pallas kernels, call(): pl.pallas_call(kernel, out_shape=tuple((jax.ShapeDtypeStruct(s, d) for s,...  8.41 us
    ppermute x1, waiting for transfers between devices, on_device(): lax.ppermute(cotangent, TM, [(i + 1, i) for i in range(slabs - 1)])  8.16 us
    ppermute x1, starting transfers between devices, on_device(): got = lax.ppermute(send, 'co', swap)  3.65 us
    ppermute x1, starting transfers between devices, on_device(): lax.ppermute(cotangent, TM, [(i + 1, i) for i in range(slabs - 1)])  3.47 us
  transfers between devices with their start and end apart: 3, of which 1 were waited for; matrix products, arithmetic and copies ran while one was open for 0% of the time, Pallas kernels for 3%

profile of v4, /device:TPU:2, one launch (start us, length us, event | category | flops | bytes accessed | tf_op | source)
XLA Modules:
  0.0 106.1 jit_solution(14363255136063399325)
XLA Ops:
  0.6 1.0 reshape.264
  1.8 27.7 %all_to_all.20 = bf16[16,7,2,128]{3,2,1,0:T(2,128)(2,1)S(1)} all-to-all(bf16[16,7,2,128]{3,2,1,0:T(2,128)(2,1)S(1)} %broadcast_in_dim.9), channel_id=1, replica_groups=mesh['xh'=2,'z'=16,'y'=4,'xl'=2,'co'=2] {'z'}, dimensions={0} | all-to-all | bytes 114688 | tf_op jit(solution)/shard_map/all_to_all | solution.py:172
  29.5 0.0 copy-start.3
  29.5 0.0 copy-start
  29.5 0.0 copy-start.1
  29.6 0.1 broadcast_in_dim.10
  29.7 20.5 %all_to_all.21.own_ref = bf16[16,7,32,128]{3,2,1,0:T(8,128)(2,1)S(1)} all-to-all(bf16[16,7,32,128]{3,2,1,0:T(8,128)(2,1)S(1)} %broadcast_in_dim.10), channel_id=1, replica_groups=mesh['xh'=2,'z'=16,'y'=4,'xl'=2,'co'=2] {'xh','y','xl'}, dimensions={0} | all-to-all | bytes 1835008 | tf_op jit(solution)/shard_map/all_to_all | solution.py:172
  50.2 1.9 %collective-permute-start.1 = (bf16[16,7,32,128]{3,2,1,0:T(8,128)(2,1)S(1)}, bf16[16,7,32,128]{3,2,1,0:T(8,128)(2,1)S(1)}, u32[]{:S(2)}, u32[]{:S(2)}) collective-permute-start(bf16[16,7,32,128]{3,2,1,0:T(8,128)(2,1)S(1)} %all_to_all.21.own_ref), channel_id=1, source_target_pairs={{0,1},{1,0},{2,3},{3,2},{4,5},{5,4},{6,7},{7,6},{8,9},{9,8},{10,11... | collective-permute-start | bytes 2752520 | tf_op jit(solution)/shard_map/ppermute | solution.py:236
  52.1 3.5 %collective-permute-start = (bf16[2,256,768]{2,1,0:T(8,128)(2,1)}, bf16[2,256,768]{2,1,0:T(8,128)(2,1)}, u32[]{:S(2)}, u32[]{:S(2)}) collective-permute-start(bf16[2,256,768]{2,1,0:T(8,128)(2,1)} %bitcast.8.cot_any), channel_id=1, source_target_pairs={{1,0},{2,1},{3,2},{4,3},{5,4},{6,5},{7,6},{8,7},{9,8},{10,9},{11,1... | collective-permute-start | bytes 2359304 | tf_op jit(solution)/shard_map/ppermute | solution.py:229
  55.6 0.0 copy-done.3
  55.7 0.0 copy-start.2
  55.7 0.0 copy-done
  55.7 0.0 copy-done.1
  55.7 1.4 %shard_map.77 = (bf16[2,256,384]{2,1,0:T(8,128)(2,1)S(1)}, bf16[2,256,1152]{2,1,0:T(8,128)(2,1)S(1)}, f32[2,256,256]{2,1,0:T(8,128)S(1)}) custom-call(bf16[2,256,384]{2,1,0:T(8,128)(2,1)S(1)} %bitcast.11, f32[1,384]{1,0:T(1,128)S(1)} %broadcast_in_dim.11.gain_ref, bf16[384,1152]{1,0:T(8,128)(2,1)S(1)} %copy-done), custom_call_target="tpu_custom_call" | custom-call | flops 553648128 | bytes 3376640 | tf_op jit(solution)/shard_map/pallas_call | solution.py:159
  57.1 0.1 fusion.order_ref
  57.3 8.2 %collective-permute-done.next_any = bf16[2,256,768]{2,1,0:T(8,128)(2,1)} collective-permute-done((bf16[2,256,768]{2,1,0:T(8,128)(2,1)}, bf16[2,256,768]{2,1,0:T(8,128)(2,1)}, u32[]{:S(2)}, u32[]{:S(2)}) %collective-permute-start) | collective-permute-done | bytes 786464 | tf_op jit(solution)/shard_map/ppermute | solution.py:229
  65.4 0.0 collective-permute-done.1.other_ref
  65.4 0.0 copy-done.2
  65.4 5.0 %shard_map.78 = (bf16[2,256,384]{2,1,0:T(8,128)(2,1)S(1)}, bf16[2,256,1152]{2,1,0:T(8,128)(2,1)S(1)}, bf16[16,112,128]{2,1,0:T(8,128)(2,1)S(1)}, bf16[16,112,128]{2,1,0:T(8,128)(2,1)S(1)}) custom-call(s32[1]{0:T(128)} %bitcast.7.core_ref, bf16[2,256,768]{2,1,0:T(8,128)(2,1)} %bitcast.8.cot_any, bf16[2,256,768]{2,1,0:T(8,128)(2,1)} %collective-permute-done.next_any, ...), custom_call_target="tpu_custom_call" | custom-call | flops 2063597568 | bytes 8585220 | tf_op jit(solution)/shard_map/pallas_call | solution.py:159
  70.5 3.6 %collective-permute-start.2 = (bf16[16,112,128]{2,1,0:T(8,128)(2,1)S(1)}, bf16[16,112,128]{2,1,0:T(8,128)(2,1)S(1)}, u32[]{:S(2)}, u32[]{:S(2)}) collective-permute-start(bf16[16,112,128]{2,1,0:T(8,128)(2,1)S(1)} %get-tuple-element.34), channel_id=1, source_target_pairs={{0,1},{1,0},{2,3},{3,2},{4,5},{5,4},{6,7},{7,6},{8,9},{9,8},{10,11... | collective-permute-start | bytes 1376264 | tf_op jit(solution)/shard_map/ppermute | solution.py:262
  74.1 0.1 broadcast_compare_fusion
  74.3 1.8 %shard_map.79 = bf16[2,256,384]{2,1,0:T(8,128)(2,1)} custom-call(bf16[2,256,384]{2,1,0:T(8,128)(2,1)S(1)} %bitcast.12, f32[1,384]{1,0:T(1,128)S(1)} %broadcast_in_dim.11.gain_ref, bf16[384,1152]{1,0:T(8,128)(2,1)S(1)} %copy-done, bf16[2,256,1152]{2,1,0:T(8,128)(2,1)S(1)} %get-tuple-element.35.qkv_cot_ref, bf16[2,256,384]{2,1,0:T(8,128)(2,1)S(1)} %get-tuple-element.36.upstream_ref), custom_call_target="tpu_custom_call" | custom-call | flops 452984832 | bytes 3245568 | tf_op jit(solution)/shard_map/pallas_call | solution.py:159
  76.0 0.0 collective-permute-done.2
  76.1 0.2 add_convert_fusion
  76.2 13.5 %all_to_all.22.got_ref = bf16[16,112,128]{2,1,0:T(8,128)(2,1)S(1)} all-to-all(bf16[16,112,128]{2,1,0:T(8,128)(2,1)S(1)} %add_convert_fusion), channel_id=1, replica_groups=mesh['xh'=2,'z'=16,'y'=4,'xl'=2,'co'=2] {'xh','y','xl'}, dimensions={0} | all-to-all | bytes 917504 | tf_op jit(solution)/shard_map/all_to_all | solution.py:272
  89.7 0.2 shard_map.80
  89.9 15.6 %all_to_all.23 = bf16[16,16,128]{2,1,0:T(8,128)(2,1)S(1)} all-to-all(bf16[16,16,128]{2,1,0:T(8,128)(2,1)S(1)} %shard_map.80), channel_id=1, replica_groups=mesh['xh'=2,'z'=16,'y'=4,'xl'=2,'co'=2] {'z'}, dimensions={0} | all-to-all | bytes 131072 | tf_op jit(solution)/shard_map/all_to_all | solution.py:280
  105.5 0.6 convert_reduce_fusion
  (11 shorter events, 0.3 us)
Async XLA Ops:
  29.5 26.1 %copy-start.3 = (f32[384]{0:T(512)S(1)}, f32[384]{0:T(512)}, u32[]{:S(2)}) copy-start(f32[384]{0:T(512)} %param.7) | copy-start | bytes 4612
  29.5 26.2 %copy-start = (bf16[384,1152]{1,0:T(8,128)(2,1)S(1)}, bf16[384,1152]{1,0:T(8,128)(2,1)}, u32[]{:S(2)}) copy-start(bf16[384,1152]{1,0:T(8,128)(2,1)} %weight_ref.3) | copy-start | bytes 2654212
  29.5 26.2 %copy-start.1 = (bf16[1,2,256,384]{3,2,1,0:T(8,128)(2,1)S(1)}, bf16[1,2,256,384]{3,2,1,0:T(8,128)(2,1)}, u32[]{:S(2)}) copy-start(bf16[1,2,256,384]{3,2,1,0:T(8,128)(2,1)} %param.6) | copy-start | bytes 1179652
  50.2 15.2 %collective-permute-start.1 = (bf16[16,7,32,128]{3,2,1,0:T(8,128)(2,1)S(1)}, bf16[16,7,32,128]{3,2,1,0:T(8,128)(2,1)S(1)}, u32[]{:S(2)}, u32[]{:S(2)}) collective-permute-start(bf16[16,7,32,128]{3,2,1,0:T(8,128)(2,1)S(1)} %all_to_all.21.own_ref), channel_id=1, source_target_pairs={{0,1},{1,0},{2,3},{3,2},{4,5},{5,4},{6,7},{7,6},{8,9},{9,8},{10,11... | collective-permute-start | bytes 2752520 | tf_op jit(solution)/shard_map/ppermute | solution.py:236
  52.1 13.3 %collective-permute-start = (bf16[2,256,768]{2,1,0:T(8,128)(2,1)}, bf16[2,256,768]{2,1,0:T(8,128)(2,1)}, u32[]{:S(2)}, u32[]{:S(2)}) collective-permute-start(bf16[2,256,768]{2,1,0:T(8,128)(2,1)} %bitcast.8.cot_any), channel_id=1, source_target_pairs={{1,0},{2,1},{3,2},{4,3},{5,4},{6,5},{7,6},{8,7},{9,8},{10,9},{11,1... | collective-permute-start | bytes 2359304 | tf_op jit(solution)/shard_map/ppermute | solution.py:229
  55.7 9.8 %copy-start.2 = (bf16[384,384]{1,0:T(8,128)(2,1)S(1)}, bf16[384,384]{1,0:T(8,128)(2,1)}, u32[]{:S(2)}) copy-start(bf16[384,384]{1,0:T(8,128)(2,1)} %out_weight_ref.1) | copy-start | bytes 884740
  70.5 5.6 %collective-permute-start.2 = (bf16[16,112,128]{2,1,0:T(8,128)(2,1)S(1)}, bf16[16,112,128]{2,1,0:T(8,128)(2,1)S(1)}, u32[]{:S(2)}, u32[]{:S(2)}) collective-permute-start(bf16[16,112,128]{2,1,0:T(8,128)(2,1)S(1)} %get-tuple-element.34), channel_id=1, source_target_pairs={{0,1},{1,0},{2,3},{3,2},{4,5},{5,4},{6,7},{7,6},{8,9},{9,8},{10,11... | collective-permute-start | bytes 1376264 | tf_op jit(solution)/shard_map/ppermute | solution.py:262

commit v5 on v4

--- a/solution.py
+++ b/solution.py
@@ -41,9 +41,8 @@
 
 
 def backward_kernel(
-    core_ref, cot_any, next_any, own_ref, other_ref, order_ref, out_weight_ref, qkv_ref, prob_ref,
-    normed_ref, upstream_ref, qkv_cot_ref, keep_ref, send_ref, taps_ref, cot_ref, next_ref,
-    grad_ref, sems,
+    core_ref, cot_ref, next_any, own_ref, other_ref, order_ref, out_weight_ref, qkv_ref, prob_ref,
+    normed_ref, upstream_ref, qkv_cot_ref, keep_ref, send_ref, taps_ref, next_ref, grad_ref, sem,
 ):
     frames, positions, width = upstream_ref.shape
     rows = frames * positions
@@ -53,12 +52,8 @@
     groups = own_ref.shape[0] // PIECES
     lanes = wide // LANES
     parts = width // (2 * groups * block)
-    copies = [
-        pltpu.make_async_copy(cot_any, cot_ref, sems.at[0]),
-        pltpu.make_async_copy(next_any, next_ref, sems.at[1]),
-    ]
-    for copy in copies:
-        copy.start()
+    copy = pltpu.make_async_copy(next_any, next_ref, sem)
+    copy.start()
     for half, source in enumerate((own_ref, other_ref)):
         for group in range(groups):
             for tile in range(taps * lanes * parts):
@@ -68,10 +63,9 @@
                 taps_ref[tap, start : start + block, lane * LANES : (lane + 1) * LANES] = source[
                     group * PIECES + tile // TILES, tile % TILES
                 ]
-    for copy in copies:
-        copy.wait()
+    total = dot(cot_ref[...].reshape(rows, wide), taps_ref[2], NT)
+    copy.wait()
     middle = jnp.concatenate([cot_ref[1], next_ref[0]], axis=0)
-    total = dot(cot_ref[...].reshape(rows, wide), taps_ref[2], NT)
     total = total + dot(middle, taps_ref[1], NT)
     total = total + dot(next_ref[...].reshape(rows, wide), taps_ref[0], NT)
     upstream = dot(total.astype(bf16), order_ref[...], NN).astype(bf16)
@@ -124,17 +118,38 @@
 
 def turn_kernel(got_ref, turn_ref, out_ref):
     columns, short = 72, got_ref.shape[1] - 72
+    depth = out_ref.shape[0]
     total = got_ref[0].astype(f32)
     for i in range(1, got_ref.shape[0]):
         total = total + got_ref[i].astype(f32)
     narrow = total[columns:]
     other = pltpu.roll(narrow, LANES // 2, 1)
-    narrow = jnp.concatenate([narrow, other[2 * short - columns :]], axis=0)
-    turned = dot(turn_ref[0], total[:columns].astype(bf16), NT)
-    turned = turned + dot(turn_ref[1], narrow.astype(bf16), NT)
-    turned = turned.astype(bf16).reshape(out_ref.shape[0], 16, columns)
-    out_ref[...] = jnp.zeros_like(out_ref)
-    out_ref[:, :, :columns] = turned
+    empty = jnp.zeros((LANES - columns, LANES), f32)
+    narrow = jnp.concatenate([narrow, other[2 * short - columns :], empty], axis=0)
+    wide = jnp.concatenate([total[:columns], empty], axis=0)
+    turned = dot(turn_ref[0], wide.astype(bf16), NT) + dot(turn_ref[1], narrow.astype(bf16), NT)
+    first, last = turned[: depth * 8], turned[depth * 8 :]
+    row = lax.broadcasted_iota(jnp.int32, first.shape, 0)
+    lane = lax.broadcasted_iota(jnp.int32, first.shape, 1)
+    last = jnp.where(
+        lax.rem(row, 2) == 0, pltpu.roll(last, columns, 1), pltpu.roll(last, columns // 2, 1)
+    )
+    turned = jnp.where(lane < columns, first, last)
+    out_ref[...] = turned.astype(bf16).reshape(out_ref.shape)
+
+
+def final_kernel(got_ref, out_ref):
+    columns = out_ref.shape[1]
+    total = got_ref[0].astype(f32)
+    for i in range(1, got_ref.shape[0]):
+        total = total + got_ref[i].astype(f32)
+    out_ref[0:8] = total[:, :columns]
+    even = pltpu.roll(total, LANES - columns, 1)
+    odd = pltpu.roll(total, LANES - columns // 2, 1)
+    left = lax.broadcasted_iota(jnp.int32, (1, LANES), 1) < columns // 2
+    for i in range(4):
+        line = jnp.where(left, even[2 * i : 2 * i + 1], odd[2 * i + 1 : 2 * i + 2])
+        out_ref[8 + i : 9 + i] = line[:, :columns]
 
 
 def input_kernel(clip_ref, gain_ref, weight_ref, qkv_cot_ref, upstream_ref, out_ref):
@@ -174,19 +189,39 @@
     )
 
 
+def piece_kernel(place_ref, shard_ref, out_ref, tiles_ref):
+    taps, held, wide = shard_ref.shape
+    lanes, parts = wide // LANES, held // 4
+    count = taps * lanes * parts
+    slots = PIECES * TILES
+    for side in range(2):
+        for tile in range(count):
+            tap, rest = divmod(tile, lanes * parts)
+            lane, part = divmod(rest, parts)
+            row = side * held // 2 + 2 * part
+            tiles_ref[side * slots + tile] = shard_ref[
+                tap, row : row + 2, lane * LANES : (lane + 1) * LANES
+            ]
+        for tile in range(count, slots):
+            tiles_ref[side * slots + tile] = jnp.zeros((2, LANES), bf16)
+    piece = tiles_ref[pl.ds(place_ref[0] * TILES, TILES)]
+    for i in range(out_ref.shape[0]):
+        out_ref[i] = piece
+
+
 def tap_column(shard, core, group):
-    taps, held, wide = shard.shape
-    lanes, parts = wide // LANES, held // 4
-    tiles = shard.reshape(taps, 2, parts, 2, lanes, LANES).transpose(1, 0, 4, 2, 3, 5)
-    count = taps * lanes * parts
-    tiles = tiles.reshape(2, count, 2, LANES)
-    tiles = jnp.concatenate([tiles, jnp.zeros((2, PIECES * TILES - count, 2, LANES), bf16)], 1)
-    tiles = tiles.reshape(2 * PIECES, TILES, 2, LANES)
-    place = lax.axis_index("y") * lax.axis_size("xl") + lax.axis_index("xl")
-    place = place + core * PIECES
-    piece = lax.dynamic_index_in_dim(tiles, place, 0, keepdims=False)
+    place = lax.axis_index("y") * lax.axis_size("xl") + lax.axis_index("xl") + core * PIECES
+    (piece,) = call(
+        piece_kernel,
+        [((lax.axis_size("z"), TILES, 2, LANES), bf16)],
+        [place.reshape(1), shard],
+        0,
+        8,
+        [pltpu.VMEM((2 * PIECES * TILES, 2, LANES), bf16)],
+        [pl.BlockSpec(memory_space=pltpu.SMEM)] + whole(1),
+    )
     piece, core, group = lax.optimization_barrier((piece, core, group))
-    column = spread(piece, ("z",))
+    column = lax.all_to_all(piece, ("z",), 0, 0, tiled=True)
     return column.transpose(1, 0, 2, 3).reshape(TILES, -1, LANES), core, group
 
 
@@ -205,8 +240,10 @@
 
 
 def turn_orders(held, depth, group):
-    row = jnp.arange(depth * 16)
-    channel = jnp.where(row % 16 < held, row // 16 * held + row % 16, -1)[:, None]
+    row = jnp.arange(depth * 8)
+    first = row // 8 * held + row % 8
+    last = row // 8 * held + 8 + row % 8 // 2
+    channel = jnp.concatenate([first, last])[:, None]
     lane = jnp.arange(LANES)[None, :]
     wide = channel == lane + 64 * group
     narrow = (channel == lane + LANES * (1 - group)) & (lane < 64)
@@ -255,9 +292,9 @@
         2 * rows * width * (3 * wide + 2 * width + 4 * positions + 3 * width),
         32,
         [pltpu.VMEM((3, width, wide), bf16), pltpu.VMEM(cotangent.shape, bf16),
-         pltpu.VMEM(cotangent.shape, bf16), pltpu.VMEM((3 * width, width), f32),
-         pltpu.SemaphoreType.DMA((2,))],
-        [pl.BlockSpec(memory_space=pltpu.SMEM)] + [pl.BlockSpec(memory_space=pl.ANY)] * 2 + whole(7),
+         pltpu.VMEM((3 * width, width), f32), pltpu.SemaphoreType.DMA],
+        [pl.BlockSpec(memory_space=pltpu.SMEM)] + whole(1) + [pl.BlockSpec(memory_space=pl.ANY)]
+        + whole(7),
     )
     got = lax.ppermute(send, "co", swap)
     (input_grad,) = call(
@@ -272,13 +309,13 @@
     share = lax.all_to_all(share, PLANE, 0, 0, tiled=True)
     (share,) = call(
         turn_kernel,
-        [((depth, 16, LANES), bf16)],
+        [((depth, 8, LANES), bf16)],
         [share, turn],
         2 * depth * 16 * 72 * 2 * LANES,
         16,
     )
     share = lax.all_to_all(share, "z", 0, 0, tiled=True)
-    qkv_grad = jnp.sum(share[:, :held, : 3 * width // slabs].astype(f32), axis=0)
+    (qkv_grad,) = call(final_kernel, [((held, 3 * width // slabs), f32)], [share], 0, 8)
     return (input_grad[None], qkv_grad)
 
 

time: 107 us -> 107 us (level)
  Pallas kernels: 8.41 us -> 10.2 us
    all_to_all x0 -> x1, blocking collectives: none -> 27.7 us  [tap_column(): column = lax.all_to_all(piece, ('z',), 0, 0, tiled=True)]
    all_to_all x2 -> x1, blocking collectives: 48.2 us -> 20.5 us  [spread(): lax.all_to_all(jnp.broadcast_to(block[None], (count,) + block.shape), axe...]
    pallas_call x4 -> x6, Pallas kernels: 8.41 us -> 10.2 us  [call(): pl.pallas_call(kernel, out_shape=tuple((jax.ShapeDtypeStruct(s, d) for s,...]
where the time goes in v5:
time: 107 us
  blocking collectives  77.1 us (72%)
  Pallas kernels  10.2 us (10%)
  starting transfers between devices  9.04 us (8%)
  waiting for transfers between devices  8.15 us (8%)
  local copies, waits for them, and re-layouts  1.07 us (1%)
    all_to_all x1, blocking collectives, tap_column(): column = lax.all_to_all(piece, ('z',), 0, 0, tiled=True)  27.7 us
    all_to_all x1, blocking collectives, spread(): lax.all_to_all(jnp.broadcast_to(block[None], (count,) + block.shape), axe...  20.5 us
    all_to_all x1, blocking collectives, on_device(): share = lax.all_to_all(share, 'z', 0, 0, tiled=True)  15.4 us
    all_to_all x1, blocking collectives, on_device(): share = lax.all_to_all(share, PLANE, 0, 0, tiled=True)  13.5 us
    pallas_call x6, Pallas kernels, call(): pl.pallas_call(kernel, out_shape=tuple((jax.ShapeDtypeStruct(s, d) for s,...  10.2 us
    ppermute x1, waiting for transfers between devices, on_device(): lax.ppermute(cotangent, TM, [(i + 1, i) for i in range(slabs - 1)])  8.14 us
    ppermute x1, starting transfers between devices, on_device(): got = lax.ppermute(send, 'co', swap)  3.65 us
    ppermute x1, starting transfers between devices, on_device(): lax.ppermute(cotangent, TM, [(i + 1, i) for i in range(slabs - 1)])  3.47 us
  transfers between devices with their start and end apart: 3, of which 1 were waited for; matrix products, arithmetic and copies ran while one was open for 0% of the time, Pallas kernels for 3%

profile of v5, /device:TPU:2, one launch (start us, length us, event | category | flops | bytes accessed | tf_op | source)
XLA Modules:
  0.0 106.8 jit_solution(1833193510694915179)
XLA Ops:
  0.6 0.0 copy-start.2
  0.7 0.9 copy-done.2
  1.5 0.1 shard_map.77
  1.6 27.7 %all_to_all.20 = bf16[16,7,2,128]{3,2,1,0:T(2,128)(2,1)S(1)} all-to-all(bf16[16,7,2,128]{3,2,1,0:T(2,128)(2,1)S(1)} %shard_map.77), channel_id=1, replica_groups=mesh['xh'=2,'z'=16,'y'=4,'xl'=2,'co'=2] {'z'}, dimensions={0} | all-to-all | bytes 114688 | tf_op jit(solution)/shard_map/all_to_all | solution.py:224
  29.4 0.0 copy-start.4
  29.4 0.0 copy-start
  29.4 0.0 copy-start.1
  29.4 0.1 broadcast_in_dim.6
  29.5 20.5 %all_to_all.21.own_ref = bf16[16,7,32,128]{3,2,1,0:T(8,128)(2,1)S(1)} all-to-all(bf16[16,7,32,128]{3,2,1,0:T(8,128)(2,1)S(1)} %broadcast_in_dim.6), channel_id=1, replica_groups=mesh['xh'=2,'z'=16,'y'=4,'xl'=2,'co'=2] {'xh','y','xl'}, dimensions={0} | all-to-all | bytes 1835008 | tf_op jit(solution)/shard_map/all_to_all | solution.py:187
  50.1 1.9 %collective-permute-start.1 = (bf16[16,7,32,128]{3,2,1,0:T(8,128)(2,1)S(1)}, bf16[16,7,32,128]{3,2,1,0:T(8,128)(2,1)S(1)}, u32[]{:S(2)}, u32[]{:S(2)}) collective-permute-start(bf16[16,7,32,128]{3,2,1,0:T(8,128)(2,1)S(1)} %all_to_all.21.own_ref), channel_id=1, source_target_pairs={{0,1},{1,0},{2,3},{3,2},{4,5},{5,4},{6,7},{7,6},{8,9},{9,8},{10,11... | collective-permute-start | bytes 2752520 | tf_op jit(solution)/shard_map/ppermute | solution.py:273
  52.0 3.5 %collective-permute-start = (bf16[2,256,768]{2,1,0:T(8,128)(2,1)}, bf16[2,256,768]{2,1,0:T(8,128)(2,1)}, u32[]{:S(2)}, u32[]{:S(2)}) collective-permute-start(bf16[2,256,768]{2,1,0:T(8,128)(2,1)} %bitcast.5.cot_ref), channel_id=1, source_target_pairs={{1,0},{2,1},{3,2},{4,3},{5,4},{6,5},{7,6},{8,7},{9,8},{10,9},{11,1... | collective-permute-start | bytes 2359304 | tf_op jit(solution)/shard_map/ppermute | solution.py:266
  55.5 0.0 copy-done.4
  55.5 0.0 copy-start.3
  55.5 0.0 copy-done
  55.6 0.0 copy-done.1
  55.6 1.4 %shard_map.78 = (bf16[2,256,384]{2,1,0:T(8,128)(2,1)S(1)}, bf16[2,256,1152]{2,1,0:T(8,128)(2,1)S(1)}, f32[2,256,256]{2,1,0:T(8,128)S(1)}) custom-call(bf16[2,256,384]{2,1,0:T(8,128)(2,1)S(1)} %bitcast.7, f32[1,384]{1,0:T(1,128)S(1)} %broadcast_in_dim.7.gain_ref, bf16[384,1152]{1,0:T(8,128)(2,1)S(1)} %copy-done), custom_call_target="tpu_custom_call" | custom-call | flops 553648128 | bytes 3376640 | tf_op jit(solution)/shard_map/pallas_call | solution.py:174
  57.0 0.1 fusion.order_ref
  57.1 8.1 %collective-permute-done.next_any = bf16[2,256,768]{2,1,0:T(8,128)(2,1)} collective-permute-done((bf16[2,256,768]{2,1,0:T(8,128)(2,1)}, bf16[2,256,768]{2,1,0:T(8,128)(2,1)}, u32[]{:S(2)}, u32[]{:S(2)}) %collective-permute-start) | collective-permute-done | bytes 786464 | tf_op jit(solution)/shard_map/ppermute | solution.py:266
  65.3 0.0 collective-permute-done.1.other_ref
  65.3 0.0 copy-done.3
  65.3 5.9 %shard_map.79 = (bf16[2,256,384]{2,1,0:T(8,128)(2,1)S(1)}, bf16[2,256,1152]{2,1,0:T(8,128)(2,1)S(1)}, bf16[16,112,128]{2,1,0:T(8,128)(2,1)S(1)}, bf16[16,112,128]{2,1,0:T(8,128)(2,1)S(1)}) custom-call(s32[1]{0:T(128)} %bitcast.4.core_ref, bf16[2,256,768]{2,1,0:T(8,128)(2,1)} %bitcast.5.cot_ref, bf16[2,256,768]{2,1,0:T(8,128)(2,1)} %collective-permute-done.next_any, ...), custom_call_target="tpu_custom_call" | custom-call | flops 2063597568 | bytes 8585220 | tf_op jit(solution)/shard_map/pallas_call | solution.py:174
  71.2 3.7 %collective-permute-start.2 = (bf16[16,112,128]{2,1,0:T(8,128)(2,1)S(1)}, bf16[16,112,128]{2,1,0:T(8,128)(2,1)S(1)}, u32[]{:S(2)}, u32[]{:S(2)}) collective-permute-start(bf16[16,112,128]{2,1,0:T(8,128)(2,1)S(1)} %get-tuple-element.34), channel_id=1, source_target_pairs={{0,1},{1,0},{2,3},{3,2},{4,5},{5,4},{6,7},{7,6},{8,9},{9,8},{10,11... | collective-permute-start | bytes 1376264 | tf_op jit(solution)/shard_map/ppermute | solution.py:299
  74.8 0.1 broadcast_compare_fusion
  75.0 1.8 %shard_map.80 = bf16[2,256,384]{2,1,0:T(8,128)(2,1)} custom-call(bf16[2,256,384]{2,1,0:T(8,128)(2,1)S(1)} %bitcast.8, f32[1,384]{1,0:T(1,128)S(1)} %broadcast_in_dim.7.gain_ref, bf16[384,1152]{1,0:T(8,128)(2,1)S(1)} %copy-done, bf16[2,256,1152]{2,1,0:T(8,128)(2,1)S(1)} %get-tuple-element.35.qkv_cot_ref, bf16[2,256,384]{2,1,0:T(8,128)(2,1)S(1)} %get-tuple-element.36.upstream_ref), custom_call_target="tpu_custom_call" | custom-call | flops 452984832 | bytes 3245568 | tf_op jit(solution)/shard_map/pallas_call | solution.py:174
  76.8 0.0 collective-permute-done.2
  76.8 0.2 add_convert_fusion
  76.9 13.5 %all_to_all.22.got_ref = bf16[16,112,128]{2,1,0:T(8,128)(2,1)S(1)} all-to-all(bf16[16,112,128]{2,1,0:T(8,128)(2,1)S(1)} %add_convert_fusion), channel_id=1, replica_groups=mesh['xh'=2,'z'=16,'y'=4,'xl'=2,'co'=2] {'xh','y','xl'}, dimensions={0} | all-to-all | bytes 917504 | tf_op jit(solution)/shard_map/all_to_all | solution.py:309
  90.4 0.3 shard_map.81
  90.7 15.4 %all_to_all.23.got_ref = bf16[16,8,128]{2,1,0:T(8,128)(2,1)S(1)} all-to-all(bf16[16,8,128]{2,1,0:T(8,128)(2,1)S(1)} %shard_map.81), channel_id=1, replica_groups=mesh['xh'=2,'z'=16,'y'=4,'xl'=2,'co'=2] {'z'}, dimensions={0} | all-to-all | bytes 65536 | tf_op jit(solution)/shard_map/all_to_all | solution.py:317
  106.1 0.7 shard_map.82
  (8 shorter events, 0.1 us)
Async XLA Ops:
  0.6 0.9 copy-start.2
  29.4 26.1 %copy-start.4 = (f32[384]{0:T(512)S(1)}, f32[384]{0:T(512)}, u32[]{:S(2)}) copy-start(f32[384]{0:T(512)} %param.7) | copy-start | bytes 4612
  29.4 26.2 %copy-start = (bf16[384,1152]{1,0:T(8,128)(2,1)S(1)}, bf16[384,1152]{1,0:T(8,128)(2,1)}, u32[]{:S(2)}) copy-start(bf16[384,1152]{1,0:T(8,128)(2,1)} %weight_ref.3) | copy-start | bytes 2654212
  29.4 26.2 %copy-start.1 = (bf16[1,2,256,384]{3,2,1,0:T(8,128)(2,1)S(1)}, bf16[1,2,256,384]{3,2,1,0:T(8,128)(2,1)}, u32[]{:S(2)}) copy-start(bf16[1,2,256,384]{3,2,1,0:T(8,128)(2,1)} %param.6) | copy-start | bytes 1179652
  50.1 15.2 %collective-permute-start.1 = (bf16[16,7,32,128]{3,2,1,0:T(8,128)(2,1)S(1)}, bf16[16,7,32,128]{3,2,1,0:T(8,128)(2,1)S(1)}, u32[]{:S(2)}, u32[]{:S(2)}) collective-permute-start(bf16[16,7,32,128]{3,2,1,0:T(8,128)(2,1)S(1)} %all_to_all.21.own_ref), channel_id=1, source_target_pairs={{0,1},{1,0},{2,3},{3,2},{4,5},{5,4},{6,7},{7,6},{8,9},{9,8},{10,11... | collective-permute-start | bytes 2752520 | tf_op jit(solution)/shard_map/ppermute | solution.py:273
  52.0 13.3 %collective-permute-start = (bf16[2,256,768]{2,1,0:T(8,128)(2,1)}, bf16[2,256,768]{2,1,0:T(8,128)(2,1)}, u32[]{:S(2)}, u32[]{:S(2)}) collective-permute-start(bf16[2,256,768]{2,1,0:T(8,128)(2,1)} %bitcast.5.cot_ref), channel_id=1, source_target_pairs={{1,0},{2,1},{3,2},{4,3},{5,4},{6,5},{7,6},{8,7},{9,8},{10,9},{11,1... | collective-permute-start | bytes 2359304 | tf_op jit(solution)/shard_map/ppermute | solution.py:266
  55.5 9.7 %copy-start.3 = (bf16[384,384]{1,0:T(8,128)(2,1)S(1)}, bf16[384,384]{1,0:T(8,128)(2,1)}, u32[]{:S(2)}) copy-start(bf16[384,384]{1,0:T(8,128)(2,1)} %out_weight_ref.1) | copy-start | bytes 884740
  71.2 5.6 %collective-permute-start.2 = (bf16[16,112,128]{2,1,0:T(8,128)(2,1)S(1)}, bf16[16,112,128]{2,1,0:T(8,128)(2,1)S(1)}, u32[]{:S(2)}, u32[]{:S(2)}) collective-permute-start(bf16[16,112,128]{2,1,0:T(8,128)(2,1)S(1)} %get-tuple-element.34), channel_id=1, source_target_pairs={{0,1},{1,0},{2,3},{3,2},{4,5},{5,4},{6,7},{7,6},{8,9},{9,8},{10,11... | collective-permute-start | bytes 1376264 | tf_op jit(solution)/shard_map/ppermute | solution.py:299

commit v6 on v5

--- a/solution.py
+++ b/solution.py
@@ -26,8 +26,12 @@
 NN, NT, TN = ((1,), (0,)), ((1,), (1,)), ((0,), (0,))
 
 
-def forward_kernel(clip_ref, gain_ref, weight_ref, normed_ref, qkv_ref, prob_ref):
+def forward_kernel(
+    clip_ref, gain_ref, weight_ref, order_ref, out_weight_ref,
+    normed_ref, qkv_ref, prob_ref, out_order_ref,
+):
     frames, _, width = clip_ref.shape
+    out_order_ref[...] = dot(out_weight_ref[...], order_ref[...], NT).astype(bf16)
     for f in range(frames):
         features = clip_ref[f].astype(f32)
         squares = jnp.mean(features * features, axis=-1, keepdims=True)
@@ -42,78 +46,81 @@
 
 def backward_kernel(
     core_ref, cot_ref, next_any, own_ref, other_ref, order_ref, out_weight_ref, qkv_ref, prob_ref,
-    normed_ref, upstream_ref, qkv_cot_ref, keep_ref, send_ref, taps_ref, next_ref, grad_ref, sem,
+    normed_ref, upstream_ref, qkv_cot_ref, keep_ref, send_ref, grad_ref, next_ref, sem,
 ):
     frames, positions, width = upstream_ref.shape
     rows = frames * positions
     wide = cot_ref.shape[-1]
-    taps = taps_ref.shape[0]
     block = own_ref.shape[2]
     groups = own_ref.shape[0] // PIECES
     lanes = wide // LANES
     parts = width // (2 * groups * block)
+
     copy = pltpu.make_async_copy(next_any, next_ref, sem)
     copy.start()
-    for half, source in enumerate((own_ref, other_ref)):
-        for group in range(groups):
-            for tile in range(taps * lanes * parts):
-                tap, rest = divmod(tile, lanes * parts)
-                lane, part = divmod(rest, parts)
-                start = ((half * groups + group) * parts + part) * block
-                taps_ref[tap, start : start + block, lane * LANES : (lane + 1) * LANES] = source[
-                    group * PIECES + tile // TILES, tile % TILES
-                ]
-    total = dot(cot_ref[...].reshape(rows, wide), taps_ref[2], NT)
+
+    def taps_of(tap):
+        columns = []
+        for lane in range(lanes):
+            column = []
+            for source in (own_ref, other_ref):
+                for group in range(groups):
+                    for part in range(parts):
+                        tile = (tap * lanes + lane) * parts + part
+                        column.append(source[group * PIECES + tile // TILES, tile % TILES])
+            columns.append(jnp.concatenate(column, axis=0))
+        return columns
+
+    total = dot(cot_ref[...].reshape(rows, wide), jnp.concatenate(taps_of(2), axis=1), NT)
     copy.wait()
     middle = jnp.concatenate([cot_ref[1], next_ref[0]], axis=0)
-    total = total + dot(middle, taps_ref[1], NT)
-    total = total + dot(next_ref[...].reshape(rows, wide), taps_ref[0], NT)
-    upstream = dot(total.astype(bf16), order_ref[...], NN).astype(bf16)
-    upstream_ref[...] = upstream.reshape(upstream_ref.shape)
-    mixed_cot = dot(upstream, out_weight_ref[...], NT).astype(bf16)
-    for f in range(frames):
-        cot = mixed_cot[f * positions : (f + 1) * positions]
+    seen = jnp.concatenate([middle, next_ref[...].reshape(rows, wide)], axis=1)
+    total = total + dot(seen, jnp.concatenate(taps_of(1) + taps_of(0), axis=1), NT)
+    arrived = total.astype(bf16)
+    mixed_cot = dot(arrived, out_weight_ref[...], NT).astype(bf16)
+    cots = [mixed_cot[f * positions : (f + 1) * positions] for f in range(frames)]
+    weights_cots = [
+        dot(cots[f], qkv_ref[f, :, 2 * width :], NT).astype(bf16).astype(f32)
+        for f in range(frames)
+    ]
+    for f in range(frames):
+        qkv_cot_ref[f, :, 2 * width :] = dot(prob_ref[f].astype(bf16), cots[f], TN).astype(bf16)
+    scores_cots = []
+    for f in range(frames):
         prob = prob_ref[f]
-        queries = qkv_ref[f, :, :width]
-        keys = qkv_ref[f, :, width : 2 * width]
-        values = qkv_ref[f, :, 2 * width :]
-        weights_cot = dot(cot, values, NT).astype(bf16).astype(f32)
-        pull = jnp.sum(weights_cot * prob, axis=-1, keepdims=True)
-        scores_cot = (prob * (weights_cot - pull) / math.sqrt(width)).astype(bf16)
-        qkv_cot_ref[f, :, :width] = dot(scores_cot, keys, NN).astype(bf16)
-        qkv_cot_ref[f, :, width : 2 * width] = dot(scores_cot, queries, TN).astype(bf16)
-        qkv_cot_ref[f, :, 2 * width :] = dot(prob.astype(bf16), cot, TN).astype(bf16)
-    grad_ref[...] = dot(
-        qkv_cot_ref[...].reshape(rows, 3 * width), normed_ref[...].reshape(rows, width), TN
-    )
+        pull = jnp.sum(weights_cots[f] * prob, axis=-1, keepdims=True)
+        scores_cots.append((prob * (weights_cots[f] - pull) / math.sqrt(width)).astype(bf16))
+    normed = normed_ref[...].reshape(rows, width)
+
+    for f in range(frames):
+        qkv_cot_ref[f, :, :width] = dot(
+            scores_cots[f], qkv_ref[f, :, width : 2 * width], NN
+        ).astype(bf16)
+    for f in range(frames):
+        qkv_cot_ref[f, :, width : 2 * width] = dot(
+            scores_cots[f], qkv_ref[f, :, :width], TN
+        ).astype(bf16)
+    upstream_ref[...] = dot(arrived, order_ref[...], NN).astype(bf16).reshape(upstream_ref.shape)
+    grad_ref[...] = dot(qkv_cot_ref[...].reshape(rows, 3 * width), normed, TN)
     columns = grad_ref.shape[0] // (2 * PIECES)
     short = keep_ref.shape[1] - columns
     left = lax.broadcasted_iota(jnp.int32, (short, LANES), 1) < LANES // 2
-    first = core_ref[0] == 0
-    for group in range(groups):
-        for chip in range(PIECES):
-            pair = []
-            for core in range(2):
-                top = (2 * chip + core) * columns
-                low = top + columns - short
-                upper = grad_ref[top : top + short, LANES : 2 * LANES]
-                lower = grad_ref[low : low + short, LANES : 2 * LANES]
+    for out_ref, core in ((keep_ref, core_ref[0]), (send_ref, 1 - core_ref[0])):
+        for group in range(groups):
+            for chip in range(PIECES):
+                top = pl.multiple_of((2 * chip + core) * columns, 8)
+                low = pl.multiple_of(top + columns - short, 8)
+                upper = grad_ref[pl.ds(top, short), LANES : 2 * LANES]
+                lower = grad_ref[pl.ds(low, short), LANES : 2 * LANES]
                 if group == 0:
                     lower = pltpu.roll(lower, LANES // 2, 1)
                 else:
                     upper = pltpu.roll(upper, LANES // 2, 1)
                 side = 2 * group * LANES
-                pair.append(
-                    jnp.concatenate(
-                        [
-                            grad_ref[top : top + columns, side : side + LANES],
-                            jnp.where(left, upper, lower),
-                        ],
-                        axis=0,
-                    )
-                )
-            keep_ref[group * PIECES + chip] = jnp.where(first, pair[0], pair[1]).astype(bf16)
-            send_ref[group * PIECES + chip] = jnp.where(first, pair[1], pair[0]).astype(bf16)
+                wide_part = grad_ref[pl.ds(top, columns), side : side + LANES]
+                out_ref[group * PIECES + chip] = jnp.concatenate(
+                    [wide_part, jnp.where(left, upper, lower)], axis=0
+                ).astype(bf16)
 
 
 def turn_kernel(got_ref, turn_ref, out_ref):
@@ -271,15 +278,15 @@
     own = spread(column, PLANE)
     own, clip, core, group = lax.optimization_barrier((own, clip, core, group))
     other = lax.ppermute(own, "co", swap)
-    normed, qkv, prob = call(
+    order = channel_order(width, core)
+    normed, qkv, prob, out_order = call(
         forward_kernel,
         [((frames, positions, width), bf16), ((frames, positions, 3 * width), bf16),
-         ((frames, positions, positions), f32)],
-        [clip, gain, qkv_weight],
+         ((frames, positions, positions), f32), ((width, width), bf16)],
+        [clip, gain, qkv_weight, order, out_weight],
         2 * rows * width * (3 * width + positions),
         16,
     )
-    order = channel_order(width, core)
     turn = turn_orders(held, depth, group)
     core = core.reshape(1)
 
@@ -288,11 +295,11 @@
     upstream, qkv_cot, keep, send = call(
         backward_kernel,
         [((frames, positions, width), bf16), ((frames, positions, 3 * width), bf16), packed, packed],
-        [core, cotangent, incoming, own, other, order, out_weight, qkv, prob, normed],
+        [core, cotangent, incoming, own, other, order, out_order, qkv, prob, normed],
         2 * rows * width * (3 * wide + 2 * width + 4 * positions + 3 * width),
         32,
-        [pltpu.VMEM((3, width, wide), bf16), pltpu.VMEM(cotangent.shape, bf16),
-         pltpu.VMEM((3 * width, width), f32), pltpu.SemaphoreType.DMA],
+        [pltpu.VMEM((3 * width, width), f32), pltpu.VMEM(cotangent.shape, bf16),
+         pltpu.SemaphoreType.DMA],
         [pl.BlockSpec(memory_space=pltpu.SMEM)] + whole(1) + [pl.BlockSpec(memory_space=pl.ANY)]
         + whole(7),
     )

time: 107 us -> 107 us (level)
  no operation moved by 1% of the time
where the time goes in v6:
time: 107 us
  blocking collectives  77.1 us (72%)
  Pallas kernels  9.94 us (9%)
  starting transfers between devices  9.03 us (8%)
  waiting for transfers between devices  8.04 us (8%)
  local copies, waits for them, and re-layouts  1.07 us (1%)
    all_to_all x1, blocking collectives, tap_column(): column = lax.all_to_all(piece, ('z',), 0, 0, tiled=True)  27.7 us
    all_to_all x1, blocking collectives, spread(): lax.all_to_all(jnp.broadcast_to(block[None], (count,) + block.shape), axe...  20.5 us
    all_to_all x1, blocking collectives, on_device(): share = lax.all_to_all(share, 'z', 0, 0, tiled=True)  15.4 us
    all_to_all x1, blocking collectives, on_device(): share = lax.all_to_all(share, PLANE, 0, 0, tiled=True)  13.5 us
    pallas_call x6, Pallas kernels, call(): pl.pallas_call(kernel, out_shape=tuple((jax.ShapeDtypeStruct(s, d) for s,...  9.94 us
    ppermute x1, waiting for transfers between devices, on_device(): lax.ppermute(cotangent, TM, [(i + 1, i) for i in range(slabs - 1)])  8.03 us
    ppermute x1, starting transfers between devices, on_device(): got = lax.ppermute(send, 'co', swap)  3.65 us
    ppermute x1, starting transfers between devices, on_device(): lax.ppermute(cotangent, TM, [(i + 1, i) for i in range(slabs - 1)])  3.47 us
  transfers between devices with their start and end apart: 3, of which 1 were waited for; matrix products, arithmetic and copies ran while one was open for 0% of the time, Pallas kernels for 3%

profile of v6, /device:TPU:2, one launch (start us, length us, event | category | flops | bytes accessed | tf_op | source)
XLA Modules:
  0.0 106.5 jit_solution(13712513794123214239)
XLA Ops:
  0.6 0.0 copy-start.2
  0.7 0.9 copy-done.2
  1.5 0.1 shard_map.77
  1.6 27.7 %all_to_all.20 = bf16[16,7,2,128]{3,2,1,0:T(2,128)(2,1)S(1)} all-to-all(bf16[16,7,2,128]{3,2,1,0:T(2,128)(2,1)S(1)} %shard_map.77), channel_id=1, replica_groups=mesh['xh'=2,'z'=16,'y'=4,'xl'=2,'co'=2] {'z'}, dimensions={0} | all-to-all | bytes 114688 | tf_op jit(solution)/shard_map/all_to_all | solution.py:231
  29.4 0.0 copy-start.4
  29.4 0.1 broadcast_in_dim.6
  29.5 0.0 copy-start
  29.5 0.0 copy-start.1
  29.5 0.0 copy-start.3
  29.5 20.5 %all_to_all.21.own_ref = bf16[16,7,32,128]{3,2,1,0:T(8,128)(2,1)S(1)} all-to-all(bf16[16,7,32,128]{3,2,1,0:T(8,128)(2,1)S(1)} %broadcast_in_dim.6), channel_id=1, replica_groups=mesh['xh'=2,'z'=16,'y'=4,'xl'=2,'co'=2] {'xh','y','xl'}, dimensions={0} | all-to-all | bytes 1835008 | tf_op jit(solution)/shard_map/all_to_all | solution.py:194
  50.1 1.9 %collective-permute-start.1 = (bf16[16,7,32,128]{3,2,1,0:T(8,128)(2,1)S(1)}, bf16[16,7,32,128]{3,2,1,0:T(8,128)(2,1)S(1)}, u32[]{:S(2)}, u32[]{:S(2)}) collective-permute-start(bf16[16,7,32,128]{3,2,1,0:T(8,128)(2,1)S(1)} %all_to_all.21.own_ref), channel_id=1, source_target_pairs={{0,1},{1,0},{2,3},{3,2},{4,5},{5,4},{6,7},{7,6},{8,9},{9,8},{10,11... | collective-permute-start | bytes 2752520 | tf_op jit(solution)/shard_map/ppermute | solution.py:280
  52.0 3.5 %collective-permute-start = (bf16[2,256,768]{2,1,0:T(8,128)(2,1)}, bf16[2,256,768]{2,1,0:T(8,128)(2,1)}, u32[]{:S(2)}, u32[]{:S(2)}) collective-permute-start(bf16[2,256,768]{2,1,0:T(8,128)(2,1)} %bitcast.5.cot_ref), channel_id=1, source_target_pairs={{1,0},{2,1},{3,2},{4,3},{5,4},{6,5},{7,6},{8,7},{9,8},{10,9},{11,1... | collective-permute-start | bytes 2359304 | tf_op jit(solution)/shard_map/ppermute | solution.py:273
  55.5 0.0 copy-done.4
  55.6 0.1 fusion.order_ref
  55.7 0.0 copy-done
  55.7 0.0 copy-done.1
  55.7 0.0 copy-done.3
  55.7 1.5 %shard_map.78 = (bf16[2,256,384]{2,1,0:T(8,128)(2,1)S(1)}, bf16[2,256,1152]{2,1,0:T(8,128)(2,1)S(1)}, f32[2,256,256]{2,1,0:T(8,128)S(1)}, bf16[384,384]{1,0:T(8,128)(2,1)S(1)}) custom-call(bf16[2,256,384]{2,1,0:T(8,128)(2,1)S(1)} %bitcast.7, f32[1,384]{1,0:T(1,128)S(1)} %broadcast_in_dim.7.gain_ref, bf16[384,1152]{1,0:T(8,128)(2,1)S(1)} %copy-done, ...), custom_call_target="tpu_custom_call" | custom-call | flops 553648128 | bytes 4261376 | tf_op jit(solution)/shard_map/pallas_call | solution.py:181
  57.2 8.0 %collective-permute-done.next_any = bf16[2,256,768]{2,1,0:T(8,128)(2,1)} collective-permute-done((bf16[2,256,768]{2,1,0:T(8,128)(2,1)}, bf16[2,256,768]{2,1,0:T(8,128)(2,1)}, u32[]{:S(2)}, u32[]{:S(2)}) %collective-permute-start) | collective-permute-done | bytes 786464 | tf_op jit(solution)/shard_map/ppermute | solution.py:273
  65.3 0.0 collective-permute-done.1.other_ref
  65.3 5.6 %shard_map.79 = (bf16[2,256,384]{2,1,0:T(8,128)(2,1)S(1)}, bf16[2,256,1152]{2,1,0:T(8,128)(2,1)S(1)}, bf16[16,112,128]{2,1,0:T(8,128)(2,1)S(1)}, bf16[16,112,128]{2,1,0:T(8,128)(2,1)S(1)}) custom-call(s32[1]{0:T(128)} %bitcast.4.core_ref, bf16[2,256,768]{2,1,0:T(8,128)(2,1)} %bitcast.5.cot_ref, bf16[2,256,768]{2,1,0:T(8,128)(2,1)} %collective-permute-done.next_any, ...), custom_call_target="tpu_custom_call" | custom-call | flops 2063597568 | bytes 8585220 | tf_op jit(solution)/shard_map/pallas_call | solution.py:181
  70.9 3.6 %collective-permute-start.2 = (bf16[16,112,128]{2,1,0:T(8,128)(2,1)S(1)}, bf16[16,112,128]{2,1,0:T(8,128)(2,1)S(1)}, u32[]{:S(2)}, u32[]{:S(2)}) collective-permute-start(bf16[16,112,128]{2,1,0:T(8,128)(2,1)S(1)} %get-tuple-element.36), channel_id=1, source_target_pairs={{0,1},{1,0},{2,3},{3,2},{4,5},{5,4},{6,7},{7,6},{8,9},{9,8},{10,11... | collective-permute-start | bytes 1376264 | tf_op jit(solution)/shard_map/ppermute | solution.py:306
  74.5 0.1 broadcast_compare_fusion
  74.7 1.8 %shard_map.80 = bf16[2,256,384]{2,1,0:T(8,128)(2,1)} custom-call(bf16[2,256,384]{2,1,0:T(8,128)(2,1)S(1)} %bitcast.8, f32[1,384]{1,0:T(1,128)S(1)} %broadcast_in_dim.7.gain_ref, bf16[384,1152]{1,0:T(8,128)(2,1)S(1)} %copy-done, bf16[2,256,1152]{2,1,0:T(8,128)(2,1)S(1)} %get-tuple-element.37.qkv_cot_ref, bf16[2,256,384]{2,1,0:T(8,128)(2,1)S(1)} %get-tuple-element.38.upstream_ref), custom_call_target="tpu_custom_call" | custom-call | flops 452984832 | bytes 3245568 | tf_op jit(solution)/shard_map/pallas_call | solution.py:181
  76.5 0.0 collective-permute-done.2
  76.5 0.2 add_convert_fusion
  76.6 13.5 %all_to_all.22.got_ref = bf16[16,112,128]{2,1,0:T(8,128)(2,1)S(1)} all-to-all(bf16[16,112,128]{2,1,0:T(8,128)(2,1)S(1)} %add_convert_fusion), channel_id=1, replica_groups=mesh['xh'=2,'z'=16,'y'=4,'xl'=2,'co'=2] {'xh','y','xl'}, dimensions={0} | all-to-all | bytes 917504 | tf_op jit(solution)/shard_map/all_to_all | solution.py:316
  90.1 0.3 shard_map.81
  90.4 15.4 %all_to_all.23.got_ref = bf16[16,8,128]{2,1,0:T(8,128)(2,1)S(1)} all-to-all(bf16[16,8,128]{2,1,0:T(8,128)(2,1)S(1)} %shard_map.81), channel_id=1, replica_groups=mesh['xh'=2,'z'=16,'y'=4,'xl'=2,'co'=2] {'z'}, dimensions={0} | all-to-all | bytes 65536 | tf_op jit(solution)/shard_map/all_to_all | solution.py:324
  105.8 0.7 shard_map.82
  (8 shorter events, 0.1 us)
Async XLA Ops:
  0.6 0.9 copy-start.2
  29.4 26.1 %copy-start.4 = (f32[384]{0:T(512)S(1)}, f32[384]{0:T(512)}, u32[]{:S(2)}) copy-start(f32[384]{0:T(512)} %param.7) | copy-start | bytes 4612
  29.5 26.2 %copy-start = (bf16[384,1152]{1,0:T(8,128)(2,1)S(1)}, bf16[384,1152]{1,0:T(8,128)(2,1)}, u32[]{:S(2)}) copy-start(bf16[384,1152]{1,0:T(8,128)(2,1)} %weight_ref.3) | copy-start | bytes 2654212
  29.5 26.2 %copy-start.1 = (bf16[1,2,256,384]{3,2,1,0:T(8,128)(2,1)S(1)}, bf16[1,2,256,384]{3,2,1,0:T(8,128)(2,1)}, u32[]{:S(2)}) copy-start(bf16[1,2,256,384]{3,2,1,0:T(8,128)(2,1)} %param.6) | copy-start | bytes 1179652
  29.5 26.2 %copy-start.3 = (bf16[384,384]{1,0:T(8,128)(2,1)S(1)}, bf16[384,384]{1,0:T(8,128)(2,1)}, u32[]{:S(2)}) copy-start(bf16[384,384]{1,0:T(8,128)(2,1)} %out_weight_ref.1) | copy-start | bytes 884740
  50.1 15.2 %collective-permute-start.1 = (bf16[16,7,32,128]{3,2,1,0:T(8,128)(2,1)S(1)}, bf16[16,7,32,128]{3,2,1,0:T(8,128)(2,1)S(1)}, u32[]{:S(2)}, u32[]{:S(2)}) collective-permute-start(bf16[16,7,32,128]{3,2,1,0:T(8,128)(2,1)S(1)} %all_to_all.21.own_ref), channel_id=1, source_target_pairs={{0,1},{1,0},{2,3},{3,2},{4,5},{5,4},{6,7},{7,6},{8,9},{9,8},{10,11... | collective-permute-start | bytes 2752520 | tf_op jit(solution)/shard_map/ppermute | solution.py:280
  52.0 13.3 %collective-permute-start = (bf16[2,256,768]{2,1,0:T(8,128)(2,1)}, bf16[2,256,768]{2,1,0:T(8,128)(2,1)}, u32[]{:S(2)}, u32[]{:S(2)}) collective-permute-start(bf16[2,256,768]{2,1,0:T(8,128)(2,1)} %bitcast.5.cot_ref), channel_id=1, source_target_pairs={{1,0},{2,1},{3,2},{4,3},{5,4},{6,5},{7,6},{8,7},{9,8},{10,9},{11,1... | collective-permute-start | bytes 2359304 | tf_op jit(solution)/shard_map/ppermute | solution.py:273
  70.9 5.6 %collective-permute-start.2 = (bf16[16,112,128]{2,1,0:T(8,128)(2,1)S(1)}, bf16[16,112,128]{2,1,0:T(8,128)(2,1)S(1)}, u32[]{:S(2)}, u32[]{:S(2)}) collective-permute-start(bf16[16,112,128]{2,1,0:T(8,128)(2,1)S(1)} %get-tuple-element.36), channel_id=1, source_target_pairs={{0,1},{1,0},{2,3},{3,2},{4,5},{5,4},{6,7},{7,6},{8,9},{9,8},{10,11... | collective-permute-start | bytes 1376264 | tf_op jit(solution)/shard_map/ppermute | solution.py:306

commit v7 on v6

--- a/solution.py
+++ b/solution.py
@@ -27,10 +27,12 @@
 
 
 def forward_kernel(
-    clip_ref, gain_ref, weight_ref, order_ref, out_weight_ref,
-    normed_ref, qkv_ref, prob_ref, out_order_ref,
+    clip_ref, gain_ref, weight_ref, order_ref, out_weight_ref, next_any,
+    normed_ref, qkv_ref, prob_ref, out_order_ref, next_ref, sem,
 ):
     frames, _, width = clip_ref.shape
+    copy = pltpu.make_async_copy(next_any, next_ref, sem)
+    copy.start()
     out_order_ref[...] = dot(out_weight_ref[...], order_ref[...], NT).astype(bf16)
     for f in range(frames):
         features = clip_ref[f].astype(f32)
@@ -42,11 +44,12 @@
         scores = dot(qkv[:, :width], qkv[:, width : 2 * width], NT) / math.sqrt(width)
         raised = jnp.exp(scores - jnp.max(scores, axis=-1, keepdims=True))
         prob_ref[f] = raised / jnp.sum(raised, axis=-1, keepdims=True)
+    copy.wait()
 
 
 def backward_kernel(
-    core_ref, cot_ref, next_any, own_ref, other_ref, order_ref, out_weight_ref, qkv_ref, prob_ref,
-    normed_ref, upstream_ref, qkv_cot_ref, keep_ref, send_ref, grad_ref, next_ref, sem,
+    core_ref, cot_ref, next_ref, own_ref, other_ref, order_ref, out_weight_ref, qkv_ref, prob_ref,
+    normed_ref, upstream_ref, qkv_cot_ref, keep_ref, send_ref, grad_ref,
 ):
     frames, positions, width = upstream_ref.shape
     rows = frames * positions
@@ -55,9 +58,6 @@
     groups = own_ref.shape[0] // PIECES
     lanes = wide // LANES
     parts = width // (2 * groups * block)
-
-    copy = pltpu.make_async_copy(next_any, next_ref, sem)
-    copy.start()
 
     def taps_of(tap):
         columns = []
@@ -71,11 +71,10 @@
             columns.append(jnp.concatenate(column, axis=0))
         return columns
 
-    total = dot(cot_ref[...].reshape(rows, wide), jnp.concatenate(taps_of(2), axis=1), NT)
-    copy.wait()
     middle = jnp.concatenate([cot_ref[1], next_ref[0]], axis=0)
-    seen = jnp.concatenate([middle, next_ref[...].reshape(rows, wide)], axis=1)
-    total = total + dot(seen, jnp.concatenate(taps_of(1) + taps_of(0), axis=1), NT)
+    seen = [cot_ref[...].reshape(rows, wide), middle, next_ref[...].reshape(rows, wide)]
+    taps = jnp.concatenate(taps_of(2) + taps_of(1) + taps_of(0), axis=1)
+    total = dot(jnp.concatenate(seen, axis=1), taps, NT)
     arrived = total.astype(bf16)
     mixed_cot = dot(arrived, out_weight_ref[...], NT).astype(bf16)
     cots = [mixed_cot[f * positions : (f + 1) * positions] for f in range(frames)]
@@ -279,13 +278,16 @@
     own, clip, core, group = lax.optimization_barrier((own, clip, core, group))
     other = lax.ppermute(own, "co", swap)
     order = channel_order(width, core)
-    normed, qkv, prob, out_order = call(
+    normed, qkv, prob, out_order, following = call(
         forward_kernel,
         [((frames, positions, width), bf16), ((frames, positions, 3 * width), bf16),
-         ((frames, positions, positions), f32), ((width, width), bf16)],
-        [clip, gain, qkv_weight, order, out_weight],
+         ((frames, positions, positions), f32), ((width, width), bf16), (incoming.shape, bf16)],
+        [clip, gain, qkv_weight, order, out_weight,
+         pltpu.with_memory_space_constraint(incoming, pltpu.HBM)],
         2 * rows * width * (3 * width + positions),
         16,
+        [pltpu.SemaphoreType.DMA],
+        whole(5) + [pl.BlockSpec(memory_space=pl.ANY)],
     )
     turn = turn_orders(held, depth, group)
     core = core.reshape(1)
@@ -295,13 +297,11 @@
     upstream, qkv_cot, keep, send = call(
         backward_kernel,
         [((frames, positions, width), bf16), ((frames, positions, 3 * width), bf16), packed, packed],
-        [core, cotangent, incoming, own, other, order, out_order, qkv, prob, normed],
+        [core, cotangent, following, own, other, order, out_order, qkv, prob, normed],
         2 * rows * width * (3 * wide + 2 * width + 4 * positions + 3 * width),
         32,
-        [pltpu.VMEM((3 * width, width), f32), pltpu.VMEM(cotangent.shape, bf16),
-         pltpu.SemaphoreType.DMA],
-        [pl.BlockSpec(memory_space=pltpu.SMEM)] + whole(1) + [pl.BlockSpec(memory_space=pl.ANY)]
-        + whole(7),
+        [pltpu.VMEM((3 * width, width), f32)],
+        [pl.BlockSpec(memory_space=pltpu.SMEM)] + whole(9),
     )
     got = lax.ppermute(send, "co", swap)
     (input_grad,) = call(

time: 107 us -> 108 us (level)
  waiting for transfers between devices: 8.04 us -> 9.57 us
    ppermute x1, waiting for transfers between devices: 8.03 us -> 9.57 us  [on_device(): lax.ppermute(cotangent, TM, [(i + 1, i) for i in range(slabs - 1)])]
where the time goes in v7:
time: 108 us; the launch traced here: 107 us
  blocking collectives  77.1 us (71%)
  waiting for transfers between devices  9.57 us (9%)
  Pallas kernels  9.13 us (8%)
  starting transfers between devices  9.03 us (8%)
    all_to_all x1, blocking collectives, tap_column(): column = lax.all_to_all(piece, ('z',), 0, 0, tiled=True)  27.7 us
    all_to_all x1, blocking collectives, spread(): lax.all_to_all(jnp.broadcast_to(block[None], (count,) + block.shape), axe...  20.5 us
    all_to_all x1, blocking collectives, on_device(): share = lax.all_to_all(share, 'z', 0, 0, tiled=True)  15.4 us
    all_to_all x1, blocking collectives, on_device(): share = lax.all_to_all(share, PLANE, 0, 0, tiled=True)  13.5 us
    ppermute x1, waiting for transfers between devices, on_device(): lax.ppermute(cotangent, TM, [(i + 1, i) for i in range(slabs - 1)])  9.57 us
    pallas_call x6, Pallas kernels, call(): pl.pallas_call(kernel, out_shape=tuple((jax.ShapeDtypeStruct(s, d) for s,...  9.13 us
    ppermute x1, starting transfers between devices, on_device(): got = lax.ppermute(send, 'co', swap)  3.65 us
    ppermute x1, starting transfers between devices, on_device(): lax.ppermute(cotangent, TM, [(i + 1, i) for i in range(slabs - 1)])  3.47 us
  transfers between devices with their start and end apart: 3, of which 1 were waited for; matrix products, arithmetic and copies ran while one was open for 0% of the time, Pallas kernels for 3%

profile of v7, /device:TPU:2, one launch (start us, length us, event | category | flops | bytes accessed | tf_op | source)
XLA Modules:
  0.0 107.2 jit_solution(16252719578344471053)
XLA Ops:
  0.6 0.0 copy-start.3
  0.7 0.9 copy-done.3
  1.5 0.1 shard_map.77
  1.6 27.7 %all_to_all.20 = bf16[16,7,2,128]{3,2,1,0:T(2,128)(2,1)S(1)} all-to-all(bf16[16,7,2,128]{3,2,1,0:T(2,128)(2,1)S(1)} %shard_map.77), channel_id=1, replica_groups=mesh['xh'=2,'z'=16,'y'=4,'xl'=2,'co'=2] {'z'}, dimensions={0} | all-to-all | bytes 114688 | tf_op jit(solution)/shard_map/all_to_all | solution.py:230
  29.4 0.0 copy-start.4
  29.4 0.1 broadcast_in_dim.6
  29.5 0.0 copy-start
  29.5 0.0 copy-start.1
  29.5 0.0 copy-start.2
  29.5 20.5 %all_to_all.21.own_ref = bf16[16,7,32,128]{3,2,1,0:T(8,128)(2,1)S(1)} all-to-all(bf16[16,7,32,128]{3,2,1,0:T(8,128)(2,1)S(1)} %broadcast_in_dim.6), channel_id=1, replica_groups=mesh['xh'=2,'z'=16,'y'=4,'xl'=2,'co'=2] {'xh','y','xl'}, dimensions={0} | all-to-all | bytes 1835008 | tf_op jit(solution)/shard_map/all_to_all | solution.py:193
  50.1 1.9 %collective-permute-start.1 = (bf16[16,7,32,128]{3,2,1,0:T(8,128)(2,1)S(1)}, bf16[16,7,32,128]{3,2,1,0:T(8,128)(2,1)S(1)}, u32[]{:S(2)}, u32[]{:S(2)}) collective-permute-start(bf16[16,7,32,128]{3,2,1,0:T(8,128)(2,1)S(1)} %all_to_all.21.own_ref), channel_id=1, source_target_pairs={{0,1},{1,0},{2,3},{3,2},{4,5},{5,4},{6,7},{7,6},{8,9},{9,8},{10,11... | collective-permute-start | bytes 2752520 | tf_op jit(solution)/shard_map/ppermute | solution.py:279
  52.0 3.5 %collective-permute-start = (bf16[2,256,768]{2,1,0:T(8,128)(2,1)}, bf16[2,256,768]{2,1,0:T(8,128)(2,1)}, u32[]{:S(2)}, u32[]{:S(2)}) collective-permute-start(bf16[2,256,768]{2,1,0:T(8,128)(2,1)} %bitcast.5.cot_ref), channel_id=1, source_target_pairs={{1,0},{2,1},{3,2},{4,3},{5,4},{6,5},{7,6},{8,7},{9,8},{10,9},{11,1... | collective-permute-start | bytes 2359304 | tf_op jit(solution)/shard_map/ppermute | solution.py:272
  55.5 0.0 copy-done.4
  55.6 0.1 fusion.order_ref
  55.7 9.6 %collective-permute-done.next_any = bf16[2,256,768]{2,1,0:T(8,128)(2,1)} collective-permute-done((bf16[2,256,768]{2,1,0:T(8,128)(2,1)}, bf16[2,256,768]{2,1,0:T(8,128)(2,1)}, u32[]{:S(2)}, u32[]{:S(2)}) %collective-permute-start) | collective-permute-done | bytes 786464 | tf_op jit(solution)/shard_map/ppermute | solution.py:272
  65.3 0.0 copy-done
  65.3 0.0 copy-done.1
  65.3 0.0 copy-done.2
  65.3 1.8 %shard_map.78 = (bf16[2,256,384]{2,1,0:T(8,128)(2,1)S(1)}, bf16[2,256,1152]{2,1,0:T(8,128)(2,1)S(1)}, f32[2,256,256]{2,1,0:T(8,128)S(1)}, bf16[384,384]{1,0:T(8,128)(2,1)S(1)}, bf16[2,256,768]{2,1,0:T(8,128)(2,1)S(1)}) custom-call(bf16[2,256,384]{2,1,0:T(8,128)(2,1)S(1)} %bitcast.7, f32[1,384]{1,0:T(1,128)S(1)} %broadcast_in_dim.7.gain_ref, ...), custom_call_target="tpu_custom_call" | custom-call | flops 553648128 | bytes 5834240 | tf_op jit(solution)/shard_map/pallas_call | solution.py:180
  67.1 0.0 collective-permute-done.1.other_ref
  67.1 4.4 %shard_map.79 = (bf16[2,256,384]{2,1,0:T(8,128)(2,1)S(1)}, bf16[2,256,1152]{2,1,0:T(8,128)(2,1)S(1)}, bf16[16,112,128]{2,1,0:T(8,128)(2,1)S(1)}, bf16[16,112,128]{2,1,0:T(8,128)(2,1)S(1)}) custom-call(s32[1]{0:T(128)} %bitcast.4.core_ref, bf16[2,256,768]{2,1,0:T(8,128)(2,1)} %bitcast.5.cot_ref, bf16[2,256,768]{2,1,0:T(8,128)(2,1)S(1)} %get-tuple-element.32.next_ref, ...), custom_call_target="tpu_custom_call" | custom-call | flops 2063597568 | bytes 8585220 | tf_op jit(solution)/shard_map/pallas_call | solution.py:180
  71.6 3.6 %collective-permute-start.2 = (bf16[16,112,128]{2,1,0:T(8,128)(2,1)S(1)}, bf16[16,112,128]{2,1,0:T(8,128)(2,1)S(1)}, u32[]{:S(2)}, u32[]{:S(2)}) collective-permute-start(bf16[16,112,128]{2,1,0:T(8,128)(2,1)S(1)} %get-tuple-element.38), channel_id=1, source_target_pairs={{0,1},{1,0},{2,3},{3,2},{4,5},{5,4},{6,7},{7,6},{8,9},{9,8},{10,11... | collective-permute-start | bytes 1376264 | tf_op jit(solution)/shard_map/ppermute | solution.py:306
  75.2 0.1 broadcast_compare_fusion
  75.4 1.8 %shard_map.80 = bf16[2,256,384]{2,1,0:T(8,128)(2,1)} custom-call(bf16[2,256,384]{2,1,0:T(8,128)(2,1)S(1)} %bitcast.8, f32[1,384]{1,0:T(1,128)S(1)} %broadcast_in_dim.7.gain_ref, bf16[384,1152]{1,0:T(8,128)(2,1)S(1)} %copy-done, bf16[2,256,1152]{2,1,0:T(8,128)(2,1)S(1)} %get-tuple-element.39.qkv_cot_ref, bf16[2,256,384]{2,1,0:T(8,128)(2,1)S(1)} %get-tuple-element.40.upstream_ref), custom_call_target="tpu_custom_call" | custom-call | flops 452984832 | bytes 3245568 | tf_op jit(solution)/shard_map/pallas_call | solution.py:180
  77.2 0.0 collective-permute-done.2
  77.2 0.2 add_convert_fusion
  77.3 13.5 %all_to_all.22.got_ref = bf16[16,112,128]{2,1,0:T(8,128)(2,1)S(1)} all-to-all(bf16[16,112,128]{2,1,0:T(8,128)(2,1)S(1)} %add_convert_fusion), channel_id=1, replica_groups=mesh['xh'=2,'z'=16,'y'=4,'xl'=2,'co'=2] {'xh','y','xl'}, dimensions={0} | all-to-all | bytes 917504 | tf_op jit(solution)/shard_map/all_to_all | solution.py:316
  90.8 0.3 shard_map.81
  91.1 15.4 %all_to_all.23.got_ref = bf16[16,8,128]{2,1,0:T(8,128)(2,1)S(1)} all-to-all(bf16[16,8,128]{2,1,0:T(8,128)(2,1)S(1)} %shard_map.81), channel_id=1, replica_groups=mesh['xh'=2,'z'=16,'y'=4,'xl'=2,'co'=2] {'z'}, dimensions={0} | all-to-all | bytes 65536 | tf_op jit(solution)/shard_map/all_to_all | solution.py:324
  106.5 0.7 shard_map.82
  (8 shorter events, 0.1 us)
Async XLA Ops:
  0.6 0.9 copy-start.3
  29.4 26.1 %copy-start.4 = (f32[384]{0:T(512)S(1)}, f32[384]{0:T(512)}, u32[]{:S(2)}) copy-start(f32[384]{0:T(512)} %param.7) | copy-start | bytes 4612
  29.5 35.8 %copy-start = (bf16[384,1152]{1,0:T(8,128)(2,1)S(1)}, bf16[384,1152]{1,0:T(8,128)(2,1)}, u32[]{:S(2)}) copy-start(bf16[384,1152]{1,0:T(8,128)(2,1)} %weight_ref.3) | copy-start | bytes 2654212
  29.5 35.8 %copy-start.1 = (bf16[1,2,256,384]{3,2,1,0:T(8,128)(2,1)S(1)}, bf16[1,2,256,384]{3,2,1,0:T(8,128)(2,1)}, u32[]{:S(2)}) copy-start(bf16[1,2,256,384]{3,2,1,0:T(8,128)(2,1)} %param.6) | copy-start | bytes 1179652
  29.5 35.8 %copy-start.2 = (bf16[384,384]{1,0:T(8,128)(2,1)S(1)}, bf16[384,384]{1,0:T(8,128)(2,1)}, u32[]{:S(2)}) copy-start(bf16[384,384]{1,0:T(8,128)(2,1)} %out_weight_ref.1) | copy-start | bytes 884740
  50.1 17.0 %collective-permute-start.1 = (bf16[16,7,32,128]{3,2,1,0:T(8,128)(2,1)S(1)}, bf16[16,7,32,128]{3,2,1,0:T(8,128)(2,1)S(1)}, u32[]{:S(2)}, u32[]{:S(2)}) collective-permute-start(bf16[16,7,32,128]{3,2,1,0:T(8,128)(2,1)S(1)} %all_to_all.21.own_ref), channel_id=1, source_target_pairs={{0,1},{1,0},{2,3},{3,2},{4,5},{5,4},{6,7},{7,6},{8,9},{9,8},{10,11... | collective-permute-start | bytes 2752520 | tf_op jit(solution)/shard_map/ppermute | solution.py:279
  52.0 13.3 %collective-permute-start = (bf16[2,256,768]{2,1,0:T(8,128)(2,1)}, bf16[2,256,768]{2,1,0:T(8,128)(2,1)}, u32[]{:S(2)}, u32[]{:S(2)}) collective-permute-start(bf16[2,256,768]{2,1,0:T(8,128)(2,1)} %bitcast.5.cot_ref), channel_id=1, source_target_pairs={{1,0},{2,1},{3,2},{4,3},{5,4},{6,5},{7,6},{8,7},{9,8},{10,9},{11,1... | collective-permute-start | bytes 2359304 | tf_op jit(solution)/shard_map/ppermute | solution.py:272
  71.6 5.6 %collective-permute-start.2 = (bf16[16,112,128]{2,1,0:T(8,128)(2,1)S(1)}, bf16[16,112,128]{2,1,0:T(8,128)(2,1)S(1)}, u32[]{:S(2)}, u32[]{:S(2)}) collective-permute-start(bf16[16,112,128]{2,1,0:T(8,128)(2,1)S(1)} %get-tuple-element.38), channel_id=1, source_target_pairs={{0,1},{1,0},{2,3},{3,2},{4,5},{5,4},{6,7},{7,6},{8,9},{9,8},{10,11... | collective-permute-start | bytes 1376264 | tf_op jit(solution)/shard_map/ppermute | solution.py:306

commit v8 on v7

--- a/solution.py
+++ b/solution.py
@@ -158,8 +158,11 @@
         out_ref[8 + i : 9 + i] = line[:, :columns]
 
 
-def input_kernel(clip_ref, gain_ref, weight_ref, qkv_cot_ref, upstream_ref, out_ref):
+def input_kernel(
+    clip_ref, gain_ref, weight_ref, qkv_cot_ref, upstream_ref, out_any, out_ref, sems
+):
     frames, _, _ = clip_ref.shape
+    copies = []
     for f in range(frames):
         features = clip_ref[f].astype(f32)
         squares = jnp.mean(features * features, axis=-1, keepdims=True)
@@ -168,20 +171,24 @@
         along = jnp.mean(features * cot, axis=-1, keepdims=True)
         direct = scale * cot - features * (scale * scale * scale * along)
         out_ref[f] = (upstream_ref[f].astype(f32) + direct).astype(bf16)
+        copies.append(pltpu.make_async_copy(out_ref.at[f], out_any.at[f], sems.at[f]))
+        copies[f].start()
+    for copy in copies:
+        copy.wait()
 
 
 def whole(count):
     return [pl.BlockSpec(memory_space=pltpu.VMEM)] * count
 
 
-def call(kernel, outs, args, flops, limit, scratch=(), specs=None):
+def call(kernel, outs, args, flops, limit, scratch=(), specs=None, out_specs=None):
     moved = sum(a.size * a.dtype.itemsize for a in args)
     moved += sum(math.prod(s) * jnp.dtype(d).itemsize for s, d in outs)
     return pl.pallas_call(
         kernel,
         out_shape=tuple(jax.ShapeDtypeStruct(s, d) for s, d in outs),
         in_specs=specs or whole(len(args)),
-        out_specs=tuple(whole(len(outs))),
+        out_specs=tuple(out_specs or whole(len(outs))),
         scratch_shapes=list(scratch),
         cost_estimate=pl.CostEstimate(flops=flops, bytes_accessed=moved, transcendentals=0),
         compiler_params=pltpu.CompilerParams(vmem_limit_bytes=limit << 20),
@@ -195,7 +202,10 @@
     )
 
 
-def piece_kernel(place_ref, shard_ref, out_ref, tiles_ref):
+def piece_kernel(place_ref, shard_any, out_ref, tiles_ref, shard_ref, sem):
+    copy = pltpu.make_async_copy(shard_any, shard_ref, sem)
+    copy.start()
+    copy.wait()
     taps, held, wide = shard_ref.shape
     lanes, parts = wide // LANES, held // 4
     count = taps * lanes * parts
@@ -220,11 +230,12 @@
     (piece,) = call(
         piece_kernel,
         [((lax.axis_size("z"), TILES, 2, LANES), bf16)],
-        [place.reshape(1), shard],
+        [place.reshape(1), pltpu.with_memory_space_constraint(shard, pltpu.HBM)],
         0,
         8,
-        [pltpu.VMEM((2 * PIECES * TILES, 2, LANES), bf16)],
-        [pl.BlockSpec(memory_space=pltpu.SMEM)] + whole(1),
+        [pltpu.VMEM((2 * PIECES * TILES, 2, LANES), bf16), pltpu.VMEM(shard.shape, bf16),
+         pltpu.SemaphoreType.DMA],
+        [pl.BlockSpec(memory_space=pltpu.SMEM), pl.BlockSpec(memory_space=pl.ANY)],
     )
     piece, core, group = lax.optimization_barrier((piece, core, group))
     column = lax.all_to_all(piece, ("z",), 0, 0, tiled=True)
@@ -310,6 +321,9 @@
         [clip, gain, qkv_weight, qkv_cot, upstream],
         2 * rows * width * 3 * width,
         16,
+        [pltpu.VMEM(clip.shape, bf16), pltpu.SemaphoreType.DMA((2,))],
+        None,
+        [pl.BlockSpec(memory_space=pl.ANY)],
     )
     got, input_grad, turn = lax.optimization_barrier((got, input_grad, turn))
     share = (keep.astype(f32) + got.astype(f32)).astype(bf16)

time: 108 us -> 108 us (level)
  no operation moved by 1% of the time
where the time goes in v8:
time: 108 us; the launch traced here: 107 us
  blocking collectives  77.1 us (71%)
  Pallas kernels  9.96 us (9%)
  waiting for transfers between devices  9.57 us (9%)
  starting transfers between devices  9.03 us (8%)
    all_to_all x1, blocking collectives, tap_column(): column = lax.all_to_all(piece, ('z',), 0, 0, tiled=True)  27.7 us
    all_to_all x1, blocking collectives, spread(): lax.all_to_all(jnp.broadcast_to(block[None], (count,) + block.shape), axe...  20.5 us
    all_to_all x1, blocking collectives, on_device(): share = lax.all_to_all(share, 'z', 0, 0, tiled=True)  15.4 us
    all_to_all x1, blocking collectives, on_device(): share = lax.all_to_all(share, PLANE, 0, 0, tiled=True)  13.5 us
    pallas_call x6, Pallas kernels, call(): pl.pallas_call(kernel, out_shape=tuple((jax.ShapeDtypeStruct(s, d) for s,...  9.96 us
    ppermute x1, waiting for transfers between devices, on_device(): lax.ppermute(cotangent, TM, [(i + 1, i) for i in range(slabs - 1)])  9.57 us
    ppermute x1, starting transfers between devices, on_device(): got = lax.ppermute(send, 'co', swap)  3.65 us
    ppermute x1, starting transfers between devices, on_device(): lax.ppermute(cotangent, TM, [(i + 1, i) for i in range(slabs - 1)])  3.47 us
  transfers between devices with their start and end apart: 3, of which 1 were waited for; matrix products, arithmetic and copies ran while one was open for 0% of the time, Pallas kernels for 3%

profile of v8, /device:TPU:2, one launch (start us, length us, event | category | flops | bytes accessed | tf_op | source)
XLA Modules:
  0.0 107.2 jit_solution(13638998216486556283)
XLA Ops:
  0.6 1.0 shard_map.77
  1.6 27.7 %all_to_all.20 = bf16[16,7,2,128]{3,2,1,0:T(2,128)(2,1)S(1)} all-to-all(bf16[16,7,2,128]{3,2,1,0:T(2,128)(2,1)S(1)} %shard_map.77), channel_id=1, replica_groups=mesh['xh'=2,'z'=16,'y'=4,'xl'=2,'co'=2] {'z'}, dimensions={0} | all-to-all | bytes 114688 | tf_op jit(solution)/shard_map/all_to_all | solution.py:241
  29.4 0.0 copy-start.3
  29.4 0.1 broadcast_in_dim.6
  29.5 0.0 copy-start
  29.5 0.0 copy-start.1
  29.5 0.0 copy-start.2
  29.5 20.5 %all_to_all.21.own_ref = bf16[16,7,32,128]{3,2,1,0:T(8,128)(2,1)S(1)} all-to-all(bf16[16,7,32,128]{3,2,1,0:T(8,128)(2,1)S(1)} %broadcast_in_dim.6), channel_id=1, replica_groups=mesh['xh'=2,'z'=16,'y'=4,'xl'=2,'co'=2] {'xh','y','xl'}, dimensions={0} | all-to-all | bytes 1835008 | tf_op jit(solution)/shard_map/all_to_all | solution.py:200
  50.1 1.9 %collective-permute-start.1 = (bf16[16,7,32,128]{3,2,1,0:T(8,128)(2,1)S(1)}, bf16[16,7,32,128]{3,2,1,0:T(8,128)(2,1)S(1)}, u32[]{:S(2)}, u32[]{:S(2)}) collective-permute-start(bf16[16,7,32,128]{3,2,1,0:T(8,128)(2,1)S(1)} %all_to_all.21.own_ref), channel_id=1, source_target_pairs={{0,1},{1,0},{2,3},{3,2},{4,5},{5,4},{6,7},{7,6},{8,9},{9,8},{10,11... | collective-permute-start | bytes 2752520 | tf_op jit(solution)/shard_map/ppermute | solution.py:290
  52.0 3.5 %collective-permute-start = (bf16[2,256,768]{2,1,0:T(8,128)(2,1)}, bf16[2,256,768]{2,1,0:T(8,128)(2,1)}, u32[]{:S(2)}, u32[]{:S(2)}) collective-permute-start(bf16[2,256,768]{2,1,0:T(8,128)(2,1)} %bitcast.5.cot_ref), channel_id=1, source_target_pairs={{1,0},{2,1},{3,2},{4,3},{5,4},{6,5},{7,6},{8,7},{9,8},{10,9},{11,1... | collective-permute-start | bytes 2359304 | tf_op jit(solution)/shard_map/ppermute | solution.py:283
  55.5 0.0 copy-done.3
  55.6 0.1 fusion.order_ref
  55.7 9.6 %collective-permute-done.next_any = bf16[2,256,768]{2,1,0:T(8,128)(2,1)} collective-permute-done((bf16[2,256,768]{2,1,0:T(8,128)(2,1)}, bf16[2,256,768]{2,1,0:T(8,128)(2,1)}, u32[]{:S(2)}, u32[]{:S(2)}) %collective-permute-start) | collective-permute-done | bytes 786464 | tf_op jit(solution)/shard_map/ppermute | solution.py:283
  65.3 0.0 copy-done
  65.3 0.0 copy-done.1
  65.3 0.0 copy-done.2
  65.3 1.8 %shard_map.78 = (bf16[2,256,384]{2,1,0:T(8,128)(2,1)S(1)}, bf16[2,256,1152]{2,1,0:T(8,128)(2,1)S(1)}, f32[2,256,256]{2,1,0:T(8,128)S(1)}, bf16[384,384]{1,0:T(8,128)(2,1)S(1)}, bf16[2,256,768]{2,1,0:T(8,128)(2,1)S(1)}) custom-call(bf16[2,256,384]{2,1,0:T(8,128)(2,1)S(1)} %bitcast.7, f32[1,384]{1,0:T(1,128)S(1)} %broadcast_in_dim.7.gain_ref, ...), custom_call_target="tpu_custom_call" | custom-call | flops 553648128 | bytes 5834240 | tf_op jit(solution)/shard_map/pallas_call | solution.py:187
  67.1 0.0 collective-permute-done.1.other_ref
  67.1 4.4 %shard_map.79 = (bf16[2,256,384]{2,1,0:T(8,128)(2,1)S(1)}, bf16[2,256,1152]{2,1,0:T(8,128)(2,1)S(1)}, bf16[16,112,128]{2,1,0:T(8,128)(2,1)S(1)}, bf16[16,112,128]{2,1,0:T(8,128)(2,1)S(1)}) custom-call(s32[1]{0:T(128)} %bitcast.4.core_ref, bf16[2,256,768]{2,1,0:T(8,128)(2,1)} %bitcast.5.cot_ref, bf16[2,256,768]{2,1,0:T(8,128)(2,1)S(1)} %get-tuple-element.32.next_ref, ...), custom_call_target="tpu_custom_call" | custom-call | flops 2063597568 | bytes 8585220 | tf_op jit(solution)/shard_map/pallas_call | solution.py:187
  71.6 3.7 %collective-permute-start.2 = (bf16[16,112,128]{2,1,0:T(8,128)(2,1)S(1)}, bf16[16,112,128]{2,1,0:T(8,128)(2,1)S(1)}, u32[]{:S(2)}, u32[]{:S(2)}) collective-permute-start(bf16[16,112,128]{2,1,0:T(8,128)(2,1)S(1)} %get-tuple-element.38), channel_id=1, source_target_pairs={{0,1},{1,0},{2,3},{3,2},{4,5},{5,4},{6,7},{7,6},{8,9},{9,8},{10,11... | collective-permute-start | bytes 1376264 | tf_op jit(solution)/shard_map/ppermute | solution.py:317
  75.3 0.1 broadcast_compare_fusion
  75.4 1.7 %shard_map.80 = bf16[2,256,384]{2,1,0:T(8,128)(2,1)} custom-call(bf16[2,256,384]{2,1,0:T(8,128)(2,1)S(1)} %bitcast.8, f32[1,384]{1,0:T(1,128)S(1)} %broadcast_in_dim.7.gain_ref, bf16[384,1152]{1,0:T(8,128)(2,1)S(1)} %copy-done, bf16[2,256,1152]{2,1,0:T(8,128)(2,1)S(1)} %get-tuple-element.39.qkv_cot_ref, bf16[2,256,384]{2,1,0:T(8,128)(2,1)S(1)} %get-tuple-element.40.upstream_ref), custom_call_target="tpu_custom_call" | custom-call | flops 452984832 | bytes 3245568 | tf_op jit(solution)/shard_map/pallas_call | solution.py:187
  77.1 0.0 collective-permute-done.2
  77.1 0.2 add_convert_fusion
  77.3 13.5 %all_to_all.22.got_ref = bf16[16,112,128]{2,1,0:T(8,128)(2,1)S(1)} all-to-all(bf16[16,112,128]{2,1,0:T(8,128)(2,1)S(1)} %add_convert_fusion), channel_id=1, replica_groups=mesh['xh'=2,'z'=16,'y'=4,'xl'=2,'co'=2] {'xh','y','xl'}, dimensions={0} | all-to-all | bytes 917504 | tf_op jit(solution)/shard_map/all_to_all | solution.py:330
  90.8 0.3 shard_map.81
  91.1 15.4 %all_to_all.23.got_ref = bf16[16,8,128]{2,1,0:T(8,128)(2,1)S(1)} all-to-all(bf16[16,8,128]{2,1,0:T(8,128)(2,1)S(1)} %shard_map.81), channel_id=1, replica_groups=mesh['xh'=2,'z'=16,'y'=4,'xl'=2,'co'=2] {'z'}, dimensions={0} | all-to-all | bytes 65536 | tf_op jit(solution)/shard_map/all_to_all | solution.py:338
  106.5 0.7 shard_map.82
  (8 shorter events, 0.1 us)
Async XLA Ops:
  29.4 26.1 %copy-start.3 = (f32[384]{0:T(512)S(1)}, f32[384]{0:T(512)}, u32[]{:S(2)}) copy-start(f32[384]{0:T(512)} %param.7) | copy-start | bytes 4612
  29.5 35.8 %copy-start = (bf16[384,1152]{1,0:T(8,128)(2,1)S(1)}, bf16[384,1152]{1,0:T(8,128)(2,1)}, u32[]{:S(2)}) copy-start(bf16[384,1152]{1,0:T(8,128)(2,1)} %weight_ref.3) | copy-start | bytes 2654212
  29.5 35.8 %copy-start.1 = (bf16[1,2,256,384]{3,2,1,0:T(8,128)(2,1)S(1)}, bf16[1,2,256,384]{3,2,1,0:T(8,128)(2,1)}, u32[]{:S(2)}) copy-start(bf16[1,2,256,384]{3,2,1,0:T(8,128)(2,1)} %param.6) | copy-start | bytes 1179652
  29.5 35.8 %copy-start.2 = (bf16[384,384]{1,0:T(8,128)(2,1)S(1)}, bf16[384,384]{1,0:T(8,128)(2,1)}, u32[]{:S(2)}) copy-start(bf16[384,384]{1,0:T(8,128)(2,1)} %out_weight_ref.1) | copy-start | bytes 884740
  50.1 17.0 %collective-permute-start.1 = (bf16[16,7,32,128]{3,2,1,0:T(8,128)(2,1)S(1)}, bf16[16,7,32,128]{3,2,1,0:T(8,128)(2,1)S(1)}, u32[]{:S(2)}, u32[]{:S(2)}) collective-permute-start(bf16[16,7,32,128]{3,2,1,0:T(8,128)(2,1)S(1)} %all_to_all.21.own_ref), channel_id=1, source_target_pairs={{0,1},{1,0},{2,3},{3,2},{4,5},{5,4},{6,7},{7,6},{8,9},{9,8},{10,11... | collective-permute-start | bytes 2752520 | tf_op jit(solution)/shard_map/ppermute | solution.py:290
  52.0 13.3 %collective-permute-start = (bf16[2,256,768]{2,1,0:T(8,128)(2,1)}, bf16[2,256,768]{2,1,0:T(8,128)(2,1)}, u32[]{:S(2)}, u32[]{:S(2)}) collective-permute-start(bf16[2,256,768]{2,1,0:T(8,128)(2,1)} %bitcast.5.cot_ref), channel_id=1, source_target_pairs={{1,0},{2,1},{3,2},{4,3},{5,4},{6,5},{7,6},{8,7},{9,8},{10,9},{11,1... | collective-permute-start | bytes 2359304 | tf_op jit(solution)/shard_map/ppermute | solution.py:283
  71.6 5.5 %collective-permute-start.2 = (bf16[16,112,128]{2,1,0:T(8,128)(2,1)S(1)}, bf16[16,112,128]{2,1,0:T(8,128)(2,1)S(1)}, u32[]{:S(2)}, u32[]{:S(2)}) collective-permute-start(bf16[16,112,128]{2,1,0:T(8,128)(2,1)S(1)} %get-tuple-element.38), channel_id=1, source_target_pairs={{0,1},{1,0},{2,3},{3,2},{4,5},{5,4},{6,7},{7,6},{8,9},{9,8},{10,11... | collective-permute-start | bytes 1376264 | tf_op jit(solution)/shard_map/ppermute | solution.py:317

commit v9 on v7

--- a/solution.py
+++ b/solution.py
@@ -117,31 +117,34 @@
                     upper = pltpu.roll(upper, LANES // 2, 1)
                 side = 2 * group * LANES
                 wide_part = grad_ref[pl.ds(top, columns), side : side + LANES]
-                out_ref[group * PIECES + chip] = jnp.concatenate(
+                out_ref[groups * chip + group] = jnp.concatenate(
                     [wide_part, jnp.where(left, upper, lower)], axis=0
                 ).astype(bf16)
 
 
 def turn_kernel(got_ref, turn_ref, out_ref):
     columns, short = 72, got_ref.shape[1] - 72
-    depth = out_ref.shape[0]
-    total = got_ref[0].astype(f32)
-    for i in range(1, got_ref.shape[0]):
-        total = total + got_ref[i].astype(f32)
-    narrow = total[columns:]
-    other = pltpu.roll(narrow, LANES // 2, 1)
-    empty = jnp.zeros((LANES - columns, LANES), f32)
-    narrow = jnp.concatenate([narrow, other[2 * short - columns :], empty], axis=0)
-    wide = jnp.concatenate([total[:columns], empty], axis=0)
-    turned = dot(turn_ref[0], wide.astype(bf16), NT) + dot(turn_ref[1], narrow.astype(bf16), NT)
-    first, last = turned[: depth * 8], turned[depth * 8 :]
-    row = lax.broadcasted_iota(jnp.int32, first.shape, 0)
-    lane = lax.broadcasted_iota(jnp.int32, first.shape, 1)
-    last = jnp.where(
-        lax.rem(row, 2) == 0, pltpu.roll(last, columns, 1), pltpu.roll(last, columns // 2, 1)
-    )
-    turned = jnp.where(lane < columns, first, last)
-    out_ref[...] = turned.astype(bf16).reshape(out_ref.shape)
+    depth = turn_ref.shape[1] // 16
+    groups = out_ref.shape[0] // depth
+    for group in range(groups):
+        total = got_ref[group].astype(f32)
+        for i in range(group + groups, got_ref.shape[0], groups):
+            total = total + got_ref[i].astype(f32)
+        narrow = total[columns:]
+        other = pltpu.roll(narrow, LANES // 2, 1)
+        empty = jnp.zeros((LANES - columns, LANES), f32)
+        narrow = jnp.concatenate([narrow, other[2 * short - columns :], empty], axis=0)
+        wide = jnp.concatenate([total[:columns], empty], axis=0)
+        turned = dot(turn_ref[2 * group], wide.astype(bf16), NT)
+        turned = turned + dot(turn_ref[2 * group + 1], narrow.astype(bf16), NT)
+        first, last = turned[: depth * 8], turned[depth * 8 :]
+        row = lax.broadcasted_iota(jnp.int32, first.shape, 0)
+        lane = lax.broadcasted_iota(jnp.int32, first.shape, 1)
+        last = jnp.where(
+            lax.rem(row, 2) == 0, pltpu.roll(last, columns, 1), pltpu.roll(last, columns // 2, 1)
+        )
+        turned = jnp.where(lane < columns, first, last).astype(bf16)
+        out_ref[group * depth : (group + 1) * depth] = turned.reshape(depth, 8, LANES)
 
 
 def final_kernel(got_ref, out_ref):
@@ -289,7 +292,7 @@
         [pltpu.SemaphoreType.DMA],
         whole(5) + [pl.BlockSpec(memory_space=pl.ANY)],
     )
-    turn = turn_orders(held, depth, group)
+    turn = jnp.concatenate([turn_orders(held, depth, g) for g in range(2)])
     core = core.reshape(1)
 
     chips = own.shape[0]
@@ -313,15 +316,15 @@
     )
     got, input_grad, turn = lax.optimization_barrier((got, input_grad, turn))
     share = (keep.astype(f32) + got.astype(f32)).astype(bf16)
-    share = lax.all_to_all(share, PLANE, 0, 0, tiled=True)
+    share = lax.all_to_all(share, ("y", "xl"), 0, 0, tiled=True)
     (share,) = call(
         turn_kernel,
-        [((depth, 8, LANES), bf16)],
+        [((2 * depth, 8, LANES), bf16)],
         [share, turn],
         2 * depth * 16 * 72 * 2 * LANES,
         16,
     )
-    share = lax.all_to_all(share, "z", 0, 0, tiled=True)
+    share = lax.all_to_all(share, DP, 0, 0, tiled=True)
     (qkv_grad,) = call(final_kernel, [((held, 3 * width // slabs), f32)], [share], 0, 8)
     return (input_grad[None], qkv_grad)
 

time: 108 us -> 110 us (1.019)
  the two profiles are of different devices: /device:TPU:2 before, /device:TPU:32 now
where the time goes in v9:
time: 110 us
  blocking collectives  80.6 us (73%)
  starting transfers between devices  14.7 us (13%)
  Pallas kernels  9.21 us (8%)
  waiting for transfers between devices  3 us (3%)
    all_to_all x1, blocking collectives, tap_column(): column = lax.all_to_all(piece, ('z',), 0, 0, tiled=True)  26.5 us
    all_to_all x1, blocking collectives, spread(): lax.all_to_all(jnp.broadcast_to(block[None], (count,) + block.shape), axe...  21.6 us
    all_to_all x1, blocking collectives, on_device(): share = lax.all_to_all(share, DP, 0, 0, tiled=True)  20.2 us
    all_to_all x1, blocking collectives, on_device(): share = lax.all_to_all(share, ('y', 'xl'), 0, 0, tiled=True)  12.3 us
    ppermute x1, starting transfers between devices, on_device(): got = lax.ppermute(send, 'co', swap)  11.5 us
    pallas_call x6, Pallas kernels, call(): pl.pallas_call(kernel, out_shape=tuple((jax.ShapeDtypeStruct(s, d) for s,...  9.21 us
    ppermute x1, waiting for transfers between devices, on_device(): lax.ppermute(cotangent, TM, [(i + 1, i) for i in range(slabs - 1)])  3 us
  transfers between devices with their start and end apart: 3, of which 1 were waited for; matrix products, arithmetic and copies ran while one was open for 0% of the time, Pallas kernels for 3%

profile of v9, /device:TPU:32, one launch (start us, length us, event | category | flops | bytes accessed | tf_op | source)
XLA Modules:
  0.0 109.9 jit_solution(13383110996206390270)
XLA Ops:
  0.6 0.0 copy-start.3
  0.7 0.9 copy-done.3
  1.5 0.1 shard_map.77
  1.6 26.5 %all_to_all.20 = bf16[16,7,2,128]{3,2,1,0:T(2,128)(2,1)S(1)} all-to-all(bf16[16,7,2,128]{3,2,1,0:T(2,128)(2,1)S(1)} %shard_map.77), channel_id=1, replica_groups=mesh['xh'=2,'z'=16,'y'=4,'xl'=2,'co'=2] {'z'}, dimensions={0} | all-to-all | bytes 114688 | tf_op jit(solution)/shard_map/all_to_all | solution.py:233
  28.1 0.0 copy-start.4
  28.2 0.1 broadcast_in_dim.6
  28.3 0.0 copy-start
  28.3 0.0 copy-start.1
  28.3 0.0 copy-start.2
  28.3 21.6 %all_to_all.21.own_ref = bf16[16,7,32,128]{3,2,1,0:T(8,128)(2,1)S(1)} all-to-all(bf16[16,7,32,128]{3,2,1,0:T(8,128)(2,1)S(1)} %broadcast_in_dim.6), channel_id=1, replica_groups=mesh['xh'=2,'z'=16,'y'=4,'xl'=2,'co'=2] {'xh','y','xl'}, dimensions={0} | all-to-all | bytes 1835008 | tf_op jit(solution)/shard_map/all_to_all | solution.py:196
  50.0 1.9 %collective-permute-start.1 = (bf16[16,7,32,128]{3,2,1,0:T(8,128)(2,1)S(1)}, bf16[16,7,32,128]{3,2,1,0:T(8,128)(2,1)S(1)}, u32[]{:S(2)}, u32[]{:S(2)}) collective-permute-start(bf16[16,7,32,128]{3,2,1,0:T(8,128)(2,1)S(1)} %all_to_all.21.own_ref), channel_id=1, source_target_pairs={{0,1},{1,0},{2,3},{3,2},{4,5},{5,4},{6,7},{7,6},{8,9},{9,8},{10,11... | collective-permute-start | bytes 2752520 | tf_op jit(solution)/shard_map/ppermute | solution.py:282
  51.9 1.3 %collective-permute-start = (bf16[2,256,768]{2,1,0:T(8,128)(2,1)}, bf16[2,256,768]{2,1,0:T(8,128)(2,1)}, u32[]{:S(2)}, u32[]{:S(2)}) collective-permute-start(bf16[2,256,768]{2,1,0:T(8,128)(2,1)} %bitcast.5.cot_ref), channel_id=1, source_target_pairs={{1,0},{2,1},{3,2},{4,3},{5,4},{6,5},{7,6},{8,7},{9,8},{10,9},{11,1... | collective-permute-start | bytes 2359304 | tf_op jit(solution)/shard_map/ppermute | solution.py:275
  53.2 0.0 copy-done.4
  53.3 0.1 fusion.order_ref
  53.4 3.0 %collective-permute-done.next_any = bf16[2,256,768]{2,1,0:T(8,128)(2,1)} collective-permute-done((bf16[2,256,768]{2,1,0:T(8,128)(2,1)}, bf16[2,256,768]{2,1,0:T(8,128)(2,1)}, u32[]{:S(2)}, u32[]{:S(2)}) %collective-permute-start) | collective-permute-done | bytes 786464 | tf_op jit(solution)/shard_map/ppermute | solution.py:275
  56.4 0.0 copy-done
  56.4 0.0 copy-done.1
  56.4 0.0 copy-done.2
  56.4 1.8 %shard_map.78 = (bf16[2,256,384]{2,1,0:T(8,128)(2,1)S(1)}, bf16[2,256,1152]{2,1,0:T(8,128)(2,1)S(1)}, f32[2,256,256]{2,1,0:T(8,128)S(1)}, bf16[384,384]{1,0:T(8,128)(2,1)S(1)}, bf16[2,256,768]{2,1,0:T(8,128)(2,1)S(1)}) custom-call(bf16[2,256,384]{2,1,0:T(8,128)(2,1)S(1)} %bitcast.7, f32[1,384]{1,0:T(1,128)S(1)} %broadcast_in_dim.7.gain_ref, ...), custom_call_target="tpu_custom_call" | custom-call | flops 553648128 | bytes 5834240 | tf_op jit(solution)/shard_map/pallas_call | solution.py:183
  58.2 0.0 collective-permute-done.1.other_ref
  58.2 4.4 %shard_map.79 = (bf16[2,256,384]{2,1,0:T(8,128)(2,1)S(1)}, bf16[2,256,1152]{2,1,0:T(8,128)(2,1)S(1)}, bf16[16,112,128]{2,1,0:T(8,128)(2,1)S(1)}, bf16[16,112,128]{2,1,0:T(8,128)(2,1)S(1)}) custom-call(s32[1]{0:T(128)} %bitcast.4.core_ref, bf16[2,256,768]{2,1,0:T(8,128)(2,1)} %bitcast.5.cot_ref, bf16[2,256,768]{2,1,0:T(8,128)(2,1)S(1)} %get-tuple-element.27.next_ref, ...), custom_call_target="tpu_custom_call" | custom-call | flops 2063597568 | bytes 8585220 | tf_op jit(solution)/shard_map/pallas_call | solution.py:183
  62.7 11.5 %collective-permute-start.2 = (bf16[16,112,128]{2,1,0:T(8,128)(2,1)S(1)}, bf16[16,112,128]{2,1,0:T(8,128)(2,1)S(1)}, u32[]{:S(2)}, u32[]{:S(2)}) collective-permute-start(bf16[16,112,128]{2,1,0:T(8,128)(2,1)S(1)} %get-tuple-element.33), channel_id=1, source_target_pairs={{0,1},{1,0},{2,3},{3,2},{4,5},{5,4},{6,7},{7,6},{8,9},{9,8},{10,11... | collective-permute-start | bytes 1376264 | tf_op jit(solution)/shard_map/ppermute | solution.py:309
  74.2 0.1 compare_and_fusion
  74.4 0.1 add_convert_fusion.1.turn_ref
  74.4 1.8 %shard_map.80 = bf16[2,256,384]{2,1,0:T(8,128)(2,1)} custom-call(bf16[2,256,384]{2,1,0:T(8,128)(2,1)S(1)} %bitcast.8, f32[1,384]{1,0:T(1,128)S(1)} %broadcast_in_dim.7.gain_ref, bf16[384,1152]{1,0:T(8,128)(2,1)S(1)} %copy-done, bf16[2,256,1152]{2,1,0:T(8,128)(2,1)S(1)} %get-tuple-element.34.qkv_cot_ref, bf16[2,256,384]{2,1,0:T(8,128)(2,1)S(1)} %get-tuple-element.35.upstream_ref), custom_call_target="tpu_custom_call" | custom-call | flops 452984832 | bytes 3245568 | tf_op jit(solution)/shard_map/pallas_call | solution.py:183
  76.2 0.0 collective-permute-done.2
  76.2 0.2 add_convert_fusion
  76.4 12.3 %all_to_all.22.got_ref = bf16[16,112,128]{2,1,0:T(8,128)(2,1)S(1)} all-to-all(bf16[16,112,128]{2,1,0:T(8,128)(2,1)S(1)} %add_convert_fusion), channel_id=1, replica_groups=mesh['xh'=2,'z'=16,'y'=4,'xl'=2,'co'=2] {'y','xl'}, dimensions={0} | all-to-all | bytes 917504 | tf_op jit(solution)/shard_map/all_to_all | solution.py:319
  88.6 0.4 shard_map.81
  89.0 20.2 %all_to_all.23.got_ref = bf16[32,8,128]{2,1,0:T(8,128)(2,1)S(1)} all-to-all(bf16[32,8,128]{2,1,0:T(8,128)(2,1)S(1)} %shard_map.81), channel_id=1, replica_groups=mesh['xh'=2,'z'=16,'y'=4,'xl'=2,'co'=2] {'xh','z'}, dimensions={0} | all-to-all | bytes 131072 | tf_op jit(solution)/shard_map/all_to_all | solution.py:327
  109.2 0.7 shard_map.82
  (7 shorter events, 0.1 us)
Async XLA Ops:
  0.6 0.9 copy-start.3
  28.1 25.0 %copy-start.4 = (f32[384]{0:T(512)S(1)}, f32[384]{0:T(512)}, u32[]{:S(2)}) copy-start(f32[384]{0:T(512)} %param.7) | copy-start | bytes 4612
  28.3 28.1 %copy-start = (bf16[384,1152]{1,0:T(8,128)(2,1)S(1)}, bf16[384,1152]{1,0:T(8,128)(2,1)}, u32[]{:S(2)}) copy-start(bf16[384,1152]{1,0:T(8,128)(2,1)} %weight_ref.3) | copy-start | bytes 2654212
  28.3 28.1 %copy-start.1 = (bf16[1,2,256,384]{3,2,1,0:T(8,128)(2,1)S(1)}, bf16[1,2,256,384]{3,2,1,0:T(8,128)(2,1)}, u32[]{:S(2)}) copy-start(bf16[1,2,256,384]{3,2,1,0:T(8,128)(2,1)} %param.6) | copy-start | bytes 1179652
  28.3 28.1 %copy-start.2 = (bf16[384,384]{1,0:T(8,128)(2,1)S(1)}, bf16[384,384]{1,0:T(8,128)(2,1)}, u32[]{:S(2)}) copy-start(bf16[384,384]{1,0:T(8,128)(2,1)} %out_weight_ref.1) | copy-start | bytes 884740
  50.0 8.3 %collective-permute-start.1 = (bf16[16,7,32,128]{3,2,1,0:T(8,128)(2,1)S(1)}, bf16[16,7,32,128]{3,2,1,0:T(8,128)(2,1)S(1)}, u32[]{:S(2)}, u32[]{:S(2)}) collective-permute-start(bf16[16,7,32,128]{3,2,1,0:T(8,128)(2,1)S(1)} %all_to_all.21.own_ref), channel_id=1, source_target_pairs={{0,1},{1,0},{2,3},{3,2},{4,5},{5,4},{6,7},{7,6},{8,9},{9,8},{10,11... | collective-permute-start | bytes 2752520 | tf_op jit(solution)/shard_map/ppermute | solution.py:282
  51.9 4.5 %collective-permute-start = (bf16[2,256,768]{2,1,0:T(8,128)(2,1)}, bf16[2,256,768]{2,1,0:T(8,128)(2,1)}, u32[]{:S(2)}, u32[]{:S(2)}) collective-permute-start(bf16[2,256,768]{2,1,0:T(8,128)(2,1)} %bitcast.5.cot_ref), channel_id=1, source_target_pairs={{1,0},{2,1},{3,2},{4,3},{5,4},{6,5},{7,6},{8,7},{9,8},{10,9},{11,1... | collective-permute-start | bytes 2359304 | tf_op jit(solution)/shard_map/ppermute | solution.py:275
  62.7 13.5 %collective-permute-start.2 = (bf16[16,112,128]{2,1,0:T(8,128)(2,1)S(1)}, bf16[16,112,128]{2,1,0:T(8,128)(2,1)S(1)}, u32[]{:S(2)}, u32[]{:S(2)}) collective-permute-start(bf16[16,112,128]{2,1,0:T(8,128)(2,1)S(1)} %get-tuple-element.33), channel_id=1, source_target_pairs={{0,1},{1,0},{2,3},{3,2},{4,5},{5,4},{6,7},{7,6},{8,9},{9,8},{10,11... | collective-permute-start | bytes 1376264 | tf_op jit(solution)/shard_map/ppermute | solution.py:309
